TPU v7x, 128 devices: a whole 4x4x4 slice. The times are simulated.
128 devices in a mesh: sec: 2 (over y_hi), rr: 8 (over y_lo, z), sr: 8 (over x, core).
Axes of the slice: x: 4, y: 4 (y_hi: 2, y_lo: 2; y = y_hi * 2 + y_lo), z: 4, core: 2. Of those that a mesh axis runs over, the one named last changes fastest.
Arguments:
- wave_prev: float32 [2, 4, 256, 256, 256], P('sec', None, 'rr', 'sr'), may hold values from -6 to 6
- wave_now: float32 [2, 4, 256, 256, 256], P('sec', None, 'rr', 'sr'), may hold values from -6 to 6
- potential: float32 [2, 256, 256, 256], P('sec', 'rr', 'sr'), may hold values from -0.5 to 0.5
- damping: float32 [2, 256, 256], P('sec', 'rr', 'sr'), may hold values from 0.7 to 1
- switch: float32 [256, 256], P('rr', 'sr'), may hold values from 0.05 to 0.5
- angular: float32 [2, 4, 256, 256], P('sec')
- coriolis: float32 [2, 3, 256, 256], P('sec'), may hold values from -0.375 to 0.375
- helicity_start: int32 [2], P('sec'), may hold values from 0 to 20
- frame_map: float32 [4, 256, 4, 256], replicated, may hold values from -0.1875 to 0.1875
- route_table: int32 [64, 64, 2], replicated, may hold values from -1 to 127, as said below
- pick_slots: int32 [8, 8, 128, 4], P('rr', 'sr'), may hold values from 0 to 127, as said below
- interp_weights: float32 [8, 8, 128, 4, 8, 8], P('rr', 'sr'), may hold values from -1 to 1
Outputs:
- wave_prev_out: float32 [2, 4, 256, 256, 256], P('sec', None, 'rr', 'sr')
- wave_now_out: float32 [2, 4, 256, 256, 256], P('sec', None, 'rr', 'sr')
Inputs may be any that keep to these rules, and one draw needn't show every extreme that they name: route_table[d, s, t] is the block of reactant slab s sent to product slab d in slot t, or -1; the filled slots of a pair come first and name different blocks; every product slab gets 2 blocks from some slab, and some product slab gets 2 blocks from every slab. Each entry e2 of pick_slots[d] has route_table[d, e2 // 2, e2 % 2] >= 0, and every such filled slot of d is named by some entry.
All inputs are finite; a program needn't handle non-finite values.
Results may differ from a plain program's by a relative error of at most 0.0003.
Values sent between devices are 32-bit elements; how exact they have to be, the bound alone decides.
No kernel may reach another device: no remote copies, remote signals or barrier semaphores. Data moves between devices by JAX's collectives and lax.ppermute only.
A program may use at most 128 MiB of HBM per device.

v0:
```python
import jax
import jax.numpy as jnp
from jax import lax
from jax.sharding import PartitionSpec as P

JTOT = 23
STEPS = 2


kinetic_radial = 0.08
kinetic_bond = 0.08
rotor_scale = 0.1
centrifugal = 0.0005
coriolis_scale = 0.005
highest = lax.Precision.HIGHEST


def with_halo(x, sides, width):
    for axis, dim in sides:
        peers, length = (lax.axis_size(axis), x.shape[dim])
        up = [(i, (i + 1) % peers) for i in range(peers - 1)]
        down = [(j, i) for i, j in up]
        last = lax.slice_in_dim(x, length - width, length, axis=dim)
        first = lax.slice_in_dim(x, 0, width, axis=dim)
        before = lax.ppermute(last, axis, up)
        after = lax.ppermute(first, axis, down)
        x = jnp.concatenate([before, x, after], axis=dim)
    return x


def extend_main(state_field):
    return with_halo(state_field, (("rr", 1), ("sr", 2)), 1)


def hamilton(state_field, extender, angles, coupling, potent, radial, bond_factor, helicity_vals):
    padded = extender(state_field)
    laplace = kinetic_radial * (2.0 * state_field - padded[:, 2:, 1:-1] - padded[:, :-2, 1:-1])
    laplace = laplace + kinetic_bond * (
        2.0 * state_field - padded[:, 1:-1, 2:] - padded[:, 1:-1, :-2]
    )
    rotated = jnp.einsum(
        "kijb,kab->kija", state_field, angles, precision=highest, preferred_element_type=jnp.float32
    )
    total_j = float(JTOT * (JTOT + 1))
    ladder = jnp.sqrt(total_j - helicity_vals * (helicity_vals + 1.0))[:-1]
    raised = (
        jnp.einsum(
            "kijb,kab->kija",
            state_field[1:],
            coupling,
            precision=highest,
            preferred_element_type=jnp.float32,
        )
        * ladder[:, None, None, None]
    )
    lowered = (
        jnp.einsum(
            "kijb,kba->kija",
            state_field[:-1],
            coupling,
            precision=highest,
            preferred_element_type=jnp.float32,
        )
        * ladder[:, None, None, None]
    )
    blank_row = jnp.zeros_like(state_field[:1])
    mixing = jnp.concatenate([raised, blank_row], 0) + jnp.concatenate([blank_row, lowered], 0)
    centre_term = centrifugal * (total_j - 2.0 * helicity_vals * helicity_vals)
    rotation = rotor_scale * (radial[:, None] + bond_factor[None, :])
    return (
        laplace
        + rotation[None, :, :, None] * rotated
        + radial[None, :, None, None]
        * (centre_term[:, None, None, None] * state_field + coriolis_scale * mixing)
        + potent[None] * state_field
    )


def transfer(absorbed, frame_map, route_table, pick_slots, interp_weights, source_id):
    helices, radial_len, bond_len, angle_len = absorbed.shape
    block_rows = interp_weights.shape[-1]
    blocks = absorbed.reshape(helices, radial_len * bond_len // block_rows, block_rows, angle_len)
    outgoing_ids = lax.dynamic_index_in_dim(route_table, source_id, axis=1, keepdims=False)
    filled = outgoing_ids >= 0
    packed = jnp.take(blocks, jnp.maximum(outgoing_ids, 0), axis=1)
    packed = jnp.where(filled[None, :, :, None, None], packed, 0.0)
    sources = outgoing_ids.shape[0]
    outgoing = jnp.concatenate([jnp.zeros_like(packed), packed], axis=1)
    arrived = lax.all_to_all(
        outgoing, ("sec", "rr", "sr"), split_axis=1, concat_axis=1, tiled=True
    )[:, :sources]
    slot_rows = arrived.reshape(helices, -1, block_rows, angle_len)
    selected = jnp.take(slot_rows, pick_slots[0, 0], axis=1)
    blended = jnp.einsum(
        "bmij,kbmja->kbia",
        interp_weights[0, 0],
        selected,
        precision=highest,
        preferred_element_type=jnp.float32,
    )
    row_values = blended.reshape(helices, radial_len * bond_len, angle_len)
    rotated = jnp.einsum(
        "kna,kalb->lnb",
        row_values,
        frame_map,
        precision=highest,
        preferred_element_type=jnp.float32,
    )
    return rotated.reshape(helices, radial_len, bond_len, angle_len)


def per_device(
    wave_prev,
    wave_now,
    potential,
    damping,
    switch,
    angular,
    coriolis,
    helicity_start,
    frame_map,
    route_table,
    pick_slots,
    interp_weights,
):
    section = lax.axis_index("sec")
    row_slab = lax.axis_index("rr")
    col_slab = lax.axis_index("sr")
    radial_slabs = lax.axis_size("rr")
    bond_slabs = lax.axis_size("sr")
    previous = wave_prev[0]
    current = wave_now[0]
    helices, radial_len, bond_len, angle_len = current.shape
    radial_pos = (row_slab * radial_len + jnp.arange(radial_len)).astype(jnp.float32)
    bond_pos = (col_slab * bond_len + jnp.arange(bond_len)).astype(jnp.float32)
    radial = (1.0 + 3.0 * radial_pos / float(radial_slabs * radial_len)) ** (-2)
    bond_factor = (1.0 + 3.0 * bond_pos / float(bond_slabs * bond_len)) ** (-2)
    helicity_vals = helicity_start[0].astype(jnp.float32) + jnp.arange(helices, dtype=jnp.float32)
    damp_grid = damping[0][None, :, :, None]
    transfer_share = jnp.where(section == 0, switch, 0.0)[None, :, :, None]
    source_id = row_slab * bond_slabs + col_slab
    own_part = current
    inflow = jnp.zeros_like(current)
    for iteration in range(STEPS):
        applied = hamilton(
            current,
            extend_main,
            angular[0],
            coriolis[0],
            potential[0],
            radial,
            bond_factor,
            helicity_vals,
        )
        renewed = damp_grid * (2.0 * applied - damp_grid * previous)
        absorbed = transfer_share * renewed
        own_part = renewed - absorbed
        inflow = transfer(absorbed, frame_map, route_table, pick_slots, interp_weights, source_id)
        previous = current
        current = own_part + inflow
    return (previous[None], current[None])


def solution(mesh):
    placed = (
        P("sec", None, "rr", "sr", None),
        P("sec", None, "rr", "sr", None),
        P("sec", "rr", "sr", None),
        P("sec", "rr", "sr"),
        P("rr", "sr"),
        P("sec", None, None, None),
        P("sec", None, None, None),
        P("sec"),
        P(),
        P(),
        P("rr", "sr", None, None),
        P("rr", "sr", None, None, None, None),
    )
    return jax.shard_map(
        per_device,
        mesh=mesh,
        in_specs=placed,
        out_specs=(P("sec", None, "rr", "sr", None), P("sec", None, "rr", "sr", None)),
        check_vma=False,
    )
```

profile of v0, /device:TPU:27, one launch (start us, length us, event | category | flops | bytes accessed | tf_op | source)
XLA Modules:
  0.0 442.6 jit_solution(9033819591984122995)
XLA Ops:
  1.8 3.7 collective-permute-start.1
  5.5 4.2 collective-permute-start
  10.4 6.5 %fusion.59 = f32[3,32,32,256]{3,2,1,0:T(8,128)} fusion(f32[1,4,32,32,256]{4,3,2,1,0:T(8,128)} %param.17, f32[3]{0:T(128)S(1)} %bitcast.144, f32[1,3,256,256]{3,2,1,0:T(8,128)} %param.22), kind=kOutput, calls=%fused_computation.80 | convolution fusion | flops 2416705536 | bytes 7077900 | tf_op jit(solution)/shard_map/kijb,kba->kija/dot_general | solution.py:57
  16.9 4.5 %fusion.56 = f32[3,32,32,256]{3,2,1,0:T(8,128)} fusion(f32[1,4,32,32,256]{4,3,2,1,0:T(8,128)S(1)} %copy-done.3, f32[3]{0:T(128)S(1)} %bitcast.145, f32[1,3,256,256]{3,2,1,0:T(8,128)S(1)} %copy-done.4), kind=kOutput, calls=%fused_computation.79 | convolution fusion | flops 2416705536 | bytes 7078400 | tf_op jit(solution)/shard_map/kijb,kab->kija/dot_general | solution.py:47
  23.6 2.9 collective-permute-start.2
  26.5 3.2 collective-permute-start.3
  31.5 18.8 %broadcast_multiply_fusion.1 = (f32[4,32,32,256]{3,2,1,0:T(8,128)}, f32[4,32,32,256]{3,2,1,0:T(8,128)}) fusion(f32[32,32]{1,0:T(8,128)S(1)} %broadcast_select_fusion, f32[1,4,32,32,256]{4,3,2,1,0:T(8,128)} %param.16, f32[4,32,32,256]{3,2,1,0:T(8,128)} %bitcast.136, f32[32,32,256]{2,1,0:T(8,128)S(1)} %bitcast.149, f32[3,32,32,256]{3,2,1,0:T(8,128)} %fusion.59, ...), kind=kOutput, calls=%fused_computation.78 | convolution fusion | flops 3252682752 | bytes 25718928 | tf_op jit(solution)/shard_map/kijb,kab->kija/dot_general | solution.py:41
  50.3 5.0 %gather_fusion = f32[128,4,8,256]{3,2,1,0:T(8,128)} fusion(f32[4,128,8,256]{3,2,1,0:T(8,128)} %bitcast.140, s32[1024]{0:T(1024)S(1)} %pad_clamp_fusion.1), kind=kCustom, calls=%fused_computation.clone | custom fusion | bytes 8389120 | tf_op jit(solution)/shard_map/jit(_take)/gather | solution.py:85
  55.3 2.5 bitcast_select_fusion.1
  57.9 4.1 concatenate.57
  62.0 9.9 %all-to-all-start = ((f32[4,128,2,8,256]{4,3,0,2,1:T(8,128)}), f32[4,128,2,8,256]{4,3,0,2,1:T(8,128)}, u32[]{:S(2)}, u32[]{:S(2)}) async-start(f32[4,128,2,8,256]{4,3,0,2,1:T(8,128)} %concatenate.57), calls=%async_computation | async-start | bytes 16777216 | tf_op jit(solution)/shard_map/all_to_all | solution.py:89
  72.3 1.8 copy.66
  74.2 101.2 %all-to-all-done = f32[4,128,2,8,256]{4,3,0,2,1:T(8,128)} async-done(((f32[4,128,2,8,256]{4,3,0,2,1:T(8,128)}), f32[4,128,2,8,256]{4,3,0,2,1:T(8,128)}, u32[]{:S(2)}, u32[]{:S(2)}) %all-to-all-start) | async-done | bytes 8388640 | tf_op jit(solution)/shard_map/all_to_all | solution.py:89
  175.4 4.8 %slice.119 = f32[4,64,2,8,256]{4,3,0,2,1:T(8,128)} slice(f32[4,128,2,8,256]{4,3,0,2,1:T(8,128)} %all-to-all-done), slice={[0:4], [0:64], [0:2], [0:8], [0:256]} | slice | bytes 8388608 | tf_op jit(solution)/shard_map/slice | solution.py:89
  180.2 23.2 %gather_fusion.1 = f32[512,4,8,256]{3,2,1,0:T(8,128)} fusion(f32[4,128,8,256]{3,2,0,1:T(8,128)} %bitcast.131, s32[1024]{0:T(1024)S(1)} %pad_clamp_fusion), kind=kCustom, calls=%fused_computation.1.clone | custom fusion | bytes 33556480 | tf_op jit(solution)/shard_map/jit(_take)/gather | solution.py:93
  203.4 13.8 %fusion.48 = f32[4,128,8,256]{3,2,0,1:T(8,128)S(1)} fusion(f32[128,4,4,8,256]{4,3,2,1,0:T(8,128)} %bitcast.133, pred[128,4]{1,0:T(8,128)(4,1)S(1)} %copy.46, f32[128,4,8,8,1]{3,2,1,4,0:T(8,128)S(1)} %copy.66), kind=kOutput, calls=%fused_computation.73 | convolution fusion | flops 406847488 | bytes 21103104 | tf_op jit(solution)/shard_map/bmij,kbmja->kbia/dot_general | solution.py:94
  217.2 14.2 %fusion.36 = f32[1024,4,256,1]{2,0,3,1:T(8,128)S(1)} fusion(f32[4,128,8,256]{3,2,0,1:T(8,128)S(1)} %fusion.48, f32[4,256,4,256]{3,2,1,0:T(4,128)S(1)} %copy-done.12), kind=kOutput, calls=%fused_computation.56 | convolution fusion | flops 12884901888 | bytes 12582912 | tf_op jit(solution)/shard_map/kna,kalb->lnb/dot_general | solution.py:102
  232.0 1.9 collective-permute-start.5
  234.0 6.0 %collective-permute-start.4 = (f32[4,1,32,256]{3,2,1,0:T(8,128)S(1)}, f32[4,1,32,256]{3,2,1,0:T(8,128)S(1)}, u32[]{:S(2)}, u32[]{:S(2)}) collective-permute-start(f32[4,1,32,256]{3,2,1,0:T(8,128)S(1)} %get-tuple-element.9), channel_id=1, source_target_pairs={{8,0},{16,8},{24,16},{32,24},{40,32},{48,40},{56,48},{9,1},{17,9},... | collective-permute-start | bytes 393224 | tf_op jit(solution)/shard_map/ppermute | solution.py:26
  240.0 4.5 %convolution_multiply_fusion.1 = f32[3,32,32,256]{3,2,1,0:T(8,128)} fusion(f32[4,32,32,256]{3,2,1,0:T(8,128)S(1)} %subtract_add_fusion, f32[3]{0:T(128)S(1)} %bitcast.146, f32[1,3,256,256]{3,2,1,0:T(8,128)S(1)} %copy-done.5), kind=kOutput, calls=%fused_computation.82 | convolution fusion | flops 2416705536 | bytes 8126476 | tf_op jit(solution)/shard_map/kijb,kab->kija/dot_general | solution.py:47
  244.7 3.1 collective-permute-start.6
  247.7 2.5 collective-permute-start.7
  250.2 4.4 convolution_multiply_fusion
  255.3 19.5 %broadcast_multiply_fusion = (f32[4,32,32,256]{3,2,1,0:T(8,128)}, f32[4,32,32,256]{3,2,1,0:T(8,128)}) fusion(f32[32,32]{1,0:T(8,128)S(1)} %broadcast_select_fusion, f32[1,4,32,32,256]{4,3,2,1,0:T(8,128)} %param.17, f32[4,32,32,256]{3,2,1,0:T(8,128)} %copy-done.2, f32[32,32,256]{2,1,0:T(8,128)} %bitcast.148, ...), kind=kOutput, calls=%fused_computation.77 | convolution fusion | flops 3252682752 | bytes 25718928 | tf_op jit(solution)/shard_map/kijb,kab->kija/dot_general | solution.py:41
  274.8 5.0 %gather_fusion.2 = f32[128,4,8,256]{3,2,1,0:T(8,128)} fusion(f32[4,128,8,256]{3,2,1,0:T(8,128)} %bitcast.139, s32[1024]{0:T(1024)S(1)} %pad_clamp_fusion.1), kind=kCustom, calls=%fused_computation.2.clone | custom fusion | bytes 8389120 | tf_op jit(solution)/shard_map/jit(_take)/gather | solution.py:85
  279.8 2.5 bitcast_select_fusion
  283.5 103.0 %all_to_all.10 = f32[4,128,2,8,256]{4,3,0,2,1:T(8,128)S(1)} all-to-all(f32[4,128,2,8,256]{4,3,0,2,1:T(8,128)S(1)} %concatenate.65), channel_id=1, replica_groups=mesh['sec'=2,'rr'=8,'sr'=8] {'sec','rr','sr'}, dimensions={1} | all-to-all | bytes 16777216 | tf_op jit(solution)/shard_map/all_to_all | solution.py:89
  386.4 2.3 slice.122
  388.8 23.2 %gather_fusion.3 = f32[512,4,8,256]{3,2,1,0:T(8,128)} fusion(f32[4,128,8,256]{3,2,0,1:T(8,128)} %bitcast.130, s32[1024]{0:T(1024)S(1)} %pad_clamp_fusion), kind=kCustom, calls=%fused_computation.3.clone | custom fusion | bytes 33556480 | tf_op jit(solution)/shard_map/jit(_take)/gather | solution.py:93
  412.0 13.5 %fusion.51 = f32[4,128,8,256]{3,2,0,1:T(8,128)S(1)} fusion(f32[128,4,4,8,256]{4,3,2,1,0:T(8,128)} %bitcast.132, pred[128,4]{1,0:T(8,128)(4,1)S(1)} %copy.46, f32[128,4,8,8,1]{3,2,1,4,0:T(8,128)S(1)} %copy.66), kind=kOutput, calls=%fused_computation.74 | convolution fusion | flops 406847488 | bytes 21103104 | tf_op jit(solution)/shard_map/bmij,kbmja->kbia/dot_general | solution.py:94
  425.5 14.2 %fusion.34 = f32[1024,4,256,1]{2,0,3,1:T(8,128)S(1)} fusion(f32[4,128,8,256]{3,2,0,1:T(8,128)S(1)} %fusion.51, f32[4,256,4,256]{3,2,1,0:T(4,128)S(1)} %copy-done.13), kind=kOutput, calls=%fused_computation.54 | convolution fusion | flops 12884901888 | bytes 12582912 | tf_op jit(solution)/shard_map/kna,kalb->lnb/dot_general | solution.py:102
  439.7 2.7 add_bitcast_fusion
  (68 shorter events, 8.2 us)
Async XLA Ops:
  0.6 30.9 %copy-start = (f32[1,4,256,256]{3,2,1,0:T(8,128)S(1)}, f32[1,4,256,256]{3,2,1,0:T(8,128)}, u32[]{:S(2)}) copy-start(f32[1,4,256,256]{3,2,1,0:T(8,128)} %param.21) | copy-start | bytes 3145732
  0.6 16.3 %copy-start.3 = (f32[1,4,32,32,256]{4,3,2,1,0:T(8,128)S(1)}, f32[1,4,32,32,256]{4,3,2,1,0:T(8,128)}, u32[]{:S(2)}) copy-start(f32[1,4,32,32,256]{4,3,2,1,0:T(8,128)} %param.17) | copy-start | bytes 12582916
  0.7 16.3 %copy-start.4 = (f32[1,3,256,256]{3,2,1,0:T(8,128)S(1)}, f32[1,3,256,256]{3,2,1,0:T(8,128)}, u32[]{:S(2)}) copy-start(f32[1,3,256,256]{3,2,1,0:T(8,128)} %param.22) | copy-start | bytes 2359300
  1.8 20.0 %collective-permute-start.1 = (f32[4,1,32,256]{3,2,1,0:T(8,128)S(1)}, f32[4,1,32,256]{3,2,1,0:T(8,128)S(1)}, u32[]{:S(2)}, u32[]{:S(2)}) collective-permute-start(f32[4,1,32,256]{3,2,1,0:T(8,128)S(1)} %get-tuple-element.10), channel_id=1, source_target_pairs={{0,8},{8,16},{16,24},{24,32},{32,40},{40,48},{48,56},{1,9},{9,17},... | collective-permute-start | bytes 393224 | tf_op jit(solution)/shard_map/ppermute | solution.py:25
  5.5 16.3 %collective-permute-start = (f32[4,1,32,256]{3,2,1,0:T(8,128)S(1)}, f32[4,1,32,256]{3,2,1,0:T(8,128)S(1)}, u32[]{:S(2)}, u32[]{:S(2)}) collective-permute-start(f32[4,1,32,256]{3,2,1,0:T(8,128)S(1)} %get-tuple-element.11), channel_id=1, source_target_pairs={{8,0},{16,8},{24,16},{32,24},{40,32},{48,40},{56,48},{9,1},{17,9},... | collective-permute-start | bytes 393224 | tf_op jit(solution)/shard_map/ppermute | solution.py:26
  16.9 4.5 %copy-start.9 = (s32[64,64,2]{1,2,0:T(2,128)S(1)}, s32[64,64,2]{1,2,0:T(2,128)}, u32[]{:S(2)}) copy-start(s32[64,64,2]{1,2,0:T(2,128)} %param.25) | copy-start | bytes 98308
  16.9 4.8 %copy-start.10 = (f32[32,32]{1,0:T(8,128)S(1)}, f32[32,32]{1,0:T(8,128)}, u32[]{:S(2)}) copy-start(f32[32,32]{1,0:T(8,128)} %param.20) | copy-start | bytes 12292
  21.5 10.1 %copy-start.14 = (f32[1,32,32,256]{3,2,1,0:T(8,128)S(1)}, f32[1,32,32,256]{3,2,1,0:T(8,128)}, u32[]{:S(2)}) copy-start(f32[1,32,32,256]{3,2,1,0:T(8,128)} %param.18) | copy-start | bytes 3145732
  21.5 10.1 %copy-start.16 = (f32[1,32,32]{2,1,0:T(8,128)S(1)}, f32[1,32,32]{2,1,0:T(8,128)}, u32[]{:S(2)}) copy-start(f32[1,32,32]{2,1,0:T(8,128)} %param.19) | copy-start | bytes 12292
  23.6 6.7 %collective-permute-start.2 = (f32[4,34,1,256]{3,2,1,0:T(1,128)S(1)}, f32[4,34,1,256]{3,2,1,0:T(1,128)S(1)}, u32[]{:S(2)}, u32[]{:S(2)}) collective-permute-start(f32[4,34,1,256]{3,2,1,0:T(1,128)S(1)} %get-tuple-element.6), channel_id=1, source_target_pairs={{1,0},{2,1},{3,2},{4,3},{5,4},{6,5},{7,6},{9,8},{10,9},{11,10},{12... | collective-permute-start | bytes 417800 | tf_op jit(solution)/shard_map/ppermute | solution.py:26
  26.5 5.0 %collective-permute-start.3 = (f32[4,34,1,256]{3,2,1,0:T(1,128)S(1)}, f32[4,34,1,256]{3,2,1,0:T(1,128)S(1)}, u32[]{:S(2)}, u32[]{:S(2)}) collective-permute-start(f32[4,34,1,256]{3,2,1,0:T(1,128)S(1)} %get-tuple-element.7), channel_id=1, source_target_pairs={{0,1},{1,2},{2,3},{3,4},{4,5},{5,6},{6,7},{8,9},{9,10},{10,11},{11... | collective-permute-start | bytes 417800 | tf_op jit(solution)/shard_map/ppermute | solution.py:25
  62.0 9.9 %copy-start.11 = (s32[1,1,128,4]{2,3,1,0:T(4,128)S(1)}, s32[1,1,128,4]{2,3,1,0:T(4,128)}, u32[]{:S(2)}) copy-start(s32[1,1,128,4]{2,3,1,0:T(4,128)} %param.26) | copy-start | bytes 6148
  62.0 10.3 %copy-start.8 = (f32[1,1,128,4,8,8]{2,5,4,3,1,0:T(8,128)S(1)}, f32[1,1,128,4,8,8]{2,5,4,3,1,0:T(8,128)}, u32[]{:S(2)}) copy-start(f32[1,1,128,4,8,8]{2,5,4,3,1,0:T(8,128)} %param.27) | copy-start | bytes 393220
  62.0 113.4 %all-to-all-start = ((f32[4,128,2,8,256]{4,3,0,2,1:T(8,128)}), f32[4,128,2,8,256]{4,3,0,2,1:T(8,128)}, u32[]{:S(2)}, u32[]{:S(2)}) async-start(f32[4,128,2,8,256]{4,3,0,2,1:T(8,128)} %concatenate.57), calls=%async_computation | async-start | bytes 16777216 | tf_op jit(solution)/shard_map/all_to_all | solution.py:89
  203.4 13.8 %copy-start.12 = (f32[4,256,4,256]{3,2,1,0:T(4,128)S(1)}, f32[4,256,4,256]{3,2,1,0:T(4,128)}, u32[]{:S(2)}) copy-start(f32[4,256,4,256]{3,2,1,0:T(4,128)} %param.24) | copy-start | bytes 12582916
  217.2 14.2 %copy-start.6 = (f32[4,32,32,256]{3,2,1,0:T(8,128)S(1)}, f32[4,32,32,256]{3,2,1,0:T(8,128)}, u32[]{:S(2)}) copy-start(f32[4,32,32,256]{3,2,1,0:T(8,128)} %get-tuple-element.13) | copy-start | bytes 12582916
  231.4 8.6 %copy-start.5 = (f32[1,3,256,256]{3,2,1,0:T(8,128)S(1)}, f32[1,3,256,256]{3,2,1,0:T(8,128)}, u32[]{:S(2)}) copy-start(f32[1,3,256,256]{3,2,1,0:T(8,128)} %param.22) | copy-start | bytes 2359300
  232.0 18.2 %copy-start.2 = (f32[4,32,32,256]{3,2,1,0:T(8,128)}, f32[4,32,32,256]{3,2,1,0:T(8,128)S(1)}, u32[]{:S(2)}) copy-start(f32[4,32,32,256]{3,2,1,0:T(8,128)S(1)} %subtract_add_fusion) | copy-start | bytes 12582916
  232.0 12.4 %collective-permute-start.5 = (f32[4,1,32,256]{3,2,1,0:T(8,128)S(1)}, f32[4,1,32,256]{3,2,1,0:T(8,128)S(1)}, u32[]{:S(2)}, u32[]{:S(2)}) collective-permute-start(f32[4,1,32,256]{3,2,1,0:T(8,128)S(1)} %get-tuple-element.8), channel_id=1, source_target_pairs={{0,8},{8,16},{16,24},{24,32},{32,40},{40,48},{48,56},{1,9},{9,17},... | collective-permute-start | bytes 393224 | tf_op jit(solution)/shard_map/ppermute | solution.py:25
  234.0 10.5 %collective-permute-start.4 = (f32[4,1,32,256]{3,2,1,0:T(8,128)S(1)}, f32[4,1,32,256]{3,2,1,0:T(8,128)S(1)}, u32[]{:S(2)}, u32[]{:S(2)}) collective-permute-start(f32[4,1,32,256]{3,2,1,0:T(8,128)S(1)} %get-tuple-element.9), channel_id=1, source_target_pairs={{8,0},{16,8},{24,16},{32,24},{40,32},{48,40},{56,48},{9,1},{17,9},... | collective-permute-start | bytes 393224 | tf_op jit(solution)/shard_map/ppermute | solution.py:26
  244.7 10.0 %collective-permute-start.6 = (f32[4,34,1,256]{3,2,1,0:T(1,128)S(1)}, f32[4,34,1,256]{3,2,1,0:T(1,128)S(1)}, u32[]{:S(2)}, u32[]{:S(2)}) collective-permute-start(f32[4,34,1,256]{3,2,1,0:T(1,128)S(1)} %get-tuple-element.4), channel_id=1, source_target_pairs={{1,0},{2,1},{3,2},{4,3},{5,4},{6,5},{7,6},{9,8},{10,9},{11,10},{12... | collective-permute-start | bytes 417800 | tf_op jit(solution)/shard_map/ppermute | solution.py:26
  247.7 7.6 %collective-permute-start.7 = (f32[4,34,1,256]{3,2,1,0:T(1,128)S(1)}, f32[4,34,1,256]{3,2,1,0:T(1,128)}, u32[]{:S(2)}, u32[]{:S(2)}) collective-permute-start(f32[4,34,1,256]{3,2,1,0:T(1,128)S(1)} %get-tuple-element.5), channel_id=1, source_target_pairs={{0,1},{1,2},{2,3},{3,4},{4,5},{5,6},{6,7},{8,9},{9,10},{10,11},{11... | collective-permute-start | bytes 417800 | tf_op jit(solution)/shard_map/ppermute | solution.py:25
  254.6 0.7 copy-start.15
  412.0 13.5 %copy-start.13 = (f32[4,256,4,256]{3,2,1,0:T(4,128)S(1)}, f32[4,256,4,256]{3,2,1,0:T(4,128)}, u32[]{:S(2)}) copy-start(f32[4,256,4,256]{3,2,1,0:T(4,128)} %param.24) | copy-start | bytes 12582916
  425.5 14.2 %copy-start.7 = (f32[4,32,32,256]{3,2,1,0:T(8,128)S(1)}, f32[4,32,32,256]{3,2,1,0:T(8,128)}, u32[]{:S(2)}) copy-start(f32[4,32,32,256]{3,2,1,0:T(8,128)} %get-tuple-element.15) | copy-start | bytes 12582916
  439.7 2.7 copy-start.1
where the time goes:
time: 451 us; the launch traced here: 443 us
  matrix products  114 us (25%)
  waiting for transfers between devices  103 us (23%)
  blocking collectives  103 us (23%)
  local copies, waits for them, and re-layouts  73.6 us (16%)
  starting transfers between devices  37.4 us (8%)
  other arithmetic  10.4 us (2%)
    all_to_all x1, blocking collectives, transfer(): lax.all_to_all(outgoing, ('sec', 'rr', 'sr'), split_axis=1, concat_axis=1...  103 us
    all_to_all x1, waiting for transfers between devices, transfer(): lax.all_to_all(outgoing, ('sec', 'rr', 'sr'), split_axis=1, concat_axis=1...  101 us
    gather x2, local copies, waits for them, and re-layouts, transfer(): selected = jnp.take(slot_rows, pick_slots[0, 0], axis=1)  46.5 us
    dot_general x2, matrix products, hamilton(): jnp.einsum('kijb,kab->kija', state_field, angles, precision=highest, pref...  38.3 us
    dot_general x2, matrix products, transfer(): jnp.einsum('kna,kalb->lnb', row_values, frame_map, precision=highest, pre...  28.3 us
    dot_general x2, matrix products, transfer(): jnp.einsum('bmij,kbmja->kbia', interp_weights[0, 0], selected, precision=...  27.2 us
    ppermute x4, starting transfers between devices, with_halo(): after = lax.ppermute(first, axis, down)  16.1 us
    ppermute x4, starting transfers between devices, with_halo(): before = lax.ppermute(last, axis, up)  11.3 us
  transfers between devices with their start and end apart: 9, of which 3 were waited for; matrix products, arithmetic and copies ran while one was open for 5% of the time, Pallas kernels for 0%

commit v1 on v0

v1 whole, which is shorter than its diff:
```python
import functools

import jax
import jax.numpy as jnp
from jax import lax
from jax.experimental import pallas as pl
from jax.experimental.pallas import tpu as pltpu
from jax.sharding import PartitionSpec as P

JTOT = 23
HEL = 4
NA = 256
CR = 32
CS = 32
PTS = CR * CS
BLK = 8
NBLK = PTS // BLK
SRCS = 64
MSLOT = 4
TI = 8
ROWS = TI * CS
MIB = 1 << 20

kinetic = 0.08
rotor_scale = 0.1
centrifugal = 0.0005
coriolis_scale = 0.005
F32 = jnp.float32
BF16 = jnp.bfloat16
ALL = ("sec", "rr", "sr")


def dot(a, b):
    return jnp.dot(a, b, preferred_element_type=F32)


def split(x):
    high = x.astype(BF16)
    return high, (x - high.astype(F32)).astype(BF16)


def whole(shape, space=pltpu.VMEM):
    return pl.BlockSpec(shape, lambda *_: (0,) * len(shape), memory_space=space)


def smem():
    return pl.BlockSpec(memory_space=pltpu.SMEM)


def split_kernel(x_ref, high_ref, low_ref):
    high, low = split(x_ref[...])
    high_ref[...] = high
    low_ref[...] = low


def split_call(x, rows):
    total, width = x.shape
    spec = pl.BlockSpec((rows, width), lambda i: (i, 0))
    return pl.pallas_call(
        split_kernel,
        grid=(total // rows,),
        in_specs=[spec],
        out_specs=[spec, spec],
        out_shape=[jax.ShapeDtypeStruct(x.shape, BF16)] * 2,
        cost_estimate=pl.CostEstimate(flops=4 * x.size, transcendentals=0, bytes_accessed=8 * x.size),
        name="split_weights",
    )(x)


def blend_kernel(column_ref, live_ref, tile_ref, high_ref, low_ref, full):
    full[...] = jnp.zeros_like(full)
    lane_block = lax.broadcasted_iota(jnp.int32, (BLK, 128), 1) // BLK
    live = live_ref[0]

    def place(b, carry):
        row = pl.multiple_of(b * BLK, BLK)
        for m in range(MSLOT):
            column = column_ref[b * MSLOT + m]
            lane = pl.multiple_of((column // 16) * 128, 128)
            piece = jnp.where(lane_block == column % 16, tile_ref[b, m] * live, 0.0)
            full[pl.ds(row, BLK), pl.ds(lane, 128)] += piece
        return carry

    lax.fori_loop(0, NBLK, place, 0)

    def store(r, carry):
        row = pl.multiple_of(r * 64, 64)
        high, low = split(full[pl.ds(row, 64), :])
        high_ref[pl.ds(row, 64), :] = high
        low_ref[pl.ds(row, 64), :] = low
        return carry

    lax.fori_loop(0, PTS // 64, store, 0)


def blend_call(columns, live, tiles):
    return pl.pallas_call(
        blend_kernel,
        in_specs=[smem(), smem(), pl.BlockSpec(memory_space=pltpu.VMEM)],
        out_specs=[pl.BlockSpec(memory_space=pltpu.VMEM)] * 2,
        out_shape=[jax.ShapeDtypeStruct((PTS, PTS), BF16)] * 2,
        scratch_shapes=[pltpu.VMEM((PTS, PTS), F32)],
        compiler_params=pltpu.CompilerParams(vmem_limit_bytes=24 * MIB),
        cost_estimate=pl.CostEstimate(flops=8 * MIB, transcendentals=0, bytes_accessed=6 * MIB),
        name="blend_matrix",
    )(columns, live, tiles)


def step_kernel(want_own, want_pack, *refs):
    refs = list(refs)
    ids = refs.pop(0)
    u_ref, centre_ref, now, up, down, left, right, prev, pot, coef, w_high, w_low = refs[:12]
    refs = refs[12:]
    own_ref = refs.pop(0) if want_own else None
    pack_one, pack_zero = (refs.pop(0), refs.pop(0)) if want_pack else (None, None)
    rot, mix = refs.pop(0), refs.pop(0)
    absorbed = refs.pop(0) if want_pack else None
    chunk = pl.program_id(0)
    first = chunk * TI
    parts = [split(now[k, pl.ds(first, TI)].reshape(ROWS, NA)) for k in range(HEL)]

    def product(k, w):
        high, low = parts[k]
        return dot(high, w_high[w]) + dot(low, w_high[w]) + dot(high, w_low[w])

    for k in range(HEL):
        rot[k] = product(k, k)
        total = None
        if k < HEL - 1:
            total = product(k + 1, HEL + k)
        if k > 0:
            lower = product(k - 1, 2 * HEL - 2 + k)
            total = lower if total is None else total + lower
        mix[k] = total

    bond = lax.broadcasted_iota(jnp.int32, (CS, NA), 0)

    def row(t, carry):
        i = first + t
        u = u_ref[i]
        start = pl.multiple_of(t * CS, CS)
        damp, share, spin = (jnp.concatenate([coef[n, t]] * 2, axis=1) for n in range(3))
        well = pot[t] + 4.0 * kinetic
        for k in range(HEL):
            v = now[k, i]
            before = jnp.where(i == 0, up[k], now[k, jnp.maximum(i - 1, 0)])
            after = jnp.where(i == CR - 1, down[k], now[k, jnp.minimum(i + 1, CR - 1)])
            lower = jnp.where(bond == 0, left[k, pl.ds(i, 1), :], pltpu.roll(v, 1, 0))
            upper = jnp.where(bond == CS - 1, right[k, pl.ds(i, 1), :], pltpu.roll(v, CS - 1, 0))
            applied = (
                (well + u * centre_ref[k]) * v
                - kinetic * ((before + after) + (lower + upper))
                + spin * rot[k, pl.ds(start, CS), :]
                + u * mix[k, pl.ds(start, CS), :]
            )
            renewed = damp * (2.0 * applied - damp * prev[k, t])
            taken = share * renewed
            if want_own:
                own_ref[k, t] = renewed - taken
            if want_pack:
                absorbed[k, i] = taken
        return carry

    lax.fori_loop(0, TI, row, 0)

    if want_pack:

        @pl.when(chunk == CR // TI - 1)
        def _():
            def move(q, carry):
                for offset, target in ((0, pack_zero), (SRCS, pack_one)):
                    e = ids[offset + q]
                    i = e // (CS // BLK)
                    j = pl.multiple_of((e % (CS // BLK)) * BLK, BLK)
                    for k in range(HEL):
                        target[q, k] = absorbed[k, i, pl.ds(j, BLK), :]
                return carry

            lax.fori_loop(0, SRCS, move, 0)


def step_call(want_own, want_pack, ids, u, centre, now, halo, prev, pot, coef, w_high, w_low):
    field = (HEL, CR, CS, NA)
    rows = pl.BlockSpec((HEL, TI, CS, NA), lambda c: (0, c, 0, 0))
    out_specs, out_shape, scratch = [], [], []
    if want_own:
        out_specs.append(rows)
        out_shape.append(jax.ShapeDtypeStruct(field, F32))
    if want_pack:
        packed = (SRCS, HEL, BLK, NA)
        out_specs += [whole(packed)] * 2
        out_shape += [jax.ShapeDtypeStruct(packed, F32)] * 2
    scratch += [pltpu.VMEM((HEL, ROWS, NA), F32)] * 2
    if want_pack:
        scratch.append(pltpu.VMEM(field, F32))
    return pl.pallas_call(
        functools.partial(step_kernel, want_own, want_pack),
        grid=(CR // TI,),
        in_specs=[
            smem(),
            smem(),
            smem(),
            whole(field),
            whole((HEL, CS, NA)),
            whole((HEL, CS, NA)),
            whole((HEL, CR, NA)),
            whole((HEL, CR, NA)),
            rows,
            pl.BlockSpec((TI, CS, NA), lambda c: (c, 0, 0)),
            pl.BlockSpec((3, TI, CS, 128), lambda c: (0, c, 0, 0)),
            whole((10, NA, NA)),
            whole((10, NA, NA)),
        ],
        out_specs=out_specs,
        out_shape=out_shape,
        scratch_shapes=scratch,
        compiler_params=pltpu.CompilerParams(vmem_limit_bytes=48 * MIB),
        cost_estimate=pl.CostEstimate(flops=30 * 2 * PTS * NA * NA, transcendentals=0, bytes_accessed=20 * MIB),
        name="step_own" if want_own and not want_pack else "step_pack" if not want_own else "step_both",
    )(ids, u, centre, now, *halo, prev, pot, coef, w_high, w_low)


def inflow_kernel(x_ref, f_high, f_low, b_high, b_low, acc_ref, out_ref, x_high, x_low):
    half = SRCS * BLK

    @pl.when(pl.program_id(0) == 0)
    def _():
        for k in range(HEL):
            high, low = split(x_ref[:, k].reshape(half, NA))
            x_high[k] = high
            x_low[k] = low

    framed = None
    for k in range(HEL):
        rows = slice(k * NA, (k + 1) * NA)
        term = dot(x_high[k], f_high[rows]) + dot(x_low[k], f_high[rows]) + dot(x_high[k], f_low[rows])
        framed = term if framed is None else framed + term
    high, low = split(framed)
    for r in range(4):
        rows = slice(r * PTS // 4, (r + 1) * PTS // 4)
        out_ref[0, rows] = acc_ref[0, rows] + (dot(b_high[rows], high) + dot(b_low[rows], high) + dot(b_high[rows], low))


def inflow_call(part, x, frame, blend, acc):
    half = SRCS * BLK
    column = pl.BlockSpec((HEL * NA, NA), lambda n: (0, n))
    weights = pl.BlockSpec((PTS, half), lambda n: (0, part))
    field = pl.BlockSpec((1, PTS, NA), lambda n: (n, 0, 0))
    return pl.pallas_call(
        inflow_kernel,
        grid=(HEL,),
        in_specs=[whole((SRCS, HEL, BLK, NA)), column, column, weights, weights, field],
        out_specs=field,
        out_shape=jax.ShapeDtypeStruct((HEL, PTS, NA), F32),
        scratch_shapes=[pltpu.VMEM((HEL, half, NA), BF16)] * 2,
        compiler_params=pltpu.CompilerParams(vmem_limit_bytes=40 * MIB),
        cost_estimate=pl.CostEstimate(flops=12 * half * PTS * PTS, transcendentals=0, bytes_accessed=16 * MIB),
        name="inflow",
    )(x, *frame, *blend, acc)


def edges(x):
    rows, columns = lax.axis_size("rr"), lax.axis_size("sr")

    def send(piece, axis, peers, forward):
        pairs = [(i, i + 1) if forward else (i + 1, i) for i in range(peers - 1)]
        return lax.ppermute(piece, axis, pairs)

    return (
        send(x[:, CR - 1], "rr", rows, True),
        send(x[:, 0], "rr", rows, False),
        send(x[:, :, CS - 1], "sr", columns, True),
        send(x[:, :, 0], "sr", columns, False),
    )


def cross(x):
    pairs = [(s, SRCS + (s ^ (SRCS // 2))) for s in range(SRCS)]
    return lax.ppermute(x, ALL, pairs)


def spread(x):
    return lax.all_to_all(x, ("rr", "sr"), split_axis=0, concat_axis=0, tiled=True)


def per_device(
    wave_prev,
    wave_now,
    potential,
    damping,
    switch,
    angular,
    coriolis,
    helicity_start,
    frame_map,
    route_table,
    pick_slots,
    interp_weights,
):
    section = lax.axis_index("sec")
    row_slab = lax.axis_index("rr")
    col_slab = lax.axis_index("sr")
    previous, current, pot = wave_prev[0], wave_now[0], potential[0]
    halo = edges(current)

    radial_pos = (row_slab * CR + jnp.arange(CR)).astype(F32)
    bond_pos = (col_slab * CS + jnp.arange(CS)).astype(F32)
    radial = (1.0 + 3.0 * radial_pos / float(lax.axis_size("rr") * CR)) ** (-2)
    bond = (1.0 + 3.0 * bond_pos / float(lax.axis_size("sr") * CS)) ** (-2)
    helicity = helicity_start[0].astype(F32) + jnp.arange(HEL, dtype=F32)
    total_j = float(JTOT * (JTOT + 1))
    ladder = coriolis_scale * jnp.sqrt(total_j - helicity * (helicity + 1.0))[:-1, None, None]
    centre = centrifugal * (total_j - 2.0 * helicity * helicity)
    coef = jnp.stack(
        [
            damping[0],
            jnp.where(section == 0, switch, 0.0),
            rotor_scale * (radial[:, None] + bond[None, :]),
        ]
    )
    coef = jnp.broadcast_to(coef[..., None], (3, CR, CS, 128))
    weights = jnp.concatenate(
        [jnp.swapaxes(angular[0], 1, 2), ladder * jnp.swapaxes(coriolis[0], 1, 2), ladder * coriolis[0]], 0
    )
    w_high, w_low = (w.reshape(10, NA, NA) for w in split_call(weights.reshape(10 * NA, NA), NA))

    me = row_slab * lax.axis_size("sr") + col_slab
    outgoing = jnp.maximum(lax.dynamic_index_in_dim(route_table, me, axis=1, keepdims=False), 0)
    flip = jnp.arange(SRCS) ^ (SRCS // 2)
    ids = jnp.concatenate([outgoing[flip, 0], outgoing[:, 1]])

    picks = pick_slots[0, 0].reshape(NBLK * MSLOT)
    source, slot = picks // 2, picks % 2
    columns = jnp.where(slot == 0, source, SRCS + (source ^ (SRCS // 2)))
    live = (section == 1).astype(F32).reshape(1)
    blend = blend_call(columns, live, jnp.tile(interp_weights[0, 0], (1, 1, 1, 128 // BLK)))
    frame = split_call(frame_map.reshape(HEL * NA, HEL * NA), NA)

    fixed = (pot, coef, w_high, w_low)
    field = (HEL, CR, CS, NA)
    flat = (HEL, PTS, NA)

    own_1, one_1, zero_1 = step_call(True, True, ids, radial, centre, current, halo, previous, *fixed)
    crossed_one_1 = cross(one_1)
    relayed_1 = spread(zero_1)
    crossed_zero_1 = cross(relayed_1)
    one_2, zero_2 = step_call(False, True, ids, radial, centre, own_1, edges(own_1), current, *fixed)
    crossed_one_2 = cross(one_2)
    shared = spread(jnp.where(section == 0, zero_2, crossed_one_1))
    crossed_zero_2 = cross(shared)

    new_1 = inflow_call(1, shared, frame, blend, own_1.reshape(flat))
    new_1 = inflow_call(0, crossed_zero_1, frame, blend, new_1).reshape(field)
    (own_2,) = step_call(True, False, ids, radial, centre, new_1, edges(new_1), current, *fixed)

    last_one = spread(crossed_one_2)
    new_2 = inflow_call(1, last_one, frame, blend, own_2.reshape(flat))
    new_2 = inflow_call(0, crossed_zero_2, frame, blend, new_2).reshape(field)
    return new_1[None], new_2[None]


def solution(mesh):
    placed = (
        P("sec", None, "rr", "sr", None),
        P("sec", None, "rr", "sr", None),
        P("sec", "rr", "sr", None),
        P("sec", "rr", "sr"),
        P("rr", "sr"),
        P("sec", None, None, None),
        P("sec", None, None, None),
        P("sec"),
        P(),
        P(),
        P("rr", "sr", None, None),
        P("rr", "sr", None, None, None, None),
    )
    return jax.shard_map(
        per_device,
        mesh=mesh,
        in_specs=placed,
        out_specs=(P("sec", None, "rr", "sr", None), P("sec", None, "rr", "sr", None)),
        check_vma=False,
    )
```

time: 451 us -> 297 us (0.66); the launches traced: 443 us -> 294 us
  Pallas kernels: 0 us -> 130 us
  matrix products: 114 us -> 0 us
  blocking collectives: 103 us -> 0 us
  waiting for transfers between devices: 103 us -> 35.8 us
  starting transfers between devices: 37.4 us -> 72.9 us
  local copies, waits for them, and re-layouts: 73.6 us -> 45.5 us
    pallas_call x0 -> x10, Pallas kernels: none -> 130 us  [the longest x4 69.5 us: inflow_call(): pl.pallas_call(inflow_kernel, grid=(HEL,), in_specs=[whole((SRCS, HEL, BL...]
    dot_general x10 -> x0, matrix products: 114 us -> none  [the longest x2 38.3 us: hamilton(): jnp.einsum('kijb,kab->kija', state_field, angles, precision=highest, pref...]
    all_to_all x1 -> x0, blocking collectives: 103 us -> none  [transfer(): lax.all_to_all(outgoing, ('sec', 'rr', 'sr'), split_axis=1, concat_axis=1...]
    all_to_all x1 -> x3, waiting for transfers between devices: 101 us -> 0.01 us  [spread(): lax.all_to_all(x, ('rr', 'sr'), split_axis=0, concat_axis=0, tiled=True)]
    gather x4 -> x1, local copies, waits for them, and re-layouts: 56.4 us -> 0.9 us  [per_device(): ids = jnp.concatenate([outgoing[flip, 0], outgoing[:, 1]])]
    ppermute x8 -> x16, waiting for transfers between devices: 1.35 us -> 35.8 us  [the longest x4 23 us: cross(): return lax.ppermute(x, ALL, pairs)]
    unnamed x35 -> x61, local copies, waits for them, and re-layouts: 0.83 us -> 24.7 us
    ppermute x8 -> x16, starting transfers between devices: 27.4 us -> 47.1 us  [the longest x12 41.7 us: send(): return lax.ppermute(piece, axis, pairs)]
  transfers between devices with their start and end apart: 9 -> 19, of which waited for: 3 -> 7; matrix products, arithmetic and copies ran while one was open for 5% -> 11% of each run, Pallas kernels for 0% -> 33%
where the time goes in v1:
time: 297 us; the launch traced here: 294 us
  Pallas kernels  130 us (44%)
  starting transfers between devices  72.9 us (25%)
  local copies, waits for them, and re-layouts  45.5 us (15%)
  waiting for transfers between devices  35.8 us (12%)
  other arithmetic  8.04 us (3%)
    pallas_call x4, Pallas kernels, inflow_call(): pl.pallas_call(inflow_kernel, grid=(HEL,), in_specs=[whole((SRCS, HEL, BL...  69.5 us
    pallas_call x3, Pallas kernels, step_call(): pl.pallas_call(functools.partial(step_kernel, want_own, want_pack), grid=...  42.9 us
    ppermute x12, starting transfers between devices, send(): return lax.ppermute(piece, axis, pairs)  41.7 us
    all_to_all x3, starting transfers between devices, spread(): lax.all_to_all(x, ('rr', 'sr'), split_axis=0, concat_axis=0, tiled=True)  25.8 us
    unnamed x61, local copies, waits for them, and re-layouts  24.7 us
    ppermute x4, waiting for transfers between devices, cross(): return lax.ppermute(x, ALL, pairs)  23 us
    ppermute x12, waiting for transfers between devices, send(): return lax.ppermute(piece, axis, pairs)  12.7 us
    pallas_call x2, Pallas kernels, split_call(): pl.pallas_call(split_kernel, grid=(total // rows,), in_specs=[spec], out_...  11.6 us
  transfers between devices with their start and end apart: 19, of which 7 were waited for; matrix products, arithmetic and copies ran while one was open for 11% of the time, Pallas kernels for 33%

profile of v1, /device:TPU:27, one launch (start us, length us, event | category | flops | bytes accessed | tf_op | source)
XLA Modules:
  0.0 293.9 jit_solution(16239645057284792873)
XLA Ops:
  2.5 3.7 %collective-permute-start.2 = (f32[4,32,256]{2,1,0:T(8,128)S(1)}, f32[4,32,256]{2,1,0:T(8,128)S(1)}, u32[]{:S(2)}, u32[]{:S(2)}) collective-permute-start(f32[4,32,256]{2,1,0:T(8,128)S(1)} %bitcast.95), channel_id=1, source_target_pairs={{0,1},{1,2},{2,3},{3,4},{4,5},{5,6},{6,7},{8,9},{9,10},{10,11},{11... | collective-permute-start | bytes 393224 | tf_op jit(solution)/shard_map/ppermute | solution.py:267
  10.5 3.5 %collective-permute-start = (f32[4,32,256]{2,1,0:T(8,128)}, f32[4,32,256]{2,1,0:T(8,128)S(1)}, u32[]{:S(2)}, u32[]{:S(2)}) collective-permute-start(f32[4,32,256]{2,1,0:T(8,128)} %get-tuple-element.35), channel_id=1, source_target_pairs={{0,8},{8,16},{16,24},{24,32},{32,40},{40,48},{48,56},{1,9},{9,17},... | collective-permute-start | bytes 393224 | tf_op jit(solution)/shard_map/ppermute | solution.py:267
  14.0 4.2 %collective-permute-start.1 = (f32[4,32,256]{2,1,0:T(8,128)}, f32[4,32,256]{2,1,0:T(8,128)S(1)}, u32[]{:S(2)}, u32[]{:S(2)}) collective-permute-start(f32[4,32,256]{2,1,0:T(8,128)} %get-tuple-element.34), channel_id=1, source_target_pairs={{8,0},{16,8},{24,16},{32,24},{40,32},{48,40},{56,48},{9,1},{17,9},... | collective-permute-start | bytes 393224 | tf_op jit(solution)/shard_map/ppermute | solution.py:267
  23.6 2.0 pad_maximum_fusion
  25.7 2.1 copy.40
  27.8 6.9 %split_weights.2 = (bf16[2560,256]{1,0:T(8,128)(2,1)}, bf16[2560,256]{1,0:T(8,128)(2,1)}) custom-call(f32[2560,256]{1,0:T(8,128)} %bitcast.81), custom_call_target="tpu_custom_call" | custom-call | flops 2621440 | bytes 5242880 | tf_op jit(solution)/shard_map/split_weights/pallas_call | solution.py:59
  38.4 15.1 %step_both.1 = (f32[4,32,32,256]{3,2,1,0:T(8,128)}, f32[64,4,8,256]{3,2,1,0:T(8,128)}, f32[64,4,8,256]{3,2,1,0:T(8,128)}) custom-call(s32[128]{0:T(128)S(1)} %pad_add_fusion.refs_0_, f32[32]{0:T(128)S(1)} %multiply_divide_fusion.1.refs_1_, f32[4]{0:T(128)S(1)} %fusion.4.refs_2_, f32[4,32,32,256]{3,2,1,0:T(8,128)} %bitcast.84, ...), custom_call_target="tpu_custom_call" | custom-call | flops 4026531840 | bytes 20971520 | tf_op jit(solution)/shard_map/step_both/pallas_call | solution.py:196
  54.9 8.4 %all-to-all-start = ((f32[64,4,8,256]{3,2,1,0:T(8,128)}), f32[64,4,8,256]{3,2,1,0:T(8,128)}, u32[]{:S(2)}, u32[]{:S(2)}) async-start(f32[64,4,8,256]{3,2,1,0:T(8,128)} %get-tuple-element.15), calls=%async_computation | async-start | bytes 4194304 | tf_op jit(solution)/shard_map/all_to_all | solution.py:283
  63.3 4.8 %copy.45 = f32[4,32,32,256]{3,1,0,2:T(8,128)S(1)} copy(f32[4,32,32,256]{3,2,1,0:T(8,128)} %get-tuple-element.20.refs_3_) | data formatting | bytes 8388608 | tf_op jit(solution)/shard_map/step_both/pallas_call | solution.py:196
  68.1 3.4 %collective-permute-start.7 = (f32[4,32,256]{2,1,0:T(8,128)S(1)}, f32[4,32,256]{2,1,0:T(8,128)S(1)}, u32[]{:S(2)}, u32[]{:S(2)}) collective-permute-start(f32[4,32,256]{2,1,0:T(8,128)S(1)} %get-tuple-element.29), channel_id=1, source_target_pairs={{0,1},{1,2},{2,3},{3,4},{4,5},{5,6},{6,7},{8,9},{9,10},{10,11},{11... | collective-permute-start | bytes 393224 | tf_op jit(solution)/shard_map/ppermute | solution.py:267
  74.4 3.1 %collective-permute-start.5 = (f32[4,32,256]{2,1,0:T(8,128)S(1)}, f32[4,32,256]{2,1,0:T(8,128)S(1)}, u32[]{:S(2)}, u32[]{:S(2)}) collective-permute-start(f32[4,32,256]{2,1,0:T(8,128)S(1)} %get-tuple-element.31), channel_id=1, source_target_pairs={{0,8},{8,16},{16,24},{24,32},{32,40},{40,48},{48,56},{1,9},{9,17},... | collective-permute-start | bytes 393224 | tf_op jit(solution)/shard_map/ppermute | solution.py:267
  77.6 4.2 %collective-permute-start.6 = (f32[4,32,256]{2,1,0:T(8,128)S(1)}, f32[4,32,256]{2,1,0:T(8,128)S(1)}, u32[]{:S(2)}, u32[]{:S(2)}) collective-permute-start(f32[4,32,256]{2,1,0:T(8,128)S(1)} %get-tuple-element.30), channel_id=1, source_target_pairs={{8,0},{16,8},{24,16},{32,24},{40,32},{48,40},{56,48},{9,1},{17,9},... | collective-permute-start | bytes 393224 | tf_op jit(solution)/shard_map/ppermute | solution.py:267
  81.8 5.5 %collective-permute-done.7.refs_6_ = f32[4,32,256]{2,1,0:T(8,128)S(1)} collective-permute-done((f32[4,32,256]{2,1,0:T(8,128)S(1)}, f32[4,32,256]{2,1,0:T(8,128)S(1)}, u32[]{:S(2)}, u32[]{:S(2)}) %collective-permute-start.7) | collective-permute-done | bytes 131104 | tf_op jit(solution)/shard_map/ppermute | solution.py:267
  87.4 2.0 collective-permute-done.8.refs_7_
  89.4 3.5 %collective-permute-done.5.refs_4_ = f32[4,32,256]{2,1,0:T(8,128)S(1)} collective-permute-done((f32[4,32,256]{2,1,0:T(8,128)S(1)}, f32[4,32,256]{2,1,0:T(8,128)S(1)}, u32[]{:S(2)}, u32[]{:S(2)}) %collective-permute-start.5) | collective-permute-done | bytes 131104 | tf_op jit(solution)/shard_map/ppermute | solution.py:267
  92.9 14.9 %step_pack.1 = (f32[64,4,8,256]{3,2,1,0:T(8,128)}, f32[64,4,8,256]{3,2,1,0:T(8,128)}) custom-call(s32[128]{0:T(128)S(1)} %pad_add_fusion.refs_0_, f32[32]{0:T(128)S(1)} %multiply_divide_fusion.1.refs_1_, f32[4]{0:T(128)S(1)} %fusion.4.refs_2_, f32[4,32,32,256]{3,2,1,0:T(8,128)} %get-tuple-element.20.refs_3_, ...), custom_call_target="tpu_custom_call" | custom-call | flops 4026531840 | bytes 20971520 | tf_op jit(solution)/shard_map/step_pack/pallas_call | solution.py:196
  109.0 3.5 %broadcast_select_fusion = f32[64,4,8,256]{3,2,1,0:T(8,128)} fusion(f32[64,4,8,256]{3,2,1,0:T(8,128)} %get-tuple-element.21, f32[64,4,8,256]{3,2,1,0:T(8,128)} %collective-permute-done.9, pred[]{:T(512)S(6)} %eq.13), kind=kLoop, calls=%fused_computation.3 | loop fusion | flops 524288 | bytes 6291457 | tf_op jit(solution)/shard_map/jit(_where)/select_n | solution.py:349
  112.6 7.1 %all-to-all-start.1 = ((f32[64,4,8,256]{3,2,1,0:T(8,128)}), f32[64,4,8,256]{3,2,1,0:T(8,128)}, u32[]{:S(2)}, u32[]{:S(2)}) async-start(f32[64,4,8,256]{3,2,1,0:T(8,128)} %broadcast_select_fusion), calls=%async_computation.1 | async-start | bytes 4194304 | tf_op jit(solution)/shard_map/all_to_all | solution.py:283
  122.7 2.4 copy.42.tile_ref
  125.3 5.2 %copy.58 = f32[128,8,4,256]{3,1,2,0:T(8,128)} copy(f32[128,8,4,256]{3,2,1,0:T(4,128)} %bitcast.92) | data formatting | bytes 8388608
  130.5 4.8 %split_weights.3 = (bf16[1024,1024]{1,0:T(8,128)(2,1)}, bf16[1024,1024]{1,0:T(8,128)(2,1)}) custom-call(f32[1024,1024]{1,0:T(8,128)} %bitcast.80), custom_call_target="tpu_custom_call" | custom-call | flops 4194304 | bytes 8388608 | tf_op jit(solution)/shard_map/split_weights/pallas_call | solution.py:59
  135.3 5.9 %blend_matrix.1 = (bf16[1024,1024]{1,0:T(8,128)(2,1)S(1)}, bf16[1024,1024]{1,0:T(8,128)(2,1)S(1)}) custom-call(s32[512]{0:T(512)S(1)} %add_select_fusion.2.column_ref, f32[1]{0:T(128)} %bitcast.17.live_ref, f32[128,4,8,128]{3,2,1,0:T(8,128)S(1)} %copy.42.tile_ref), custom_call_target="tpu_custom_call" | custom-call | flops 8388608 | bytes 6291456 | tf_op jit(solution)/shard_map/blend_matrix/pallas_call | solution.py:97
  143.8 13.6 %collective-permute-done.11 = f32[64,4,8,256]{3,2,1,0:T(8,128)} collective-permute-done((f32[64,4,8,256]{3,2,1,0:T(8,128)}, f32[64,4,8,256]{3,2,1,0:T(8,128)}, u32[]{:S(2)}, u32[]{:S(2)}) %collective-permute-start.11) | collective-permute-done | bytes 2097184 | tf_op jit(solution)/shard_map/ppermute | solution.py:279
  157.4 10.3 %all-to-all-start.2 = ((f32[64,4,8,256]{3,2,1,0:T(8,128)}), f32[64,4,8,256]{3,2,1,0:T(8,128)S(1)}, u32[]{:S(2)}, u32[]{:S(2)}) async-start(f32[64,4,8,256]{3,2,1,0:T(8,128)} %collective-permute-done.11), calls=%async_computation.2 | async-start | bytes 4194304 | tf_op jit(solution)/shard_map/all_to_all | solution.py:283
  175.3 17.5 %inflow.4.acc_ref = f32[4,1024,256]{2,1,0:T(8,128)} custom-call(f32[64,4,8,256]{3,2,1,0:T(8,128)} %all-to-all-done.1.x_ref, bf16[1024,1024]{1,0:T(8,128)(2,1)S(1)} %copy-done.12, bf16[1024,1024]{1,0:T(8,128)(2,1)S(1)} %copy-done.14, bf16[1024,1024]{1,0:T(8,128)(2,1)S(1)} %copy-done.17, bf16[1024,1024]{1,0:T(8,128)(2,1)S(1)} %copy-done.20, ...), custom_call_target="tpu_custom_call" | custom-call | flops 6442450944 | bytes 16777216 | tf_op jit(solution)/shard_map/inflow/pallas_call | solution.py:249
  192.8 9.5 %collective-permute-done.4.x_ref = f32[64,4,8,256]{3,2,1,0:T(8,128)} collective-permute-done((f32[64,4,8,256]{3,2,1,0:T(8,128)}, f32[64,4,8,256]{3,2,1,0:T(8,128)}, u32[]{:S(2)}, u32[]{:S(2)}) %collective-permute-start.4) | collective-permute-done | bytes 2097184 | tf_op jit(solution)/shard_map/ppermute | solution.py:279
  202.3 17.5 %inflow.5 = f32[4,1024,256]{2,1,0:T(8,128)} custom-call(f32[64,4,8,256]{3,2,1,0:T(8,128)} %collective-permute-done.4.x_ref, bf16[1024,1024]{1,0:T(8,128)(2,1)S(1)} %copy-done.12, bf16[1024,1024]{1,0:T(8,128)(2,1)S(1)} %copy-done.14, bf16[1024,1024]{1,0:T(8,128)(2,1)S(1)} %copy-done.17, bf16[1024,1024]{1,0:T(8,128)(2,1)S(1)} %copy-done.20, ...), custom_call_target="tpu_custom_call" | custom-call | flops 6442450944 | bytes 16777216 | tf_op jit(solution)/shard_map/inflow/pallas_call | solution.py:249
  221.7 6.2 %collective-permute-start.14 = (f32[4,32,256]{2,1,0:T(8,128)S(1)}, f32[4,32,256]{2,1,0:T(8,128)S(1)}, u32[]{:S(2)}, u32[]{:S(2)}) collective-permute-start(f32[4,32,256]{2,1,0:T(8,128)S(1)} %bitcast.96), channel_id=1, source_target_pairs={{0,1},{1,2},{2,3},{3,4},{4,5},{5,6},{6,7},{8,9},{9,10},{10,11},{11... | collective-permute-start | bytes 393224 | tf_op jit(solution)/shard_map/ppermute | solution.py:267
  232.8 5.7 %collective-permute-start.13 = (f32[4,32,256]{2,1,0:T(8,128)S(1)}, f32[4,32,256]{2,1,0:T(8,128)S(1)}, u32[]{:S(2)}, u32[]{:S(2)}) collective-permute-start(f32[4,32,256]{2,1,0:T(8,128)S(1)} %get-tuple-element.26), channel_id=1, source_target_pairs={{8,0},{16,8},{24,16},{32,24},{40,32},{48,40},{56,48},{9,1},{17,9},... | collective-permute-start | bytes 393224 | tf_op jit(solution)/shard_map/ppermute | solution.py:267
  240.2 12.9 %step_own.1 = f32[4,32,32,256]{3,2,1,0:T(8,128)} custom-call(s32[128]{0:T(128)S(1)} %pad_add_fusion.refs_0_, f32[32]{0:T(128)S(1)} %multiply_divide_fusion.1.refs_1_, f32[4]{0:T(128)S(1)} %fusion.4.refs_2_, f32[4,32,32,256]{3,2,1,0:T(8,128)} %bitcast.89, f32[4,32,256]{2,1,0:T(8,128)S(1)} %collective-permute-done.12.refs_4_, ...), custom_call_target="tpu_custom_call" | custom-call | flops 4026531840 | bytes 20971520 | tf_op jit(solution)/shard_map/step_own/pallas_call | solution.py:196
  259.5 16.8 %inflow.6.acc_ref = f32[4,1024,256]{2,1,0:T(8,128)} custom-call(f32[64,4,8,256]{3,2,1,0:T(8,128)S(1)} %all-to-all-done.2.x_ref, bf16[1024,1024]{1,0:T(8,128)(2,1)S(1)} %copy-done.13, bf16[1024,1024]{1,0:T(8,128)(2,1)S(1)} %copy-done.15, bf16[1024,1024]{1,0:T(8,128)(2,1)S(1)} %copy-done.18, bf16[1024,1024]{1,0:T(8,128)(2,1)S(1)} %copy-done.21, ...), custom_call_target="tpu_custom_call" | custom-call | flops 6442450944 | bytes 16777216 | tf_op jit(solution)/shard_map/inflow/pallas_call | solution.py:249
  276.3 17.6 %inflow.7 = f32[4,1024,256]{2,1,0:T(8,128)} custom-call(f32[64,4,8,256]{3,2,1,0:T(8,128)} %collective-permute-done.10.x_ref, bf16[1024,1024]{1,0:T(8,128)(2,1)S(1)} %copy-done.13, bf16[1024,1024]{1,0:T(8,128)(2,1)S(1)} %copy-done.15, bf16[1024,1024]{1,0:T(8,128)(2,1)S(1)} %copy-done.18, bf16[1024,1024]{1,0:T(8,128)(2,1)S(1)} %copy-done.21, ...), custom_call_target="tpu_custom_call" | custom-call | flops 6442450944 | bytes 16777216 | tf_op jit(solution)/shard_map/inflow/pallas_call | solution.py:249
  (109 shorter events, 48.3 us)
Async XLA Ops:
  0.6 120.6 %copy-start = (f32[1,1,128,4,8,8]{2,5,4,3,1,0:T(8,128)S(1)}, f32[1,1,128,4,8,8]{2,5,4,3,1,0:T(8,128)}, u32[]{:S(2)}) copy-start(f32[1,1,128,4,8,8]{2,5,4,3,1,0:T(8,128)} %param.23) | copy-start | bytes 393220
  0.6 19.6 %copy-start.22 = (f32[1,3,256,256]{3,2,1,0:T(8,128)S(1)}, f32[1,3,256,256]{3,2,1,0:T(8,128)}, u32[]{:S(2)}) copy-start(f32[1,3,256,256]{3,2,1,0:T(8,128)} %param.18) | copy-start | bytes 2359300
  0.7 20.6 %copy-start.23 = (s32[64,64,2]{1,2,0:T(2,128)S(1)}, s32[64,64,2]{1,2,0:T(2,128)}, u32[]{:S(2)}) copy-start(s32[64,64,2]{1,2,0:T(2,128)} %param.21) | copy-start | bytes 98308
  2.5 32.2 %collective-permute-start.2 = (f32[4,32,256]{2,1,0:T(8,128)S(1)}, f32[4,32,256]{2,1,0:T(8,128)S(1)}, u32[]{:S(2)}, u32[]{:S(2)}) collective-permute-start(f32[4,32,256]{2,1,0:T(8,128)S(1)} %bitcast.95), channel_id=1, source_target_pairs={{0,1},{1,2},{2,3},{3,4},{4,5},{5,6},{6,7},{8,9},{9,10},{10,11},{11... | collective-permute-start | bytes 393224 | tf_op jit(solution)/shard_map/ppermute | solution.py:267
  6.8 27.9 %collective-permute-start.3 = (f32[4,32,256]{2,1,0:T(8,128)}, f32[4,32,256]{2,1,0:T(8,128)S(1)}, u32[]{:S(2)}, u32[]{:S(2)}) collective-permute-start(f32[4,32,256]{2,1,0:T(8,128)} %bitcast.68), channel_id=1, source_target_pairs={{1,0},{2,1},{3,2},{4,3},{5,4},{6,5},{7,6},{9,8},{10,9},{11,10},{12... | collective-permute-start | bytes 393224 | tf_op jit(solution)/shard_map/ppermute | solution.py:267
  10.5 24.3 %collective-permute-start = (f32[4,32,256]{2,1,0:T(8,128)}, f32[4,32,256]{2,1,0:T(8,128)S(1)}, u32[]{:S(2)}, u32[]{:S(2)}) collective-permute-start(f32[4,32,256]{2,1,0:T(8,128)} %get-tuple-element.35), channel_id=1, source_target_pairs={{0,8},{8,16},{16,24},{24,32},{32,40},{40,48},{48,56},{1,9},{9,17},... | collective-permute-start | bytes 393224 | tf_op jit(solution)/shard_map/ppermute | solution.py:267
  14.0 20.7 %collective-permute-start.1 = (f32[4,32,256]{2,1,0:T(8,128)}, f32[4,32,256]{2,1,0:T(8,128)S(1)}, u32[]{:S(2)}, u32[]{:S(2)}) collective-permute-start(f32[4,32,256]{2,1,0:T(8,128)} %get-tuple-element.34), channel_id=1, source_target_pairs={{8,0},{16,8},{24,16},{32,24},{40,32},{48,40},{56,48},{9,1},{17,9},... | collective-permute-start | bytes 393224 | tf_op jit(solution)/shard_map/ppermute | solution.py:267
  27.8 6.9 %copy-start.25 = (f32[1,32,32]{2,1,0:T(8,128)S(1)}, f32[1,32,32]{2,1,0:T(8,128)}, u32[]{:S(2)}) copy-start(f32[1,32,32]{2,1,0:T(8,128)} %param.15) | copy-start | bytes 12292
  27.8 7.4 %copy-start.9 = (f32[1,32,32,256]{3,2,1,0:T(8,128)S(1)}, f32[1,32,32,256]{3,2,1,0:T(8,128)}, u32[]{:S(2)}) copy-start(f32[1,32,32,256]{3,2,1,0:T(8,128)} %param.14) | copy-start | bytes 3145732
  35.2 57.7 %copy-start.2 = (f32[3,32,32,128]{3,2,1,0:T(8,128)}, f32[3,32,32,128]{3,2,1,0:T(8,128)S(1)}, u32[]{:S(2)}) copy-start(f32[3,32,32,128]{3,2,1,0:T(8,128)S(1)} %broadcast_in_dim.7.refs_10_) | copy-start | bytes 4718596
  53.6 55.5 %collective-permute-start.9 = (f32[64,4,8,256]{3,2,1,0:T(8,128)}, f32[64,4,8,256]{3,2,1,0:T(8,128)}, u32[]{:S(2)}, u32[]{:S(2)}) collective-permute-start(f32[64,4,8,256]{3,2,1,0:T(8,128)} %get-tuple-element.22), channel_id=1, source_target_pairs={{0,96},{1,97},{2,98},{3,99},{4,100},{5,101},{6,102},{7,103},{8,104... | collective-permute-start | bytes 6291464 | tf_op jit(solution)/shard_map/ppermute | solution.py:279
  54.9 57.7 %all-to-all-start = ((f32[64,4,8,256]{3,2,1,0:T(8,128)}), f32[64,4,8,256]{3,2,1,0:T(8,128)}, u32[]{:S(2)}, u32[]{:S(2)}) async-start(f32[64,4,8,256]{3,2,1,0:T(8,128)} %get-tuple-element.15), calls=%async_computation | async-start | bytes 4194304 | tf_op jit(solution)/shard_map/all_to_all | solution.py:283
  63.3 29.6 %copy-start.5 = (bf16[2560,256]{1,0:T(8,128)(2,1)S(1)}, bf16[2560,256]{1,0:T(8,128)(2,1)}, u32[]{:S(2)}) copy-start(bf16[2560,256]{1,0:T(8,128)(2,1)} %get-tuple-element.13) | copy-start | bytes 3932164
  63.3 29.6 %copy-start.7 = (bf16[2560,256]{1,0:T(8,128)(2,1)S(1)}, bf16[2560,256]{1,0:T(8,128)(2,1)}, u32[]{:S(2)}) copy-start(bf16[2560,256]{1,0:T(8,128)(2,1)} %get-tuple-element.14) | copy-start | bytes 3932164
  63.3 29.6 %copy-start.10 = (f32[1,32,32,256]{3,2,1,0:T(8,128)S(1)}, f32[1,32,32,256]{3,2,1,0:T(8,128)}, u32[]{:S(2)}) copy-start(f32[1,32,32,256]{3,2,1,0:T(8,128)} %param.14) | copy-start | bytes 3145732
  68.1 19.2 %collective-permute-start.7 = (f32[4,32,256]{2,1,0:T(8,128)S(1)}, f32[4,32,256]{2,1,0:T(8,128)S(1)}, u32[]{:S(2)}, u32[]{:S(2)}) collective-permute-start(f32[4,32,256]{2,1,0:T(8,128)S(1)} %get-tuple-element.29), channel_id=1, source_target_pairs={{0,1},{1,2},{2,3},{3,4},{4,5},{5,6},{6,7},{8,9},{9,10},{10,11},{11... | collective-permute-start | bytes 393224 | tf_op jit(solution)/shard_map/ppermute | solution.py:267
  71.5 17.9 %collective-permute-start.8 = (f32[4,32,256]{2,1,0:T(8,128)S(1)}, f32[4,32,256]{2,1,0:T(8,128)S(1)}, u32[]{:S(2)}, u32[]{:S(2)}) collective-permute-start(f32[4,32,256]{2,1,0:T(8,128)S(1)} %get-tuple-element.28), channel_id=1, source_target_pairs={{1,0},{2,1},{3,2},{4,3},{5,4},{6,5},{7,6},{9,8},{10,9},{11,10},{12... | collective-permute-start | bytes 393224 | tf_op jit(solution)/shard_map/ppermute | solution.py:267
  74.4 18.4 %collective-permute-start.5 = (f32[4,32,256]{2,1,0:T(8,128)S(1)}, f32[4,32,256]{2,1,0:T(8,128)S(1)}, u32[]{:S(2)}, u32[]{:S(2)}) collective-permute-start(f32[4,32,256]{2,1,0:T(8,128)S(1)} %get-tuple-element.31), channel_id=1, source_target_pairs={{0,8},{8,16},{16,24},{24,32},{32,40},{40,48},{48,56},{1,9},{9,17},... | collective-permute-start | bytes 393224 | tf_op jit(solution)/shard_map/ppermute | solution.py:267
  77.6 15.3 %collective-permute-start.6 = (f32[4,32,256]{2,1,0:T(8,128)S(1)}, f32[4,32,256]{2,1,0:T(8,128)S(1)}, u32[]{:S(2)}, u32[]{:S(2)}) collective-permute-start(f32[4,32,256]{2,1,0:T(8,128)S(1)} %get-tuple-element.30), channel_id=1, source_target_pairs={{8,0},{16,8},{24,16},{32,24},{40,32},{48,40},{56,48},{9,1},{17,9},... | collective-permute-start | bytes 393224 | tf_op jit(solution)/shard_map/ppermute | solution.py:267
  107.8 49.6 %collective-permute-start.11 = (f32[64,4,8,256]{3,2,1,0:T(8,128)}, f32[64,4,8,256]{3,2,1,0:T(8,128)}, u32[]{:S(2)}, u32[]{:S(2)}) collective-permute-start(f32[64,4,8,256]{3,2,1,0:T(8,128)} %get-tuple-element.23), channel_id=1, source_target_pairs={{0,96},{1,97},{2,98},{3,99},{4,100},{5,101},{6,102},{7,103},{8,104... | collective-permute-start | bytes 6291464 | tf_op jit(solution)/shard_map/ppermute | solution.py:279
  112.6 44.8 %all-to-all-start.1 = ((f32[64,4,8,256]{3,2,1,0:T(8,128)}), f32[64,4,8,256]{3,2,1,0:T(8,128)}, u32[]{:S(2)}, u32[]{:S(2)}) async-start(f32[64,4,8,256]{3,2,1,0:T(8,128)} %broadcast_select_fusion), calls=%async_computation.1 | async-start | bytes 4194304 | tf_op jit(solution)/shard_map/all_to_all | solution.py:283
  119.7 82.6 %collective-permute-start.4 = (f32[64,4,8,256]{3,2,1,0:T(8,128)}, f32[64,4,8,256]{3,2,1,0:T(8,128)}, u32[]{:S(2)}, u32[]{:S(2)}) collective-permute-start(f32[64,4,8,256]{3,2,1,0:T(8,128)} %all-to-all-done), channel_id=1, source_target_pairs={{0,96},{1,97},{2,98},{3,99},{4,100},{5,101},{6,102},{7,103},{8,104... | collective-permute-start | bytes 6291464 | tf_op jit(solution)/shard_map/ppermute | solution.py:279
  157.4 95.8 %all-to-all-start.2 = ((f32[64,4,8,256]{3,2,1,0:T(8,128)}), f32[64,4,8,256]{3,2,1,0:T(8,128)S(1)}, u32[]{:S(2)}, u32[]{:S(2)}) async-start(f32[64,4,8,256]{3,2,1,0:T(8,128)} %collective-permute-done.11), calls=%async_computation.2 | async-start | bytes 4194304 | tf_op jit(solution)/shard_map/all_to_all | solution.py:283
  167.6 108.7 %collective-permute-start.10 = (f32[64,4,8,256]{3,2,1,0:T(8,128)}, f32[64,4,8,256]{3,2,1,0:T(8,128)}, u32[]{:S(2)}, u32[]{:S(2)}) collective-permute-start(f32[64,4,8,256]{3,2,1,0:T(8,128)} %all-to-all-done.1.x_ref), channel_id=1, source_target_pairs={{0,96},{1,97},{2,98},{3,99},{4,100},{5,101},{6,102},{7,103},{8,104... | collective-permute-start | bytes 6291464 | tf_op jit(solution)/shard_map/ppermute | solution.py:279
  192.8 47.4 %copy-start.8 = (bf16[2560,256]{1,0:T(8,128)(2,1)S(1)}, bf16[2560,256]{1,0:T(8,128)(2,1)}, u32[]{:S(2)}) copy-start(bf16[2560,256]{1,0:T(8,128)(2,1)} %get-tuple-element.14) | copy-start | bytes 3932164
  192.8 47.4 %copy-start.11 = (f32[1,32,32,256]{3,2,1,0:T(8,128)S(1)}, f32[1,32,32,256]{3,2,1,0:T(8,128)}, u32[]{:S(2)}) copy-start(f32[1,32,32,256]{3,2,1,0:T(8,128)} %param.14) | copy-start | bytes 3145732
  219.8 20.4 %copy-start.3 = (f32[3,32,32,128]{3,2,1,0:T(8,128)S(1)}, f32[3,32,32,128]{3,2,1,0:T(8,128)}, u32[]{:S(2)}) copy-start(f32[3,32,32,128]{3,2,1,0:T(8,128)} %copy-done.2) | copy-start | bytes 4718596
  221.7 16.8 %collective-permute-start.14 = (f32[4,32,256]{2,1,0:T(8,128)S(1)}, f32[4,32,256]{2,1,0:T(8,128)S(1)}, u32[]{:S(2)}, u32[]{:S(2)}) collective-permute-start(f32[4,32,256]{2,1,0:T(8,128)S(1)} %bitcast.96), channel_id=1, source_target_pairs={{0,1},{1,2},{2,3},{3,4},{4,5},{5,6},{6,7},{8,9},{9,10},{10,11},{11... | collective-permute-start | bytes 393224 | tf_op jit(solution)/shard_map/ppermute | solution.py:267
  227.9 10.6 %collective-permute-start.15 = (f32[4,32,256]{2,1,0:T(8,128)S(1)}, f32[4,32,256]{2,1,0:T(8,128)S(1)}, u32[]{:S(2)}, u32[]{:S(2)}) collective-permute-start(f32[4,32,256]{2,1,0:T(8,128)S(1)} %bitcast.97), channel_id=1, source_target_pairs={{1,0},{2,1},{3,2},{4,3},{5,4},{6,5},{7,6},{9,8},{10,9},{11,10},{12... | collective-permute-start | bytes 393224 | tf_op jit(solution)/shard_map/ppermute | solution.py:267
  230.9 8.3 %collective-permute-start.12 = (f32[4,32,256]{2,1,0:T(8,128)S(1)}, f32[4,32,256]{2,1,0:T(8,128)S(1)}, u32[]{:S(2)}, u32[]{:S(2)}) collective-permute-start(f32[4,32,256]{2,1,0:T(8,128)S(1)} %get-tuple-element.27), channel_id=1, source_target_pairs={{0,8},{8,16},{16,24},{24,32},{32,40},{40,48},{48,56},{1,9},{9,17},... | collective-permute-start | bytes 393224 | tf_op jit(solution)/shard_map/ppermute | solution.py:267
  232.8 7.4 %collective-permute-start.13 = (f32[4,32,256]{2,1,0:T(8,128)S(1)}, f32[4,32,256]{2,1,0:T(8,128)S(1)}, u32[]{:S(2)}, u32[]{:S(2)}) collective-permute-start(f32[4,32,256]{2,1,0:T(8,128)S(1)} %get-tuple-element.26), channel_id=1, source_target_pairs={{8,0},{16,8},{24,16},{32,24},{40,32},{48,40},{56,48},{9,1},{17,9},... | collective-permute-start | bytes 393224 | tf_op jit(solution)/shard_map/ppermute | solution.py:267
  276.3 17.6 %copy-start.1 = (f32[1,1,128,4,8,8]{2,5,4,3,1,0:T(8,128)S(1)}, f32[1,1,128,4,8,8]{2,5,4,3,1,0:T(8,128)}, u32[]{:S(2)}) copy-start(f32[1,1,128,4,8,8]{2,5,4,3,1,0:T(8,128)} %param.23) | copy-start | bytes 393220
  (14 other events, 25.7 us)

commit v2 on v1

v2 whole, which is shorter than its diff:
```python
import functools

import jax
import jax.numpy as jnp
from jax import lax
from jax.experimental import pallas as pl
from jax.experimental.pallas import tpu as pltpu
from jax.sharding import PartitionSpec as P

JTOT = 23
HEL = 4
NA = 256
CR = 32
CS = 32
PTS = CR * CS
BLK = 8
NBLK = PTS // BLK
SRCS = 64
MSLOT = 4
TI = 8
ROWS = TI * CS
MIB = 1 << 20

kinetic = 0.08
rotor_scale = 0.1
centrifugal = 0.0005
coriolis_scale = 0.005
F32 = jnp.float32
BF16 = jnp.bfloat16
ALL = ("sec", "rr", "sr")


def dot(a, b):
    return jnp.dot(a, b, preferred_element_type=F32)


def split(x):
    high = x.astype(BF16)
    return high, (x - high.astype(F32)).astype(BF16)


def whole(shape, space=pltpu.VMEM):
    return pl.BlockSpec(shape, lambda *_: (0,) * len(shape), memory_space=space)


def smem():
    return pl.BlockSpec(memory_space=pltpu.SMEM)


def frame_terms(frame_map):
    turned = frame_map.transpose(2, 0, 1, 3).reshape(HEL, HEL * NA, NA)
    high = lax.reduce_precision(turned, 8, 7)
    return high.astype(BF16), (turned - high).astype(BF16)


def blend_kernel(pick_ref, tile_ref, high_ref, low_ref, full):
    full[...] = jnp.zeros_like(full)
    lane_block = lax.broadcasted_iota(jnp.int32, (BLK, 128), 1) // BLK

    def place(b, carry):
        row = pl.multiple_of(b * BLK, BLK)
        for m in range(MSLOT):
            pick = pick_ref[m * NBLK + b]
            source, slot = pick // 2, pick % 2
            column = jnp.where(slot == 0, source, SRCS + (source ^ (SRCS // 2)))
            lane = pl.multiple_of((column // 16) * 128, 128)
            piece = jnp.where(lane_block == column % 16, tile_ref[b, m], 0.0)
            full[pl.ds(row, BLK), pl.ds(lane, 128)] += piece
        return carry

    lax.fori_loop(0, NBLK, place, 0)

    def store(r, carry):
        row = pl.multiple_of(r * 64, 64)
        high, low = split(full[pl.ds(row, 64), :])
        high_ref[pl.ds(row, 64), :] = high
        low_ref[pl.ds(row, 64), :] = low
        return carry

    lax.fori_loop(0, PTS // 64, store, 0)


def blend_call(picks, tiles):
    return pl.pallas_call(
        blend_kernel,
        in_specs=[smem(), pl.BlockSpec(memory_space=pltpu.VMEM)],
        out_specs=[pl.BlockSpec(memory_space=pltpu.VMEM)] * 2,
        out_shape=[jax.ShapeDtypeStruct((PTS, PTS), BF16)] * 2,
        scratch_shapes=[pltpu.VMEM((PTS, PTS), F32)],
        compiler_params=pltpu.CompilerParams(vmem_limit_bytes=24 * MIB),
        cost_estimate=pl.CostEstimate(flops=8 * MIB, transcendentals=0, bytes_accessed=6 * MIB),
        name="blend_matrix",
    )(picks, tiles)


ABOVE = (4, 5, 7)
BELOW = (6, 8, 9)


def step_kernel(first_step, want_own, want_pack, *refs):
    refs = list(refs)
    ids = refs.pop(0) if want_pack else None
    start_ref, now, up, down, left, right, prev, pot, damping, switch = refs[:10]
    refs = refs[10:]
    if first_step:
        angular, coriolis = refs.pop(0), refs.pop(0)
    else:
        w_ref = refs.pop(0)
    own_ref = refs.pop(0) if want_own else None
    if want_pack:
        pack_one, pack_zero = refs.pop(0), refs.pop(0)
    if first_step:
        top_ref, bottom_ref, left_ref, right_ref, w_ref = refs[:5]
        refs = refs[5:]
    rot, mix = refs.pop(0), refs.pop(0)
    absorbed = refs.pop(0) if want_pack else None
    chunk = pl.program_id(0)
    first = chunk * TI
    lowest = start_ref[0]
    total_j = float(JTOT * (JTOT + 1))

    if first_step:

        @pl.when(chunk == 0)
        def _():
            def put(n, w):
                high, low = split(w)
                w_ref[n, 0:NA] = high
                w_ref[n, NA : 2 * NA] = high
                w_ref[n, 2 * NA : 3 * NA] = low

            for k in range(HEL):
                put(k, angular[k].T)
            for k in range(HEL - 1):
                helicity = (lowest + k).astype(F32)
                ladder = coriolis_scale * jnp.sqrt(jnp.full((NA, NA), total_j - helicity * (helicity + 1.0), F32))
                scaled = ladder * coriolis[k]
                put(ABOVE[k], scaled.T)
                put(BELOW[k], scaled)

    parts = []
    for k in range(HEL):
        high, low = split(now[k, pl.ds(first, TI)].reshape(ROWS, NA))
        parts.append(jnp.concatenate([high, low, high], axis=1))
    for k in range(HEL):
        rot[k] = dot(parts[k], w_ref[k])
    mix[0] = dot(parts[1], w_ref[ABOVE[0]])
    for k in (1, 2):
        both = jnp.concatenate([parts[k + 1], parts[k - 1]], axis=1)
        mix[k] = dot(both, w_ref[ABOVE[k] : ABOVE[k] + 2].reshape(6 * NA, NA))
    mix[3] = dot(parts[2], w_ref[BELOW[2]])

    bond = lax.broadcasted_iota(jnp.int32, (CS, NA), 0)
    diagonal = lax.broadcasted_iota(jnp.int32, (CS, CS), 0) == lax.broadcasted_iota(jnp.int32, (CS, CS), 1)
    live = jnp.where(lax.axis_index("sec") == 0, 1.0, 0.0)

    def factor(position, cells):
        base = 1.0 + 3.0 * position.astype(F32) / float(cells)
        return 1.0 / (base * base)

    bond_cells = lax.axis_size("sr") * CS
    bond_factor = factor(lax.axis_index("sr") * CS + bond, bond_cells)
    radial_cells = lax.axis_size("rr") * CR
    radial_start = lax.axis_index("rr") * CR + first
    helicities = [(lowest + k).astype(F32) for k in range(HEL)]
    centre = [centrifugal * (total_j - 2.0 * h * h) for h in helicities]

    def column(ref, i):
        line = jnp.broadcast_to(ref[pl.ds(i, 1), :], (CS, CS))
        return jnp.sum(jnp.where(diagonal, line, 0.0), axis=1, keepdims=True)

    def row(t, carry):
        i = first + t
        u = factor(jnp.full((CS, NA), radial_start + t, jnp.int32), radial_cells)
        start = pl.multiple_of(t * CS, CS)
        damp = jnp.broadcast_to(column(damping, i), (CS, NA))
        share = jnp.broadcast_to(column(switch, i) * live, (CS, NA))
        spin = rotor_scale * (u + bond_factor)
        well = pot[t] + 4.0 * kinetic
        for k in range(HEL):
            v = now[k, i]
            before = jnp.where(i == 0, up[k], now[k, jnp.maximum(i - 1, 0)])
            after = jnp.where(i == CR - 1, down[k], now[k, jnp.minimum(i + 1, CR - 1)])
            lower = jnp.where(bond == 0, left[k, pl.ds(i, 1), :], pltpu.roll(v, 1, 0))
            upper = jnp.where(bond == CS - 1, right[k, pl.ds(i, 1), :], pltpu.roll(v, CS - 1, 0))
            applied = (
                (well + u * centre[k]) * v
                - kinetic * ((before + after) + (lower + upper))
                + spin * rot[k, pl.ds(start, CS), :]
                + u * mix[k, pl.ds(start, CS), :]
            )
            renewed = damp * (2.0 * applied - damp * prev[k, t])
            taken = share * renewed
            if want_own:
                own_ref[k, t] = renewed - taken
            if want_pack:
                absorbed[k, i] = taken
        return carry

    lax.fori_loop(0, TI, row, 0)

    if first_step:
        for k in range(HEL):
            left_ref[k, pl.ds(pl.multiple_of(first, TI), TI), :] = own_ref[k, :, 0, :]
            right_ref[k, pl.ds(pl.multiple_of(first, TI), TI), :] = own_ref[k, :, CS - 1, :]

        @pl.when(chunk == 0)
        def _():
            top_ref[...] = own_ref[:, 0]

        @pl.when(chunk == CR // TI - 1)
        def _():
            bottom_ref[...] = own_ref[:, TI - 1]

    if want_pack:

        @pl.when(chunk == CR // TI - 1)
        def _():
            def move(q, carry):
                for slot, target in ((q ^ (SRCS // 2), pack_zero), (SRCS + (q if first_step else q ^ (SRCS // 2)), pack_one)):
                    e = jnp.maximum(ids[slot], 0)
                    i = e // (CS // BLK)
                    j = pl.multiple_of((e % (CS // BLK)) * BLK, BLK)
                    for k in range(HEL):
                        target[q, k] = absorbed[k, i, pl.ds(j, BLK), :]
                return carry

            lax.fori_loop(0, SRCS, move, 0)


def step_call(first_step, want_own, want_pack, ids, helicity_start, now, halo, prev, pot, damping, switch, *weights):
    field = (HEL, CR, CS, NA)
    edge = (HEL, CR, NA)
    stack = (10, 3 * NA, NA)
    rows = pl.BlockSpec((HEL, TI, CS, NA), lambda c: (0, c, 0, 0))
    out_specs, out_shape, scratch = [], [], []
    if want_own:
        out_specs.append(rows)
        out_shape.append(jax.ShapeDtypeStruct(field, F32))
    if want_pack:
        packed = (SRCS, HEL, BLK, NA)
        out_specs += [whole(packed)] * 2
        out_shape += [jax.ShapeDtypeStruct(packed, F32)] * 2
    if first_step:
        out_specs += [whole(edge)] * 4 + [whole(stack)]
        out_shape += [jax.ShapeDtypeStruct(edge, F32)] * 4 + [jax.ShapeDtypeStruct(stack, BF16)]
    scratch += [pltpu.VMEM((HEL, ROWS, NA), F32)] * 2
    if want_pack:
        scratch.append(pltpu.VMEM(field, F32))
    weight_specs = [whole((HEL, NA, NA)), whole((HEL - 1, NA, NA))] if first_step else [whole(stack)]
    return pl.pallas_call(
        functools.partial(step_kernel, first_step, want_own, want_pack),
        grid=(CR // TI,),
        in_specs=([smem()] if want_pack else [])
        + [
            smem(),
            whole(field),
            whole(edge),
            whole(edge),
            whole(edge),
            whole(edge),
            rows,
            pl.BlockSpec((TI, CS, NA), lambda c: (c, 0, 0)),
            whole((CR, CS)),
            whole((CR, CS)),
        ]
        + weight_specs,
        out_specs=out_specs,
        out_shape=out_shape,
        scratch_shapes=scratch,
        compiler_params=pltpu.CompilerParams(vmem_limit_bytes=56 * MIB),
        cost_estimate=pl.CostEstimate(flops=1000, transcendentals=0, bytes_accessed=1000),
        name="step_first" if first_step else "step_own" if want_own else "step_pack",
    )(*((ids,) if want_pack else ()), helicity_start, now, *halo, prev, pot, damping, switch, *weights)


def inflow_kernel(want_edges, swap, x_ref, f_high, f_low, b_high, b_low, acc_ref, *refs):
    half = SRCS * BLK
    out_ref = refs[0]
    terms = refs[-1]
    product_section = lax.axis_index("sec") == 1

    @pl.when(jnp.logical_and(product_section, pl.program_id(0) == 0))
    def _():
        for k in range(HEL):
            lanes = slice(k * NA, (k + 1) * NA)
            for part in range(2):
                source = (1 - part if swap else part) * (SRCS // 2)
                row = part * half // 2
                high, low = split(x_ref[source : source + SRCS // 2, k].reshape(half // 2, NA))
                terms[row : row + half // 2, lanes] = high
                terms[half + row : half + row + half // 2, lanes] = low

    @pl.when(product_section)
    def _():
        wide = dot(terms[...], f_high[0])
        high, low = split(wide[:half] + wide[half:] + dot(terms[0:half], f_low[0]))
        for r in range(2):
            rows = slice(r * PTS // 2, (r + 1) * PTS // 2)
            gain = dot(b_high[rows], high) + dot(b_low[rows], high) + dot(b_high[rows], low)
            lines = slice(r * CR // 2, (r + 1) * CR // 2)
            out_ref[0, lines] = acc_ref[0, lines] + gain.reshape(CR // 2, CS, NA)

    @pl.when(jnp.logical_not(product_section))
    def _():
        out_ref[...] = acc_ref[...]

    if want_edges:
        top_ref, bottom_ref, left_ref, right_ref = refs[1:5]
        top_ref[0] = out_ref[0, 0]
        bottom_ref[0] = out_ref[0, CR - 1]
        left_ref[0] = out_ref[0, :, 0, :]
        right_ref[0] = out_ref[0, :, CS - 1, :]


def inflow_call(part, want_edges, swap, x, frame, blend, acc, flops=1000):
    half = SRCS * BLK
    column = pl.BlockSpec((1, HEL * NA, NA), lambda n: (n, 0, 0))
    weights = pl.BlockSpec((PTS, half), lambda n: (0, part))
    field = pl.BlockSpec((1, CR, CS, NA), lambda n: (n, 0, 0, 0))
    edge = pl.BlockSpec((1, CR, NA), lambda n: (n, 0, 0))
    count = 4 if want_edges else 0
    return pl.pallas_call(
        functools.partial(inflow_kernel, want_edges, swap),
        grid=(HEL,),
        in_specs=[whole((SRCS, HEL, BLK, NA)), column, column, weights, weights, field],
        out_specs=[field] + [edge] * count,
        out_shape=[jax.ShapeDtypeStruct((HEL, CR, CS, NA), F32)] + [jax.ShapeDtypeStruct((HEL, CR, NA), F32)] * count,
        scratch_shapes=[pltpu.VMEM((2 * half, HEL * NA), BF16)],
        compiler_params=pltpu.CompilerParams(vmem_limit_bytes=56 * MIB),
        cost_estimate=pl.CostEstimate(flops=flops, transcendentals=0, bytes_accessed=1000),
        name="inflow_edges" if want_edges else "inflow",
    )(x, *frame, *blend, acc)


def exchange(top, bottom, left, right):
    rows, columns = lax.axis_size("rr"), lax.axis_size("sr")

    def send(piece, axis, peers, forward):
        pairs = [(i, i + 1) if forward else (i + 1, i) for i in range(peers - 1)]
        return lax.ppermute(piece, axis, pairs)

    return (
        send(bottom, "rr", rows, True),
        send(top, "rr", rows, False),
        send(right, "sr", columns, True),
        send(left, "sr", columns, False),
    )


def cross(x):
    pairs = [(s, SRCS + (s ^ (SRCS // 2))) for s in range(SRCS)]
    return lax.ppermute(x, ALL, pairs)


def spread(x):
    return lax.all_to_all(x, ("rr", "sr"), split_axis=0, concat_axis=0, tiled=True)


def per_device(
    wave_prev,
    wave_now,
    potential,
    damping,
    switch,
    angular,
    coriolis,
    helicity_start,
    frame_map,
    route_table,
    pick_slots,
    interp_weights,
):
    section = lax.axis_index("sec")
    me = lax.axis_index("rr") * lax.axis_size("sr") + lax.axis_index("sr")
    previous, current = wave_prev[0], wave_now[0]
    halo = exchange(current[:, 0], current[:, CR - 1], current[:, :, 0], current[:, :, CS - 1])
    outgoing = lax.dynamic_index_in_dim(route_table, me, axis=1, keepdims=False)
    ids = outgoing.T.reshape(2 * SRCS)

    fixed = (potential[0], damping[0], switch)

    own_1, one_1, zero_1, *rims, weights = step_call(
        True, True, True, ids, helicity_start, current, halo, previous, *fixed, angular[0], coriolis[0]
    )
    crossed_one_1 = cross(one_1)
    halo = exchange(*rims)
    zero_1, halo = lax.optimization_barrier((zero_1, halo))
    relayed_1 = spread(zero_1)
    packed = (SRCS, HEL, BLK, NA)

    def reactant(own, halo, weights, *_):
        one, zero = step_call(False, False, True, ids, helicity_start, own, halo, current, *fixed, weights)
        return one, zero, (jnp.zeros((PTS, PTS), BF16),) * 2, (jnp.zeros((HEL, HEL * NA, NA), BF16),) * 2

    def product(own, halo, weights, picks, tiles, frame_map):
        blend = blend_call(picks, jnp.tile(tiles, (1, 1, 1, 128 // BLK)))
        return jnp.zeros(packed, F32), jnp.zeros(packed, F32), tuple(blend), frame_terms(frame_map)

    picks = pick_slots[0, 0].T.reshape(MSLOT * NBLK)
    one_2, zero_2, blend, frame = lax.cond(
        section == 0, reactant, product, own_1, halo, weights, picks, interp_weights[0, 0], frame_map
    )
    crossed_zero_1 = cross(relayed_1)
    shared = spread(jnp.where(section == 0, zero_2, crossed_one_1))
    crossed_zero_2 = cross(shared)
    one_2, shared = lax.optimization_barrier((one_2, shared))
    relayed_2 = spread(one_2)

    (new_1,) = inflow_call(0, False, False, crossed_zero_1, frame, blend, own_1, 40 << 30)
    new_1, *rims = inflow_call(1, True, False, shared, frame, blend, new_1)
    relayed_2, rims = lax.optimization_barrier((relayed_2, rims))
    crossed_one_2 = cross(relayed_2)
    halo = exchange(*rims)
    (own_2,) = step_call(False, True, False, ids, helicity_start, new_1, halo, current, *fixed, weights)
    (new_2,) = inflow_call(0, False, False, crossed_zero_2, frame, blend, own_2)
    (new_2,) = inflow_call(1, False, True, crossed_one_2, frame, blend, new_2)
    return new_1[None], new_2[None]


def solution(mesh):
    placed = (
        P("sec", None, "rr", "sr", None),
        P("sec", None, "rr", "sr", None),
        P("sec", "rr", "sr", None),
        P("sec", "rr", "sr"),
        P("rr", "sr"),
        P("sec", None, None, None),
        P("sec", None, None, None),
        P("sec"),
        P(),
        P(),
        P("rr", "sr", None, None),
        P("rr", "sr", None, None, None, None),
    )
    return jax.shard_map(
        per_device,
        mesh=mesh,
        in_specs=placed,
        out_specs=(P("sec", None, "rr", "sr", None), P("sec", None, "rr", "sr", None)),
        check_vma=False,
    )
```

time: 297 us -> 267 us (0.90)
  blocking collectives: 0 us -> 35.8 us
  local copies, waits for them, and re-layouts: 45.5 us -> 15.4 us
  Pallas kernels: 130 us -> 115 us
  starting transfers between devices: 72.9 us -> 60 us
  waiting for transfers between devices: 35.8 us -> 31.9 us
    all_to_all x0 -> x1, blocking collectives: none -> 35.8 us  [spread(): lax.all_to_all(x, ('rr', 'sr'), split_axis=0, concat_axis=0, tiled=True)]
    unnamed x61 -> x38, local copies, waits for them, and re-layouts: 24.7 us -> 3.38 us
    pallas_call x10 -> x7, Pallas kernels: 130 us -> 115 us  [the longest x4 72.1 us: inflow_call(): pl.pallas_call(functools.partial(inflow_kernel, want_edges, swap), grid=(...]
    all_to_all x3 -> x2, starting transfers between devices: 25.8 us -> 13.1 us  [spread(): lax.all_to_all(x, ('rr', 'sr'), split_axis=0, concat_axis=0, tiled=True)]
    ppermute x4, waiting for transfers between devices: 23 us -> 15.4 us  [cross(): return lax.ppermute(x, ALL, pairs)]
    pallas_call x1 -> x0, local copies, waits for them, and re-layouts: 4.77 us -> none  [step_call(): pl.pallas_call(functools.partial(step_kernel, want_own, want_pack), grid=...]
    all_to_all x3 -> x2, waiting for transfers between devices: 0.01 us -> 3.55 us  [spread(): lax.all_to_all(x, ('rr', 'sr'), split_axis=0, concat_axis=0, tiled=True)]
    convert_element_type x0 -> x1, other arithmetic: none -> 3.49 us  [frame_terms(): return (high.astype(BF16), (turned - high).astype(BF16))]
  transfers between devices with their start and end apart: 19 -> 18, of which waited for: 7 -> 7; matrix products, arithmetic and copies ran while one was open for 11% -> 6% of each run, Pallas kernels for 33% -> 30%
where the time goes in v2:
time: 267 us; the launch traced here: 266 us
  Pallas kernels  115 us (43%)
  starting transfers between devices  60 us (22%)
  blocking collectives  35.8 us (13%)
  waiting for transfers between devices  31.9 us (12%)
  local copies, waits for them, and re-layouts  15.4 us (6%)
  other arithmetic  5.53 us (2%)
    pallas_call x4, Pallas kernels, inflow_call(): pl.pallas_call(functools.partial(inflow_kernel, want_edges, swap), grid=(...  72.1 us
    ppermute x12, starting transfers between devices, send(): return lax.ppermute(piece, axis, pairs)  41.5 us
    all_to_all x1, blocking collectives, spread(): lax.all_to_all(x, ('rr', 'sr'), split_axis=0, concat_axis=0, tiled=True)  35.8 us
    pallas_call x2, Pallas kernels, step_call(): pl.pallas_call(functools.partial(step_kernel, first_step, want_own, want_...  32.3 us
    ppermute x4, waiting for transfers between devices, cross(): return lax.ppermute(x, ALL, pairs)  15.4 us
    all_to_all x2, starting transfers between devices, spread(): lax.all_to_all(x, ('rr', 'sr'), split_axis=0, concat_axis=0, tiled=True)  13.1 us
    ppermute x12, waiting for transfers between devices, send(): return lax.ppermute(piece, axis, pairs)  13 us
    pallas_call x1, Pallas kernels, blend_call(): pl.pallas_call(blend_kernel, in_specs=[smem(), pl.BlockSpec(memory_space=...  11 us
  transfers between devices with their start and end apart: 18, of which 7 were waited for; matrix products, arithmetic and copies ran while one was open for 6% of the time, Pallas kernels for 30%

profile of v2, /device:TPU:27, one launch (start us, length us, event | category | flops | bytes accessed | tf_op | source)
XLA Modules:
  0.0 265.9 jit_solution(13740470593029517485)
XLA Ops:
  2.5 3.7 %collective-permute-start.2 = (f32[4,32,256]{2,1,0:T(8,128)S(1)}, f32[4,32,256]{2,1,0:T(8,128)S(1)}, u32[]{:S(2)}, u32[]{:S(2)}) collective-permute-start(f32[4,32,256]{2,1,0:T(8,128)S(1)} %bitcast.50), channel_id=1, source_target_pairs={{0,1},{1,2},{2,3},{3,4},{4,5},{5,6},{6,7},{8,9},{9,10},{10,11},{11... | collective-permute-start | bytes 393224 | tf_op jit(solution)/shard_map/ppermute | solution.py:341
  6.2 1.9 collective-permute-start.3
  9.1 5.8 %collective-permute-start.1 = (f32[4,32,256]{2,1,0:T(8,128)S(1)}, f32[4,32,256]{2,1,0:T(8,128)S(1)}, u32[]{:S(2)}, u32[]{:S(2)}) collective-permute-start(f32[4,32,256]{2,1,0:T(8,128)S(1)} %get-tuple-element.127), channel_id=1, source_target_pairs={{8,0},{16,8},{24,16},{32,24},{40,32},{48,40},{56,48},{9,1},{17,9},... | collective-permute-start | bytes 393224 | tf_op jit(solution)/shard_map/ppermute | solution.py:341
  15.0 1.9 collective-permute-start
  17.9 4.9 %collective-permute-done.refs_3_ = f32[4,32,256]{2,1,0:T(8,128)S(1)} collective-permute-done((f32[4,32,256]{2,1,0:T(8,128)S(1)}, f32[4,32,256]{2,1,0:T(8,128)S(1)}, u32[]{:S(2)}, u32[]{:S(2)}) %collective-permute-start) | collective-permute-done | bytes 131104 | tf_op jit(solution)/shard_map/ppermute | solution.py:341
  23.5 18.2 %step_first.1 = (f32[4,32,32,256]{3,2,1,0:T(8,128)}, f32[64,4,8,256]{3,2,1,0:T(8,128)}, f32[64,4,8,256]{3,2,1,0:T(8,128)}, f32[4,32,256]{2,1,0:T(8,128)}, f32[4,...) custom-call(s32[128]{0:T(128)S(1)} %reshape.18.refs_0_, ...), custom_call_target="tpu_custom_call" | custom-call | flops 1000 | bytes 1000 | tf_op jit(solution)/shard_map/step_first/pallas_call | solution.py:251
  41.7 1.9 collective-permute-start.4
  43.6 5.5 %collective-permute-start.5 = (f32[4,32,256]{2,1,0:T(8,128)}, f32[4,32,256]{2,1,0:T(8,128)S(1)}, u32[]{:S(2)}, u32[]{:S(2)}) collective-permute-start(f32[4,32,256]{2,1,0:T(8,128)} %get-tuple-element.85), channel_id=1, source_target_pairs={{8,0},{16,8},{24,16},{32,24},{40,32},{48,40},{56,48},{9,1},{17,9},... | collective-permute-start | bytes 393224 | tf_op jit(solution)/shard_map/ppermute | solution.py:341
  49.1 5.6 %collective-permute-start.6 = (f32[4,32,256]{2,1,0:T(8,128)}, f32[4,32,256]{2,1,0:T(8,128)S(1)}, u32[]{:S(2)}, u32[]{:S(2)}) collective-permute-start(f32[4,32,256]{2,1,0:T(8,128)} %get-tuple-element.86), channel_id=1, source_target_pairs={{0,1},{1,2},{2,3},{3,4},{4,5},{5,6},{6,7},{8,9},{9,10},{10,11},{11... | collective-permute-start | bytes 393224 | tf_op jit(solution)/shard_map/ppermute | solution.py:341
  54.7 1.9 collective-permute-start.7
  58.0 3.2 %collective-permute-done.7 = f32[4,32,256]{2,1,0:T(8,128)S(1)} collective-permute-done((f32[4,32,256]{2,1,0:T(8,128)}, f32[4,32,256]{2,1,0:T(8,128)S(1)}, u32[]{:S(2)}, u32[]{:S(2)}) %collective-permute-start.7) | collective-permute-done | bytes 131104 | tf_op jit(solution)/shard_map/ppermute | solution.py:341
  61.9 6.2 %all-to-all-start.1 = ((f32[64,4,8,256]{3,2,1,0:T(8,128)}), f32[64,4,8,256]{3,2,1,0:T(8,128)}, u32[]{:S(2)}, u32[]{:S(2)}) async-start(f32[64,4,8,256]{3,2,1,0:T(8,128)} %get-tuple-element.101), calls=%async_computation.1 | async-start | bytes 4194304 | tf_op jit(solution)/shard_map/all_to_all | solution.py:357
  68.2 23.5 %conditional.1 = (f32[64,4,8,256]{3,2,1,0:T(8,128)}, f32[64,4,8,256]{3,2,1,0:T(8,128)}, bf16[1024,1024]{1,0:T(8,128)(2,1)}, bf16[1024,1024]{1,0:T(8,128)(2,1)}, ...) conditional(s32[]{:T(128)} %convert_element_type.9, (f32[1,1,128,4,8,8]{2,5,4,3,1,0:T(8,128)S(1)}, ...), branch_computations={%region_0.1_spmd, %region_1.2_spmd} | conditional | flops 12582912 | bytes 33685560 | solution.py:401
  69.7 2.4 copy.26.tile_ref
  72.0 11.0 %blend_matrix.1 = (bf16[1024,1024]{1,0:T(8,128)(2,1)}, bf16[1024,1024]{1,0:T(8,128)(2,1)}) custom-call(s32[512]{0:T(512)S(1)} %bitcast.53, f32[128,4,8,128]{3,2,1,0:T(8,128)S(1)} %copy.26.tile_ref), custom_call_target="tpu_custom_call" | custom-call | flops 8388608 | bytes 6291456 | tf_op jit(solution)/shard_map/cond/branch_0_fun/blend_matrix/pallas_call | solution.py:84
  83.1 3.5 %fusion = (bf16[4,1024,256]{2,0,1:T(4,128)(2,1)S(1)}, bf16[4,1024,256]{2,0,1:T(4,128)(2,1)S(1)}) fusion(f32[4,256,4,256]{3,2,1,0:T(4,128)} %get-tuple-element.117), kind=kLoop, calls=%fused_computation.2 | loop fusion | flops 4194304 | bytes 8388608 | tf_op jit(solution)/shard_map/cond/branch_0_fun/convert_element_type | solution.py:53
  91.7 3.6 %all-to-all-done.1 = f32[64,4,8,256]{3,2,1,0:T(8,128)} async-done(((f32[64,4,8,256]{3,2,1,0:T(8,128)}), f32[64,4,8,256]{3,2,1,0:T(8,128)}, u32[]{:S(2)}, u32[]{:S(2)}) %all-to-all-start.1) | async-done | bytes 2097184 | tf_op jit(solution)/shard_map/all_to_all | solution.py:357
  96.5 10.1 %collective-permute-done.8 = f32[64,4,8,256]{3,2,1,0:T(8,128)} collective-permute-done((f32[64,4,8,256]{3,2,1,0:T(8,128)}, f32[64,4,8,256]{3,2,1,0:T(8,128)}, u32[]{:S(2)}, u32[]{:S(2)}) %collective-permute-start.8) | collective-permute-done | bytes 2097184 | tf_op jit(solution)/shard_map/ppermute | solution.py:353
  106.6 2.0 broadcast_select_fusion
  108.6 35.8 %all_to_all.15.x_ref = f32[64,4,8,256]{3,2,1,0:T(8,128)} all-to-all(f32[64,4,8,256]{3,2,1,0:T(8,128)S(1)} %broadcast_select_fusion), channel_id=1, replica_groups=mesh['sec'=2,'rr'=8,'sr'=8] {'rr','sr'}, dimensions={0} | all-to-all | bytes 4194304 | tf_op jit(solution)/shard_map/all_to_all | solution.py:357
  144.5 6.9 %all-to-all-start.2 = ((f32[64,4,8,256]{3,2,1,0:T(8,128)}), f32[64,4,8,256]{3,2,1,0:T(8,128)}, u32[]{:S(2)}, u32[]{:S(2)}) async-start(f32[64,4,8,256]{3,2,1,0:T(8,128)} %get-tuple-element.103), calls=%async_computation.2 | async-start | bytes 4194304 | tf_op jit(solution)/shard_map/all_to_all | solution.py:357
  152.9 18.0 %inflow.3.acc_ref = f32[4,32,32,256]{3,2,1,0:T(8,128)} custom-call(f32[64,4,8,256]{3,2,1,0:T(8,128)} %collective-permute-done.9.x_ref, bf16[4,1024,256]{2,1,0:T(8,128)(2,1)} %get-tuple-element.121.f_high, bf16[4,1024,256]{2,1,0:T(8,128)(2,1)S(1)} %get-tuple-element.122.f_low, bf16[1024,1024]{1,0:T(8,128)(2,1)} %get-tuple-element.99.b_high, ...), custom_call_target="tpu_custom_call" | custom-call | flops 42949672960 | bytes 1000 | tf_op jit(solution)/shard_map/inflow/pallas_call | solution.py:323
  170.8 18.2 %inflow_edges.1 = (f32[4,32,32,256]{3,2,1,0:T(8,128)}, f32[4,32,256]{2,1,0:T(8,128)}, f32[4,32,256]{2,1,0:T(8,128)}, f32[4,32,256]{2,1,0:T(8,128)}, f32[4,32,256]{2,1,0:T(8,128)}) custom-call(f32[64,4,8,256]{3,2,1,0:T(8,128)} %all_to_all.15.x_ref, bf16[4,1024,256]{2,1,0:T(8,128)(2,1)} %get-tuple-element.121.f_high, ...), custom_call_target="tpu_custom_call" | custom-call | flops 1000 | bytes 1000 | tf_op jit(solution)/shard_map/inflow_edges/pallas_call | solution.py:323
  190.4 3.1 %collective-permute-start.12 = (f32[4,32,256]{2,1,0:T(8,128)}, f32[4,32,256]{2,1,0:T(8,128)S(1)}, u32[]{:S(2)}, u32[]{:S(2)}) collective-permute-start(f32[4,32,256]{2,1,0:T(8,128)} %get-tuple-element.109), channel_id=1, source_target_pairs={{0,8},{8,16},{16,24},{24,32},{32,40},{40,48},{48,56},{1,9},{9,17},... | collective-permute-start | bytes 393224 | tf_op jit(solution)/shard_map/ppermute | solution.py:341
  193.5 4.2 %collective-permute-start.13 = (f32[4,32,256]{2,1,0:T(8,128)}, f32[4,32,256]{2,1,0:T(8,128)S(1)}, u32[]{:S(2)}, u32[]{:S(2)}) collective-permute-start(f32[4,32,256]{2,1,0:T(8,128)} %get-tuple-element.110), channel_id=1, source_target_pairs={{8,0},{16,8},{24,16},{32,24},{40,32},{48,40},{56,48},{9,1},{17,9},... | collective-permute-start | bytes 393224 | tf_op jit(solution)/shard_map/ppermute | solution.py:341
  197.8 3.9 %collective-permute-start.14 = (f32[4,32,256]{2,1,0:T(8,128)}, f32[4,32,256]{2,1,0:T(8,128)S(1)}, u32[]{:S(2)}, u32[]{:S(2)}) collective-permute-start(f32[4,32,256]{2,1,0:T(8,128)} %get-tuple-element.111), channel_id=1, source_target_pairs={{0,1},{1,2},{2,3},{3,4},{4,5},{5,6},{6,7},{8,9},{9,10},{10,11},{11... | collective-permute-start | bytes 393224 | tf_op jit(solution)/shard_map/ppermute | solution.py:341
  201.7 1.9 collective-permute-start.15
  203.9 4.6 %collective-permute-done.15.refs_5_ = f32[4,32,256]{2,1,0:T(8,128)S(1)} collective-permute-done((f32[4,32,256]{2,1,0:T(8,128)}, f32[4,32,256]{2,1,0:T(8,128)S(1)}, u32[]{:S(2)}, u32[]{:S(2)}) %collective-permute-start.15) | collective-permute-done | bytes 131104 | tf_op jit(solution)/shard_map/ppermute | solution.py:341
  209.2 14.1 %step_own.1.acc_ref = f32[4,32,32,256]{3,2,1,0:T(8,128)} custom-call(s32[1]{0:T(128)S(6)} %copy.58.refs_1_.refs_0_, f32[4,32,32,256]{3,2,1,0:T(8,128)} %get-tuple-element.102.refs_1_, f32[4,32,256]{2,1,0:T(8,128)} %copy-done.12, f32[4,32,256]{2,1,0:T(8,128)} %copy-done.13, f32[4,32,256]{2,1,0:T(8,128)} %copy-done.14, f32[4,32,256]{2,1,0:T(8,128)} %copy-done.15, ...), custom_call_target="tpu_custom_call" | custom-call | flops 1000 | bytes 1000 | tf_op jit(solution)/shard_map/step_own/pallas_call | solution.py:251
  223.2 18.0 %inflow.4.acc_ref = f32[4,32,32,256]{3,2,1,0:T(8,128)} custom-call(f32[64,4,8,256]{3,2,1,0:T(8,128)} %collective-permute-done.11.x_ref, bf16[4,1024,256]{2,1,0:T(8,128)(2,1)} %get-tuple-element.121.f_high, bf16[4,1024,256]{2,1,0:T(8,128)(2,1)S(1)} %get-tuple-element.122.f_low, bf16[1024,1024]{1,0:T(8,128)(2,1)} %get-tuple-element.99.b_high, ...), custom_call_target="tpu_custom_call" | custom-call | flops 1000 | bytes 1000 | tf_op jit(solution)/shard_map/inflow/pallas_call | solution.py:323
  241.2 5.3 %collective-permute-done.10.x_ref = f32[64,4,8,256]{3,2,1,0:T(8,128)S(1)} collective-permute-done((f32[64,4,8,256]{3,2,1,0:T(8,128)}, f32[64,4,8,256]{3,2,1,0:T(8,128)S(1)}, u32[]{:S(2)}, u32[]{:S(2)}) %collective-permute-start.10) | collective-permute-done | bytes 2097184 | tf_op jit(solution)/shard_map/ppermute | solution.py:353
  247.9 18.0 %inflow.5 = f32[4,32,32,256]{3,2,1,0:T(8,128)} custom-call(f32[64,4,8,256]{3,2,1,0:T(8,128)} %copy-done.3, bf16[4,1024,256]{2,1,0:T(8,128)(2,1)} %get-tuple-element.121.f_high, bf16[4,1024,256]{2,1,0:T(8,128)(2,1)S(1)} %get-tuple-element.122.f_low, bf16[1024,1024]{1,0:T(8,128)(2,1)} %get-tuple-element.99.b_high, ...), custom_call_target="tpu_custom_call" | custom-call | flops 1000 | bytes 1000 | tf_op jit(solution)/shard_map/inflow/pallas_call | solution.py:323
  (64 shorter events, 18.7 us)
Async XLA Ops:
  0.6 16.9 %copy-start = (s32[64,64,2]{1,2,0:T(2,128)S(1)}, s32[64,64,2]{1,2,0:T(2,128)}, u32[]{:S(2)}) copy-start(s32[64,64,2]{1,2,0:T(2,128)} %param.23) | copy-start | bytes 98308
  0.6 22.8 %copy-start.2 = (f32[1,32,32,256]{3,2,1,0:T(8,128)S(1)}, f32[1,32,32,256]{3,2,1,0:T(8,128)}, u32[]{:S(2)}) copy-start(f32[1,32,32,256]{3,2,1,0:T(8,128)} %param.16) | copy-start | bytes 3145732
  2.5 15.4 %collective-permute-start.2 = (f32[4,32,256]{2,1,0:T(8,128)S(1)}, f32[4,32,256]{2,1,0:T(8,128)S(1)}, u32[]{:S(2)}, u32[]{:S(2)}) collective-permute-start(f32[4,32,256]{2,1,0:T(8,128)S(1)} %bitcast.50), channel_id=1, source_target_pairs={{0,1},{1,2},{2,3},{3,4},{4,5},{5,6},{6,7},{8,9},{9,10},{10,11},{11... | collective-permute-start | bytes 393224 | tf_op jit(solution)/shard_map/ppermute | solution.py:341
  6.2 11.7 %collective-permute-start.3 = (f32[4,32,256]{2,1,0:T(8,128)S(1)}, f32[4,32,256]{2,1,0:T(8,128)S(1)}, u32[]{:S(2)}, u32[]{:S(2)}) collective-permute-start(f32[4,32,256]{2,1,0:T(8,128)S(1)} %bitcast.51), channel_id=1, source_target_pairs={{1,0},{2,1},{3,2},{4,3},{5,4},{6,5},{7,6},{9,8},{10,9},{11,10},{12... | collective-permute-start | bytes 393224 | tf_op jit(solution)/shard_map/ppermute | solution.py:341
  9.1 8.8 %collective-permute-start.1 = (f32[4,32,256]{2,1,0:T(8,128)S(1)}, f32[4,32,256]{2,1,0:T(8,128)S(1)}, u32[]{:S(2)}, u32[]{:S(2)}) collective-permute-start(f32[4,32,256]{2,1,0:T(8,128)S(1)} %get-tuple-element.127), channel_id=1, source_target_pairs={{8,0},{16,8},{24,16},{32,24},{40,32},{48,40},{56,48},{9,1},{17,9},... | collective-permute-start | bytes 393224 | tf_op jit(solution)/shard_map/ppermute | solution.py:341
  15.0 7.8 %collective-permute-start = (f32[4,32,256]{2,1,0:T(8,128)S(1)}, f32[4,32,256]{2,1,0:T(8,128)S(1)}, u32[]{:S(2)}, u32[]{:S(2)}) collective-permute-start(f32[4,32,256]{2,1,0:T(8,128)S(1)} %get-tuple-element.128), channel_id=1, source_target_pairs={{0,8},{8,16},{16,24},{24,32},{32,40},{40,48},{48,56},{1,9},{9,17},... | collective-permute-start | bytes 393224 | tf_op jit(solution)/shard_map/ppermute | solution.py:341
  17.9 4.9 %copy-start.8 = (f32[4,32,256]{2,1,0:T(8,128)}, f32[4,32,256]{2,1,0:T(8,128)S(1)}, u32[]{:S(2)}) copy-start(f32[4,32,256]{2,1,0:T(8,128)S(1)} %collective-permute-done.2.refs_5_) | copy-start | bytes 393220
  17.9 4.9 %copy-start.9 = (f32[4,32,256]{2,1,0:T(8,128)}, f32[4,32,256]{2,1,0:T(8,128)S(1)}, u32[]{:S(2)}) copy-start(f32[4,32,256]{2,1,0:T(8,128)S(1)} %collective-permute-done.3.refs_6_) | copy-start | bytes 393220
  17.9 4.9 %copy-start.10 = (f32[4,32,256]{2,1,0:T(8,128)}, f32[4,32,256]{2,1,0:T(8,128)S(1)}, u32[]{:S(2)}) copy-start(f32[4,32,256]{2,1,0:T(8,128)S(1)} %collective-permute-done.1.refs_4_) | copy-start | bytes 393220
  41.7 16.3 %collective-permute-start.4 = (f32[4,32,256]{2,1,0:T(8,128)}, f32[4,32,256]{2,1,0:T(8,128)S(1)}, u32[]{:S(2)}, u32[]{:S(2)}) collective-permute-start(f32[4,32,256]{2,1,0:T(8,128)} %get-tuple-element.84), channel_id=1, source_target_pairs={{0,8},{8,16},{16,24},{24,32},{32,40},{40,48},{48,56},{1,9},{9,17},... | collective-permute-start | bytes 393224 | tf_op jit(solution)/shard_map/ppermute | solution.py:341
  43.6 14.4 %collective-permute-start.5 = (f32[4,32,256]{2,1,0:T(8,128)}, f32[4,32,256]{2,1,0:T(8,128)S(1)}, u32[]{:S(2)}, u32[]{:S(2)}) collective-permute-start(f32[4,32,256]{2,1,0:T(8,128)} %get-tuple-element.85), channel_id=1, source_target_pairs={{8,0},{16,8},{24,16},{32,24},{40,32},{48,40},{56,48},{9,1},{17,9},... | collective-permute-start | bytes 393224 | tf_op jit(solution)/shard_map/ppermute | solution.py:341
  49.1 8.9 %collective-permute-start.6 = (f32[4,32,256]{2,1,0:T(8,128)}, f32[4,32,256]{2,1,0:T(8,128)S(1)}, u32[]{:S(2)}, u32[]{:S(2)}) collective-permute-start(f32[4,32,256]{2,1,0:T(8,128)} %get-tuple-element.86), channel_id=1, source_target_pairs={{0,1},{1,2},{2,3},{3,4},{4,5},{5,6},{6,7},{8,9},{9,10},{10,11},{11... | collective-permute-start | bytes 393224 | tf_op jit(solution)/shard_map/ppermute | solution.py:341
  54.7 6.5 %collective-permute-start.7 = (f32[4,32,256]{2,1,0:T(8,128)}, f32[4,32,256]{2,1,0:T(8,128)S(1)}, u32[]{:S(2)}, u32[]{:S(2)}) collective-permute-start(f32[4,32,256]{2,1,0:T(8,128)} %get-tuple-element.87), channel_id=1, source_target_pairs={{1,0},{2,1},{3,2},{4,3},{5,4},{6,5},{7,6},{9,8},{10,9},{11,10},{12... | collective-permute-start | bytes 393224 | tf_op jit(solution)/shard_map/ppermute | solution.py:341
  56.7 49.9 %collective-permute-start.8 = (f32[64,4,8,256]{3,2,1,0:T(8,128)}, f32[64,4,8,256]{3,2,1,0:T(8,128)}, u32[]{:S(2)}, u32[]{:S(2)}) collective-permute-start(f32[64,4,8,256]{3,2,1,0:T(8,128)} %get-tuple-element.95), channel_id=1, source_target_pairs={{0,96},{1,97},{2,98},{3,99},{4,100},{5,101},{6,102},{7,103},{8,104... | collective-permute-start | bytes 6291464 | tf_op jit(solution)/shard_map/ppermute | solution.py:353
  58.0 3.2 %copy-start.6 = (f32[4,32,256]{2,1,0:T(8,128)}, f32[4,32,256]{2,1,0:T(8,128)S(1)}, u32[]{:S(2)}) copy-start(f32[4,32,256]{2,1,0:T(8,128)S(1)} %collective-permute-done.6) | copy-start | bytes 393220
  61.9 6.2 %copy-start.4 = (f32[1,32,32]{2,1,0:T(8,128)S(1)}, f32[1,32,32]{2,1,0:T(8,128)}, u32[]{:S(2)}) copy-start(f32[1,32,32]{2,1,0:T(8,128)} %param.17) | copy-start | bytes 12292
  61.9 6.2 %copy-start.5 = (f32[32,32]{1,0:T(8,128)S(1)}, f32[32,32]{1,0:T(8,128)}, u32[]{:S(2)}) copy-start(f32[32,32]{1,0:T(8,128)} %refs_9_.1) | copy-start | bytes 12292
  61.9 6.2 %copy-start.16 = (f32[1,1,128,4,8,8]{2,5,4,3,1,0:T(8,128)S(1)}, f32[1,1,128,4,8,8]{2,5,4,3,1,0:T(8,128)}, u32[]{:S(2)}) copy-start(f32[1,1,128,4,8,8]{2,5,4,3,1,0:T(8,128)} %param.25) | copy-start | bytes 393220
  61.9 6.3 %copy-start.17 = (s32[1,1,128,4]{2,3,1,0:T(4,128)S(1)}, s32[1,1,128,4]{2,3,1,0:T(4,128)}, u32[]{:S(2)}) copy-start(s32[1,1,128,4]{2,3,1,0:T(4,128)} %param.24) | copy-start | bytes 6148
  61.9 33.3 %all-to-all-start.1 = ((f32[64,4,8,256]{3,2,1,0:T(8,128)}), f32[64,4,8,256]{3,2,1,0:T(8,128)}, u32[]{:S(2)}, u32[]{:S(2)}) async-start(f32[64,4,8,256]{3,2,1,0:T(8,128)} %get-tuple-element.101), calls=%async_computation.1 | async-start | bytes 4194304 | tf_op jit(solution)/shard_map/all_to_all | solution.py:357
  95.2 57.6 %collective-permute-start.9 = (f32[64,4,8,256]{3,2,1,0:T(8,128)}, f32[64,4,8,256]{3,2,1,0:T(8,128)}, u32[]{:S(2)}, u32[]{:S(2)}) collective-permute-start(f32[64,4,8,256]{3,2,1,0:T(8,128)} %all-to-all-done.1), channel_id=1, source_target_pairs={{0,96},{1,97},{2,98},{3,99},{4,100},{5,101},{6,102},{7,103},{8,104... | collective-permute-start | bytes 6291464 | tf_op jit(solution)/shard_map/ppermute | solution.py:353
  144.5 44.6 %all-to-all-start.2 = ((f32[64,4,8,256]{3,2,1,0:T(8,128)}), f32[64,4,8,256]{3,2,1,0:T(8,128)}, u32[]{:S(2)}, u32[]{:S(2)}) async-start(f32[64,4,8,256]{3,2,1,0:T(8,128)} %get-tuple-element.103), calls=%async_computation.2 | async-start | bytes 4194304 | tf_op jit(solution)/shard_map/all_to_all | solution.py:357
  151.4 71.8 %collective-permute-start.11 = (f32[64,4,8,256]{3,2,1,0:T(8,128)}, f32[64,4,8,256]{3,2,1,0:T(8,128)}, u32[]{:S(2)}, u32[]{:S(2)}) collective-permute-start(f32[64,4,8,256]{3,2,1,0:T(8,128)} %all_to_all.15.x_ref), channel_id=1, source_target_pairs={{0,96},{1,97},{2,98},{3,99},{4,100},{5,101},{6,102},{7,103},{8,104... | collective-permute-start | bytes 6291464 | tf_op jit(solution)/shard_map/ppermute | solution.py:353
  189.1 57.4 %collective-permute-start.10 = (f32[64,4,8,256]{3,2,1,0:T(8,128)}, f32[64,4,8,256]{3,2,1,0:T(8,128)S(1)}, u32[]{:S(2)}, u32[]{:S(2)}) collective-permute-start(f32[64,4,8,256]{3,2,1,0:T(8,128)} %all-to-all-done.2), channel_id=1, source_target_pairs={{0,96},{1,97},{2,98},{3,99},{4,100},{5,101},{6,102},{7,103},{8,104... | collective-permute-start | bytes 6291464 | tf_op jit(solution)/shard_map/ppermute | solution.py:353
  190.4 11.3 %collective-permute-start.12 = (f32[4,32,256]{2,1,0:T(8,128)}, f32[4,32,256]{2,1,0:T(8,128)S(1)}, u32[]{:S(2)}, u32[]{:S(2)}) collective-permute-start(f32[4,32,256]{2,1,0:T(8,128)} %get-tuple-element.109), channel_id=1, source_target_pairs={{0,8},{8,16},{16,24},{24,32},{32,40},{40,48},{48,56},{1,9},{9,17},... | collective-permute-start | bytes 393224 | tf_op jit(solution)/shard_map/ppermute | solution.py:341
  193.5 10.1 %collective-permute-start.13 = (f32[4,32,256]{2,1,0:T(8,128)}, f32[4,32,256]{2,1,0:T(8,128)S(1)}, u32[]{:S(2)}, u32[]{:S(2)}) collective-permute-start(f32[4,32,256]{2,1,0:T(8,128)} %get-tuple-element.110), channel_id=1, source_target_pairs={{8,0},{16,8},{24,16},{32,24},{40,32},{48,40},{56,48},{9,1},{17,9},... | collective-permute-start | bytes 393224 | tf_op jit(solution)/shard_map/ppermute | solution.py:341
  197.8 6.2 %collective-permute-start.14 = (f32[4,32,256]{2,1,0:T(8,128)}, f32[4,32,256]{2,1,0:T(8,128)S(1)}, u32[]{:S(2)}, u32[]{:S(2)}) collective-permute-start(f32[4,32,256]{2,1,0:T(8,128)} %get-tuple-element.111), channel_id=1, source_target_pairs={{0,1},{1,2},{2,3},{3,4},{4,5},{5,6},{6,7},{8,9},{9,10},{10,11},{11... | collective-permute-start | bytes 393224 | tf_op jit(solution)/shard_map/ppermute | solution.py:341
  201.7 6.8 %copy-start.12 = (f32[4,32,256]{2,1,0:T(8,128)}, f32[4,32,256]{2,1,0:T(8,128)S(1)}, u32[]{:S(2)}) copy-start(f32[4,32,256]{2,1,0:T(8,128)S(1)} %collective-permute-done.12.refs_2_) | copy-start | bytes 393220
  201.7 6.8 %collective-permute-start.15 = (f32[4,32,256]{2,1,0:T(8,128)}, f32[4,32,256]{2,1,0:T(8,128)S(1)}, u32[]{:S(2)}, u32[]{:S(2)}) collective-permute-start(f32[4,32,256]{2,1,0:T(8,128)} %get-tuple-element.112), channel_id=1, source_target_pairs={{1,0},{2,1},{3,2},{4,3},{5,4},{6,5},{7,6},{9,8},{10,9},{11,10},{12... | collective-permute-start | bytes 393224 | tf_op jit(solution)/shard_map/ppermute | solution.py:341
  203.6 4.9 %copy-start.13 = (f32[4,32,256]{2,1,0:T(8,128)}, f32[4,32,256]{2,1,0:T(8,128)S(1)}, u32[]{:S(2)}) copy-start(f32[4,32,256]{2,1,0:T(8,128)S(1)} %collective-permute-done.13.refs_3_) | copy-start | bytes 393220
  203.9 4.6 %copy-start.14 = (f32[4,32,256]{2,1,0:T(8,128)}, f32[4,32,256]{2,1,0:T(8,128)S(1)}, u32[]{:S(2)}) copy-start(f32[4,32,256]{2,1,0:T(8,128)S(1)} %collective-permute-done.14.refs_4_) | copy-start | bytes 393220
  247.9 18.0 %copy-start.1 = (s32[64,64,2]{1,2,0:T(2,128)S(1)}, s32[64,64,2]{1,2,0:T(2,128)}, u32[]{:S(2)}) copy-start(s32[64,64,2]{1,2,0:T(2,128)} %param.23) | copy-start | bytes 98308
  (4 other events, 3.3 us)

commit v3 on v2

--- a/solution.py
+++ b/solution.py
@@ -53,40 +53,41 @@
     return high.astype(BF16), (turned - high).astype(BF16)
 
 
-def blend_kernel(pick_ref, tile_ref, high_ref, low_ref, full):
-    full[...] = jnp.zeros_like(full)
-    lane_block = lax.broadcasted_iota(jnp.int32, (BLK, 128), 1) // BLK
-
-    def place(b, carry):
-        row = pl.multiple_of(b * BLK, BLK)
+def blend_kernel(pick_ref, tile_ref, high_ref, low_ref, *unused):
+    lane_block = lax.broadcasted_iota(jnp.int32, (BLK, PTS), 1) // BLK
+
+    def rows_of(b):
+        total = None
         for m in range(MSLOT):
             pick = pick_ref[m * NBLK + b]
             source, slot = pick // 2, pick % 2
             column = jnp.where(slot == 0, source, SRCS + (source ^ (SRCS // 2)))
-            lane = pl.multiple_of((column // 16) * 128, 128)
-            piece = jnp.where(lane_block == column % 16, tile_ref[b, m], 0.0)
-            full[pl.ds(row, BLK), pl.ds(lane, 128)] += piece
+            spread_tile = jnp.concatenate([tile_ref[b, m]] * (PTS // 128), axis=1)
+            piece = jnp.where(lane_block == column, spread_tile, 0.0)
+            total = piece if total is None else total + piece
+        return total
+
+    def pair(n, carry):
+        row = pl.multiple_of(n * 2 * BLK, 2 * BLK)
+        high, low = split(jnp.concatenate([rows_of(2 * n), rows_of(2 * n + 1)], axis=0))
+        high_ref[pl.ds(row, 2 * BLK), :] = high
+        low_ref[pl.ds(row, 2 * BLK), :] = low
         return carry
 
-    lax.fori_loop(0, NBLK, place, 0)
-
-    def store(r, carry):
-        row = pl.multiple_of(r * 64, 64)
-        high, low = split(full[pl.ds(row, 64), :])
-        high_ref[pl.ds(row, 64), :] = high
-        low_ref[pl.ds(row, 64), :] = low
-        return carry
-
-    lax.fori_loop(0, PTS // 64, store, 0)
-
-
-def blend_call(picks, tiles):
+    lax.fori_loop(0, NBLK // 2, pair, 0)
+
+
+def untouched(shapes):
+    return [pl.BlockSpec(memory_space=pl.ANY)] * len(shapes), list(shapes)
+
+
+def blend_call(picks, tiles, others):
+    specs, shapes = untouched(others)
     return pl.pallas_call(
         blend_kernel,
         in_specs=[smem(), pl.BlockSpec(memory_space=pltpu.VMEM)],
-        out_specs=[pl.BlockSpec(memory_space=pltpu.VMEM)] * 2,
-        out_shape=[jax.ShapeDtypeStruct((PTS, PTS), BF16)] * 2,
-        scratch_shapes=[pltpu.VMEM((PTS, PTS), F32)],
+        out_specs=[pl.BlockSpec(memory_space=pltpu.VMEM)] * 2 + specs,
+        out_shape=[jax.ShapeDtypeStruct((PTS, PTS), BF16)] * 2 + shapes,
         compiler_params=pltpu.CompilerParams(vmem_limit_bytes=24 * MIB),
         cost_estimate=pl.CostEstimate(flops=8 * MIB, transcendentals=0, bytes_accessed=6 * MIB),
         name="blend_matrix",
@@ -112,8 +113,8 @@
     if first_step:
         top_ref, bottom_ref, left_ref, right_ref, w_ref = refs[:5]
         refs = refs[5:]
-    rot, mix = refs.pop(0), refs.pop(0)
-    absorbed = refs.pop(0) if want_pack else None
+    rot, mix = refs[-3:-1] if want_pack else refs[-2:]
+    absorbed = refs[-1] if want_pack else None
     chunk = pl.program_id(0)
     first = chunk * TI
     lowest = start_ref[0]
@@ -228,7 +229,7 @@
             lax.fori_loop(0, SRCS, move, 0)
 
 
-def step_call(first_step, want_own, want_pack, ids, helicity_start, now, halo, prev, pot, damping, switch, *weights):
+def step_call(first_step, want_own, want_pack, ids, helicity_start, now, halo, prev, pot, damping, switch, *weights, others=()):
     field = (HEL, CR, CS, NA)
     edge = (HEL, CR, NA)
     stack = (10, 3 * NA, NA)
@@ -244,6 +245,9 @@
     if first_step:
         out_specs += [whole(edge)] * 4 + [whole(stack)]
         out_shape += [jax.ShapeDtypeStruct(edge, F32)] * 4 + [jax.ShapeDtypeStruct(stack, BF16)]
+    specs, shapes = untouched(others)
+    out_specs += specs
+    out_shape += shapes
     scratch += [pltpu.VMEM((HEL, ROWS, NA), F32)] * 2
     if want_pack:
         scratch.append(pltpu.VMEM(field, F32))
@@ -274,8 +278,11 @@
     )(*((ids,) if want_pack else ()), helicity_start, now, *halo, prev, pot, damping, switch, *weights)
 
 
-def inflow_kernel(want_edges, swap, x_ref, f_high, f_low, b_high, b_low, acc_ref, *refs):
-    half = SRCS * BLK
+def inflow_kernel(count, want_edges, *refs):
+    x_refs, refs = refs[:count], refs[count:]
+    f_high, f_low, b_high, b_low, acc_ref, *refs = refs
+    step = x_refs[0].shape[0] * BLK
+    rows_in = count * step
     out_ref = refs[0]
     terms = refs[-1]
     product_section = lax.axis_index("sec") == 1
@@ -284,17 +291,15 @@
     def _():
         for k in range(HEL):
             lanes = slice(k * NA, (k + 1) * NA)
-            for part in range(2):
-                source = (1 - part if swap else part) * (SRCS // 2)
-                row = part * half // 2
-                high, low = split(x_ref[source : source + SRCS // 2, k].reshape(half // 2, NA))
-                terms[row : row + half // 2, lanes] = high
-                terms[half + row : half + row + half // 2, lanes] = low
+            for n, x_ref in enumerate(x_refs):
+                high, low = split(x_ref[:, k].reshape(step, NA))
+                terms[n * step : (n + 1) * step, lanes] = high
+                terms[rows_in + n * step : rows_in + (n + 1) * step, lanes] = low
 
     @pl.when(product_section)
     def _():
         wide = dot(terms[...], f_high[0])
-        high, low = split(wide[:half] + wide[half:] + dot(terms[0:half], f_low[0]))
+        high, low = split(wide[:rows_in] + wide[rows_in:] + dot(terms[0:rows_in], f_low[0]))
         for r in range(2):
             rows = slice(r * PTS // 2, (r + 1) * PTS // 2)
             gain = dot(b_high[rows], high) + dot(b_low[rows], high) + dot(b_high[rows], low)
@@ -313,24 +318,24 @@
         right_ref[0] = out_ref[0, :, CS - 1, :]
 
 
-def inflow_call(part, want_edges, swap, x, frame, blend, acc, flops=1000):
-    half = SRCS * BLK
+def inflow_call(part, want_edges, xs, frame, blend, acc, flops=1000):
+    rows_in = len(xs) * xs[0].shape[0] * BLK
     column = pl.BlockSpec((1, HEL * NA, NA), lambda n: (n, 0, 0))
-    weights = pl.BlockSpec((PTS, half), lambda n: (0, part))
+    weights = pl.BlockSpec((PTS, rows_in), lambda n: (0, part))
     field = pl.BlockSpec((1, CR, CS, NA), lambda n: (n, 0, 0, 0))
     edge = pl.BlockSpec((1, CR, NA), lambda n: (n, 0, 0))
     count = 4 if want_edges else 0
     return pl.pallas_call(
-        functools.partial(inflow_kernel, want_edges, swap),
+        functools.partial(inflow_kernel, len(xs), want_edges),
         grid=(HEL,),
-        in_specs=[whole((SRCS, HEL, BLK, NA)), column, column, weights, weights, field],
+        in_specs=[whole(x.shape) for x in xs] + [column, column, weights, weights, field],
         out_specs=[field] + [edge] * count,
         out_shape=[jax.ShapeDtypeStruct((HEL, CR, CS, NA), F32)] + [jax.ShapeDtypeStruct((HEL, CR, NA), F32)] * count,
-        scratch_shapes=[pltpu.VMEM((2 * half, HEL * NA), BF16)],
+        scratch_shapes=[pltpu.VMEM((2 * rows_in, HEL * NA), BF16)],
         compiler_params=pltpu.CompilerParams(vmem_limit_bytes=56 * MIB),
         cost_estimate=pl.CostEstimate(flops=flops, transcendentals=0, bytes_accessed=1000),
         name="inflow_edges" if want_edges else "inflow",
-    )(x, *frame, *blend, acc)
+    )(*xs, *frame, *blend, acc)
 
 
 def exchange(top, bottom, left, right):
@@ -385,17 +390,20 @@
     )
     crossed_one_1 = cross(one_1)
     halo = exchange(*rims)
-    zero_1, halo = lax.optimization_barrier((zero_1, halo))
     relayed_1 = spread(zero_1)
-    packed = (SRCS, HEL, BLK, NA)
+    pack_shapes = [jax.ShapeDtypeStruct((SRCS, HEL, BLK, NA), F32)] * 2
+    blend_shapes = [jax.ShapeDtypeStruct((PTS, PTS), BF16)] * 2
+    frame_shapes = [jax.ShapeDtypeStruct((HEL, HEL * NA, NA), BF16)] * 2
 
     def reactant(own, halo, weights, *_):
-        one, zero = step_call(False, False, True, ids, helicity_start, own, halo, current, *fixed, weights)
-        return one, zero, (jnp.zeros((PTS, PTS), BF16),) * 2, (jnp.zeros((HEL, HEL * NA, NA), BF16),) * 2
+        one, zero, *rest = step_call(
+            False, False, True, ids, helicity_start, own, halo, current, *fixed, weights, others=blend_shapes + frame_shapes
+        )
+        return one, zero, tuple(rest[:2]), tuple(rest[2:])
 
     def product(own, halo, weights, picks, tiles, frame_map):
-        blend = blend_call(picks, jnp.tile(tiles, (1, 1, 1, 128 // BLK)))
-        return jnp.zeros(packed, F32), jnp.zeros(packed, F32), tuple(blend), frame_terms(frame_map)
+        high, low, one, zero = blend_call(picks, jnp.tile(tiles, (1, 1, 1, 128 // BLK)), pack_shapes)
+        return one, zero, (high, low), frame_terms(frame_map)
 
     picks = pick_slots[0, 0].T.reshape(MSLOT * NBLK)
     one_2, zero_2, blend, frame = lax.cond(
@@ -407,14 +415,14 @@
     one_2, shared = lax.optimization_barrier((one_2, shared))
     relayed_2 = spread(one_2)
 
-    (new_1,) = inflow_call(0, False, False, crossed_zero_1, frame, blend, own_1, 40 << 30)
-    new_1, *rims = inflow_call(1, True, False, shared, frame, blend, new_1)
+    new_1, *rims = inflow_call(0, True, (crossed_zero_1, shared), frame, blend, own_1, 40 << 30)
     relayed_2, rims = lax.optimization_barrier((relayed_2, rims))
-    crossed_one_2 = cross(relayed_2)
+    first_2, last_2 = cross(relayed_2[: SRCS // 2]), cross(relayed_2[SRCS // 2 :])
     halo = exchange(*rims)
     (own_2,) = step_call(False, True, False, ids, helicity_start, new_1, halo, current, *fixed, weights)
-    (new_2,) = inflow_call(0, False, False, crossed_zero_2, frame, blend, own_2)
-    (new_2,) = inflow_call(1, False, True, crossed_one_2, frame, blend, new_2)
+    (new_2,) = inflow_call(0, False, (crossed_zero_2,), frame, blend, own_2)
+    (new_2,) = inflow_call(3, False, (first_2,), frame, blend, new_2)
+    (new_2,) = inflow_call(2, False, (last_2,), frame, blend, new_2)
     return new_1[None], new_2[None]
 
 

time: 267 us -> 263 us (0.985)
  starting transfers between devices: 60 us -> 64.3 us
  Pallas kernels: 115 us -> 111 us
    ppermute x12, waiting for transfers between devices: 13 us -> 26.7 us  [send(): return lax.ppermute(piece, axis, pairs)]
    ppermute x4 -> x5, waiting for transfers between devices: 15.4 us -> 3.7 us  [cross(): return lax.ppermute(x, ALL, pairs)]
    pallas_call x1, Pallas kernels: 11 us -> 6.97 us  [blend_call(): pl.pallas_call(blend_kernel, in_specs=[smem(), pl.BlockSpec(memory_space=...]
    all_to_all x2, waiting for transfers between devices: 3.55 us -> 0.01 us  [spread(): lax.all_to_all(x, ('rr', 'sr'), split_axis=0, concat_axis=0, tiled=True)]
    slice x0 -> x1, local copies, waits for them, and re-layouts: none -> 3.28 us  [per_device(): relayed_2[:SRCS // 2]]
    another operation x4 -> x2, local copies, waits for them, and re-layouts: 7.03 us -> 3.86 us  [product(): jnp.tile(tiles, (1, 1, 1, 128 // BLK))]
    ppermute x4 -> x5, starting transfers between devices: 5.34 us -> 6.62 us  [cross(): return lax.ppermute(x, ALL, pairs)]
  transfers between devices with their start and end apart: 18 -> 19, of which waited for: 7 -> 6; matrix products, arithmetic and copies ran while one was open for 6% -> 7% of each run, Pallas kernels for 30% -> 31%
where the time goes in v3:
time: 263 us; the launch traced here: 262 us
  Pallas kernels  111 us (42%)
  starting transfers between devices  64.3 us (24%)
  blocking collectives  34 us (13%)
  waiting for transfers between devices  30.4 us (12%)
  local copies, waits for them, and re-layouts  15 us (6%)
  other arithmetic  5.55 us (2%)
    pallas_call x4, Pallas kernels, inflow_call(): pl.pallas_call(functools.partial(inflow_kernel, len(xs), want_edges), gri...  71.7 us
    ppermute x12, starting transfers between devices, send(): return lax.ppermute(piece, axis, pairs)  42.2 us
    all_to_all x1, blocking collectives, spread(): lax.all_to_all(x, ('rr', 'sr'), split_axis=0, concat_axis=0, tiled=True)  34 us
    pallas_call x2, Pallas kernels, step_call(): pl.pallas_call(functools.partial(step_kernel, first_step, want_own, want_...  32.2 us
    ppermute x12, waiting for transfers between devices, send(): return lax.ppermute(piece, axis, pairs)  26.7 us
    all_to_all x2, starting transfers between devices, spread(): lax.all_to_all(x, ('rr', 'sr'), split_axis=0, concat_axis=0, tiled=True)  15.5 us
    pallas_call x1, Pallas kernels, blend_call(): pl.pallas_call(blend_kernel, in_specs=[smem(), pl.BlockSpec(memory_space=...  6.97 us
    ppermute x5, starting transfers between devices, cross(): return lax.ppermute(x, ALL, pairs)  6.62 us
  transfers between devices with their start and end apart: 19, of which 6 were waited for; matrix products, arithmetic and copies ran while one was open for 7% of the time, Pallas kernels for 31%

profile of v3, /device:TPU:27, one launch (start us, length us, event | category | flops | bytes accessed | tf_op | source)
XLA Modules:
  0.0 261.9 jit_solution(5789329659235637978)
XLA Ops:
  0.7 1.8 fusion.1
  2.5 3.7 %collective-permute-start.2 = (f32[4,32,256]{2,1,0:T(8,128)S(1)}, f32[4,32,256]{2,1,0:T(8,128)S(1)}, u32[]{:S(2)}, u32[]{:S(2)}) collective-permute-start(f32[4,32,256]{2,1,0:T(8,128)S(1)} %bitcast.50), channel_id=1, source_target_pairs={{0,1},{1,2},{2,3},{3,4},{4,5},{5,6},{6,7},{8,9},{9,10},{10,11},{11... | collective-permute-start | bytes 393224 | tf_op jit(solution)/shard_map/ppermute | solution.py:346
  6.2 1.9 collective-permute-start.3
  9.1 5.8 %collective-permute-start.1 = (f32[4,32,256]{2,1,0:T(8,128)S(1)}, f32[4,32,256]{2,1,0:T(8,128)S(1)}, u32[]{:S(2)}, u32[]{:S(2)}) collective-permute-start(f32[4,32,256]{2,1,0:T(8,128)S(1)} %get-tuple-element.129), channel_id=1, source_target_pairs={{8,0},{16,8},{24,16},{32,24},{40,32},{48,40},{56,48},{9,1},{17,9},... | collective-permute-start | bytes 393224 | tf_op jit(solution)/shard_map/ppermute | solution.py:346
  15.0 1.9 collective-permute-start
  17.9 4.9 %collective-permute-done.refs_3_ = f32[4,32,256]{2,1,0:T(8,128)S(1)} collective-permute-done((f32[4,32,256]{2,1,0:T(8,128)S(1)}, f32[4,32,256]{2,1,0:T(8,128)S(1)}, u32[]{:S(2)}, u32[]{:S(2)}) %collective-permute-start) | collective-permute-done | bytes 131104 | tf_op jit(solution)/shard_map/ppermute | solution.py:346
  23.5 18.2 %step_first.1 = (f32[4,32,32,256]{3,2,1,0:T(8,128)}, f32[64,4,8,256]{3,2,1,0:T(8,128)}, f32[64,4,8,256]{3,2,1,0:T(8,128)}, f32[4,32,256]{2,1,0:T(8,128)}, f32[4,...) custom-call(s32[128]{0:T(128)S(1)} %reshape.17.refs_0_, ...), custom_call_target="tpu_custom_call" | custom-call | flops 1000 | bytes 1000 | tf_op jit(solution)/shard_map/step_first/pallas_call | solution.py:255
  43.0 8.4 %all-to-all-start = ((f32[64,4,8,256]{3,2,1,0:T(8,128)}), f32[64,4,8,256]{3,2,1,0:T(8,128)}, u32[]{:S(2)}, u32[]{:S(2)}) async-start(f32[64,4,8,256]{3,2,1,0:T(8,128)} %get-tuple-element.77), calls=%async_computation | async-start | bytes 4194304 | tf_op jit(solution)/shard_map/all_to_all | solution.py:362
  51.5 3.1 %collective-permute-start.5 = (f32[4,32,256]{2,1,0:T(8,128)S(1)}, f32[4,32,256]{2,1,0:T(8,128)S(1)}, u32[]{:S(2)}, u32[]{:S(2)}) collective-permute-start(f32[4,32,256]{2,1,0:T(8,128)S(1)} %copy-done.22), channel_id=1, source_target_pairs={{0,8},{8,16},{16,24},{24,32},{32,40},{40,48},{48,56},{1,9},{9,17},... | collective-permute-start | bytes 393224 | tf_op jit(solution)/shard_map/ppermute | solution.py:346
  54.7 4.2 %collective-permute-start.6 = (f32[4,32,256]{2,1,0:T(8,128)S(1)}, f32[4,32,256]{2,1,0:T(8,128)S(1)}, u32[]{:S(2)}, u32[]{:S(2)}) collective-permute-start(f32[4,32,256]{2,1,0:T(8,128)S(1)} %copy-done.21), channel_id=1, source_target_pairs={{8,0},{16,8},{24,16},{32,24},{40,32},{48,40},{56,48},{9,1},{17,9},... | collective-permute-start | bytes 393224 | tf_op jit(solution)/shard_map/ppermute | solution.py:346
  58.9 3.9 %collective-permute-start.7 = (f32[4,32,256]{2,1,0:T(8,128)S(1)}, f32[4,32,256]{2,1,0:T(8,128)S(1)}, u32[]{:S(2)}, u32[]{:S(2)}) collective-permute-start(f32[4,32,256]{2,1,0:T(8,128)S(1)} %copy-done.20), channel_id=1, source_target_pairs={{0,1},{1,2},{2,3},{3,4},{4,5},{5,6},{6,7},{8,9},{9,10},{10,11},{11... | collective-permute-start | bytes 393224 | tf_op jit(solution)/shard_map/ppermute | solution.py:346
  62.8 1.9 collective-permute-start.8
  64.8 16.2 %collective-permute-done.5 = f32[4,32,256]{2,1,0:T(8,128)S(1)} collective-permute-done((f32[4,32,256]{2,1,0:T(8,128)S(1)}, f32[4,32,256]{2,1,0:T(8,128)S(1)}, u32[]{:S(2)}, u32[]{:S(2)}) %collective-permute-start.5) | collective-permute-done | bytes 131104 | tf_op jit(solution)/shard_map/ppermute | solution.py:346
  81.1 17.7 %conditional.1 = ((f32[64,4,8,256]{3,2,1,0:T(8,128)}, f32[64,4,8,256]{3,2,1,0:T(8,128)}, bf16[1024,1024]{1,0:T(8,128)(2,1)}, bf16[1024,1024]{1,0:T(8,128)(2,1)},...) conditional(s32[]{:T(128)} %convert_element_type.9, (f32[1,1,128,4,8,8]{2,5,4,3,1,0:T(8,128)S(1)}, ...), branch_computations={%region_0.1_spmd, %region_1.2_spmd} | conditional | flops 12582912 | bytes 29491256 | solution.py:409
  82.6 2.4 copy.28.tile_ref
  85.0 3.5 %fusion = (bf16[4,1024,256]{2,0,1:T(4,128)(2,1)S(1)}, bf16[4,1024,256]{2,0,1:T(4,128)(2,1)S(1)}) fusion(f32[4,256,4,256]{3,2,1,0:T(4,128)} %get-tuple-element.107), kind=kLoop, calls=%fused_computation.2 | loop fusion | flops 4194304 | bytes 8388608 | tf_op jit(solution)/shard_map/cond/branch_0_fun/convert_element_type | solution.py:53
  91.8 7.0 %blend_matrix.1 = (bf16[1024,1024]{1,0:T(8,128)(2,1)}, bf16[1024,1024]{1,0:T(8,128)(2,1)}, f32[64,4,8,256]{3,2,1,0:T(8,128)}, f32[64,4,8,256]{3,2,1,0:T(8,128)}) custom-call(s32[512]{0:T(512)S(1)} %bitcast.53, f32[128,4,8,128]{3,2,1,0:T(8,128)S(1)} %copy.28.tile_ref), custom_call_target="tpu_custom_call" | custom-call | flops 8388608 | bytes 6291456 | tf_op jit(solution)/shard_map/cond/branch_0_fun/blend_matrix/pallas_call | solution.py:86
  100.1 2.1 broadcast_select_fusion
  102.1 34.0 %all_to_all.15.refs_1_ = f32[64,4,8,256]{3,2,1,0:T(8,128)} all-to-all(f32[64,4,8,256]{3,2,1,0:T(8,128)S(1)} %broadcast_select_fusion), channel_id=1, replica_groups=mesh['sec'=2,'rr'=8,'sr'=8] {'rr','sr'}, dimensions={0} | all-to-all | bytes 4194304 | tf_op jit(solution)/shard_map/all_to_all | solution.py:362
  136.1 7.0 %all-to-all-start.2 = ((f32[64,4,8,256]{3,2,1,0:T(8,128)}), f32[64,4,8,256]{3,2,1,0:T(8,128)}, u32[]{:S(2)}, u32[]{:S(2)}) async-start(f32[64,4,8,256]{3,2,1,0:T(8,128)} %get-tuple-element.93), calls=%async_computation.2 | async-start | bytes 4194304 | tf_op jit(solution)/shard_map/all_to_all | solution.py:362
  144.7 3.7 %collective-permute-done.4.refs_0_ = f32[64,4,8,256]{3,2,1,0:T(8,128)} collective-permute-done((f32[64,4,8,256]{3,2,1,0:T(8,128)}, f32[64,4,8,256]{3,2,1,0:T(8,128)}, u32[]{:S(2)}, u32[]{:S(2)}) %collective-permute-start.4) | collective-permute-done | bytes 2097184 | tf_op jit(solution)/shard_map/ppermute | solution.py:358
  148.4 32.3 %inflow_edges.1 = (f32[4,32,32,256]{3,2,1,0:T(8,128)}, f32[4,32,256]{2,1,0:T(8,128)}, f32[4,32,256]{2,1,0:T(8,128)}, f32[4,32,256]{2,1,0:T(8,128)}, f32[4,32,256]{2,1,0:T(8,128)}) custom-call(f32[64,4,8,256]{3,2,1,0:T(8,128)} %collective-permute-done.4.refs_0_, f32[64,4,8,256]{3,2,1,0:T(8,128)} %all_to_all.15.refs_1_, ...), custom_call_target="tpu_custom_call" | custom-call | flops 42949672960 | bytes 1000 | tf_op jit(solution)/shard_map/inflow_edges/pallas_call | solution.py:328
  180.7 3.3 %fusion.2 = (f32[32,4,8,256]{3,2,1,0:T(8,128)}, f32[32,4,8,256]{3,2,1,0:T(8,128)}) fusion(f32[64,4,8,256]{3,2,1,0:T(8,128)} %all-to-all-done.2), kind=kLoop, calls=%fused_computation.11 | loop fusion | bytes 4194304 | tf_op jit(solution)/shard_map/slice | solution.py:420
  186.6 1.9 collective-permute-start.13
  188.5 5.5 %collective-permute-start.14 = (f32[4,32,256]{2,1,0:T(8,128)}, f32[4,32,256]{2,1,0:T(8,128)S(1)}, u32[]{:S(2)}, u32[]{:S(2)}) collective-permute-start(f32[4,32,256]{2,1,0:T(8,128)} %get-tuple-element.100), channel_id=1, source_target_pairs={{8,0},{16,8},{24,16},{32,24},{40,32},{48,40},{56,48},{9,1},{17,9},... | collective-permute-start | bytes 393224 | tf_op jit(solution)/shard_map/ppermute | solution.py:346
  194.6 6.3 %collective-permute-start.15 = (f32[4,32,256]{2,1,0:T(8,128)}, f32[4,32,256]{2,1,0:T(8,128)S(1)}, u32[]{:S(2)}, u32[]{:S(2)}) collective-permute-start(f32[4,32,256]{2,1,0:T(8,128)} %get-tuple-element.101), channel_id=1, source_target_pairs={{0,1},{1,2},{2,3},{3,4},{4,5},{5,6},{6,7},{8,9},{9,10},{10,11},{11... | collective-permute-start | bytes 393224 | tf_op jit(solution)/shard_map/ppermute | solution.py:346
  200.9 1.9 collective-permute-start.16
  203.1 4.7 %collective-permute-done.16.refs_5_ = f32[4,32,256]{2,1,0:T(8,128)S(1)} collective-permute-done((f32[4,32,256]{2,1,0:T(8,128)}, f32[4,32,256]{2,1,0:T(8,128)S(1)}, u32[]{:S(2)}, u32[]{:S(2)}) %collective-permute-start.16) | collective-permute-done | bytes 131104 | tf_op jit(solution)/shard_map/ppermute | solution.py:346
  208.4 14.1 %step_own.1.refs_5_ = f32[4,32,32,256]{3,2,1,0:T(8,128)} custom-call(s32[1]{0:T(128)S(6)} %copy.62.refs_1_.refs_0_, f32[4,32,32,256]{3,2,1,0:T(8,128)} %get-tuple-element.92.refs_1_, f32[4,32,256]{2,1,0:T(8,128)} %copy-done.13, f32[4,32,256]{2,1,0:T(8,128)} %copy-done.14, f32[4,32,256]{2,1,0:T(8,128)} %copy-done.15, f32[4,32,256]{2,1,0:T(8,128)} %copy-done.16, ...), custom_call_target="tpu_custom_call" | custom-call | flops 1000 | bytes 1000 | tf_op jit(solution)/shard_map/step_own/pallas_call | solution.py:255
  222.5 18.1 %inflow.3.refs_5_ = f32[4,32,32,256]{3,2,1,0:T(8,128)} custom-call(f32[64,4,8,256]{3,2,1,0:T(8,128)} %collective-permute-done.12.refs_0_, bf16[4,1024,256]{2,1,0:T(8,128)(2,1)} %get-tuple-element.123.refs_2_.refs_1_, bf16[4,1024,256]{2,1,0:T(8,128)(2,1)S(1)} %copy-done.3, bf16[1024,1024]{1,0:T(8,128)(2,1)} %get-tuple-element.90.refs_4_.refs_3_, ...), custom_call_target="tpu_custom_call" | custom-call | flops 1000 | bytes 1000 | tf_op jit(solution)/shard_map/inflow/pallas_call | solution.py:328
  240.7 10.7 %inflow.4.refs_5_ = f32[4,32,32,256]{3,2,1,0:T(8,128)} custom-call(f32[32,4,8,256]{3,2,1,0:T(8,128)} %collective-permute-done.11.refs_0_, bf16[4,1024,256]{2,1,0:T(8,128)(2,1)S(1)} %copy-done.4, bf16[4,1024,256]{2,1,0:T(8,128)(2,1)S(1)} %copy-done.3, bf16[1024,1024]{1,0:T(8,128)(2,1)S(1)} %copy-done.5, bf16[1024,1024]{1,0:T(8,128)(2,1)} %get-tuple-element.91.refs_5_.refs_4_, ...), custom_call_target="tpu_custom_call" | custom-call | flops 1000 | bytes 1000 | tf_op jit(solution)/shard_map/inflow/pallas_call | solution.py:328
  251.3 10.6 %inflow.5 = f32[4,32,32,256]{3,2,1,0:T(8,128)} custom-call(f32[32,4,8,256]{3,2,1,0:T(8,128)} %collective-permute-done.10.refs_0_, bf16[4,1024,256]{2,1,0:T(8,128)(2,1)S(1)} %copy-done.4, bf16[4,1024,256]{2,1,0:T(8,128)(2,1)S(1)} %copy-done.3, bf16[1024,1024]{1,0:T(8,128)(2,1)S(1)} %copy-done.5, bf16[1024,1024]{1,0:T(8,128)(2,1)} %get-tuple-element.91.refs_5_.refs_4_, ...), custom_call_target="tpu_custom_call" | custom-call | flops 1000 | bytes 1000 | tf_op jit(solution)/shard_map/inflow/pallas_call | solution.py:328
  (75 shorter events, 15.1 us)
Async XLA Ops:
  0.6 16.9 %copy-start = (s32[64,64,2]{1,2,0:T(2,128)S(1)}, s32[64,64,2]{1,2,0:T(2,128)}, u32[]{:S(2)}) copy-start(s32[64,64,2]{1,2,0:T(2,128)} %param.23) | copy-start | bytes 98308
  0.6 22.8 %copy-start.6 = (f32[1,32,32,256]{3,2,1,0:T(8,128)S(1)}, f32[1,32,32,256]{3,2,1,0:T(8,128)}, u32[]{:S(2)}) copy-start(f32[1,32,32,256]{3,2,1,0:T(8,128)} %param.16) | copy-start | bytes 3145732
  2.5 15.4 %collective-permute-start.2 = (f32[4,32,256]{2,1,0:T(8,128)S(1)}, f32[4,32,256]{2,1,0:T(8,128)S(1)}, u32[]{:S(2)}, u32[]{:S(2)}) collective-permute-start(f32[4,32,256]{2,1,0:T(8,128)S(1)} %bitcast.50), channel_id=1, source_target_pairs={{0,1},{1,2},{2,3},{3,4},{4,5},{5,6},{6,7},{8,9},{9,10},{10,11},{11... | collective-permute-start | bytes 393224 | tf_op jit(solution)/shard_map/ppermute | solution.py:346
  6.2 11.7 %collective-permute-start.3 = (f32[4,32,256]{2,1,0:T(8,128)S(1)}, f32[4,32,256]{2,1,0:T(8,128)S(1)}, u32[]{:S(2)}, u32[]{:S(2)}) collective-permute-start(f32[4,32,256]{2,1,0:T(8,128)S(1)} %bitcast.51), channel_id=1, source_target_pairs={{1,0},{2,1},{3,2},{4,3},{5,4},{6,5},{7,6},{9,8},{10,9},{11,10},{12... | collective-permute-start | bytes 393224 | tf_op jit(solution)/shard_map/ppermute | solution.py:346
  9.1 8.8 %collective-permute-start.1 = (f32[4,32,256]{2,1,0:T(8,128)S(1)}, f32[4,32,256]{2,1,0:T(8,128)S(1)}, u32[]{:S(2)}, u32[]{:S(2)}) collective-permute-start(f32[4,32,256]{2,1,0:T(8,128)S(1)} %get-tuple-element.129), channel_id=1, source_target_pairs={{8,0},{16,8},{24,16},{32,24},{40,32},{48,40},{56,48},{9,1},{17,9},... | collective-permute-start | bytes 393224 | tf_op jit(solution)/shard_map/ppermute | solution.py:346
  15.0 7.8 %collective-permute-start = (f32[4,32,256]{2,1,0:T(8,128)S(1)}, f32[4,32,256]{2,1,0:T(8,128)S(1)}, u32[]{:S(2)}, u32[]{:S(2)}) collective-permute-start(f32[4,32,256]{2,1,0:T(8,128)S(1)} %get-tuple-element.130), channel_id=1, source_target_pairs={{0,8},{8,16},{16,24},{24,32},{32,40},{40,48},{48,56},{1,9},{9,17},... | collective-permute-start | bytes 393224 | tf_op jit(solution)/shard_map/ppermute | solution.py:346
  41.6 58.4 %collective-permute-start.9 = (f32[64,4,8,256]{3,2,1,0:T(8,128)}, f32[64,4,8,256]{3,2,1,0:T(8,128)}, u32[]{:S(2)}, u32[]{:S(2)}) collective-permute-start(f32[64,4,8,256]{3,2,1,0:T(8,128)} %get-tuple-element.86), channel_id=1, source_target_pairs={{0,96},{1,97},{2,98},{3,99},{4,100},{5,101},{6,102},{7,103},{8,104... | collective-permute-start | bytes 6291464 | tf_op jit(solution)/shard_map/ppermute | solution.py:358
  43.0 15.9 %copy-start.20 = (f32[4,32,256]{2,1,0:T(8,128)S(1)}, f32[4,32,256]{2,1,0:T(8,128)}, u32[]{:S(2)}) copy-start(f32[4,32,256]{2,1,0:T(8,128)} %get-tuple-element.81) | copy-start | bytes 393220
  43.0 19.9 %copy-start.19 = (f32[4,32,256]{2,1,0:T(8,128)S(1)}, f32[4,32,256]{2,1,0:T(8,128)}, u32[]{:S(2)}) copy-start(f32[4,32,256]{2,1,0:T(8,128)} %get-tuple-element.82) | copy-start | bytes 393220
  43.0 38.1 %copy-start.7 = (f32[1,32,32]{2,1,0:T(8,128)S(1)}, f32[1,32,32]{2,1,0:T(8,128)}, u32[]{:S(2)}) copy-start(f32[1,32,32]{2,1,0:T(8,128)} %param.17) | copy-start | bytes 12292
  43.0 38.1 %copy-start.8 = (f32[32,32]{1,0:T(8,128)S(1)}, f32[32,32]{1,0:T(8,128)}, u32[]{:S(2)}) copy-start(f32[32,32]{1,0:T(8,128)} %refs_9_.1) | copy-start | bytes 12292
  43.0 38.1 %copy-start.17 = (f32[1,1,128,4,8,8]{2,5,4,3,1,0:T(8,128)S(1)}, f32[1,1,128,4,8,8]{2,5,4,3,1,0:T(8,128)}, u32[]{:S(2)}) copy-start(f32[1,1,128,4,8,8]{2,5,4,3,1,0:T(8,128)} %param.25) | copy-start | bytes 393220
  43.0 38.1 %copy-start.18 = (s32[1,1,128,4]{2,3,1,0:T(4,128)S(1)}, s32[1,1,128,4]{2,3,1,0:T(4,128)}, u32[]{:S(2)}) copy-start(s32[1,1,128,4]{2,3,1,0:T(4,128)} %param.24) | copy-start | bytes 6148
  43.0 55.7 %all-to-all-start = ((f32[64,4,8,256]{3,2,1,0:T(8,128)}), f32[64,4,8,256]{3,2,1,0:T(8,128)}, u32[]{:S(2)}, u32[]{:S(2)}) async-start(f32[64,4,8,256]{3,2,1,0:T(8,128)} %get-tuple-element.77), calls=%async_computation | async-start | bytes 4194304 | tf_op jit(solution)/shard_map/all_to_all | solution.py:362
  51.5 29.5 %collective-permute-start.5 = (f32[4,32,256]{2,1,0:T(8,128)S(1)}, f32[4,32,256]{2,1,0:T(8,128)S(1)}, u32[]{:S(2)}, u32[]{:S(2)}) collective-permute-start(f32[4,32,256]{2,1,0:T(8,128)S(1)} %copy-done.22), channel_id=1, source_target_pairs={{0,8},{8,16},{16,24},{24,32},{32,40},{40,48},{48,56},{1,9},{9,17},... | collective-permute-start | bytes 393224 | tf_op jit(solution)/shard_map/ppermute | solution.py:346
  54.7 26.4 %collective-permute-start.6 = (f32[4,32,256]{2,1,0:T(8,128)S(1)}, f32[4,32,256]{2,1,0:T(8,128)S(1)}, u32[]{:S(2)}, u32[]{:S(2)}) collective-permute-start(f32[4,32,256]{2,1,0:T(8,128)S(1)} %copy-done.21), channel_id=1, source_target_pairs={{8,0},{16,8},{24,16},{32,24},{40,32},{48,40},{56,48},{9,1},{17,9},... | collective-permute-start | bytes 393224 | tf_op jit(solution)/shard_map/ppermute | solution.py:346
  58.9 22.1 %collective-permute-start.7 = (f32[4,32,256]{2,1,0:T(8,128)S(1)}, f32[4,32,256]{2,1,0:T(8,128)S(1)}, u32[]{:S(2)}, u32[]{:S(2)}) collective-permute-start(f32[4,32,256]{2,1,0:T(8,128)S(1)} %copy-done.20), channel_id=1, source_target_pairs={{0,1},{1,2},{2,3},{3,4},{4,5},{5,6},{6,7},{8,9},{9,10},{10,11},{11... | collective-permute-start | bytes 393224 | tf_op jit(solution)/shard_map/ppermute | solution.py:346
  62.8 18.2 %collective-permute-start.8 = (f32[4,32,256]{2,1,0:T(8,128)S(1)}, f32[4,32,256]{2,1,0:T(8,128)S(1)}, u32[]{:S(2)}, u32[]{:S(2)}) collective-permute-start(f32[4,32,256]{2,1,0:T(8,128)S(1)} %copy-done.19), channel_id=1, source_target_pairs={{1,0},{2,1},{3,2},{4,3},{5,4},{6,5},{7,6},{9,8},{10,9},{11,10},{12... | collective-permute-start | bytes 393224 | tf_op jit(solution)/shard_map/ppermute | solution.py:346
  98.8 49.6 %collective-permute-start.4 = (f32[64,4,8,256]{3,2,1,0:T(8,128)}, f32[64,4,8,256]{3,2,1,0:T(8,128)}, u32[]{:S(2)}, u32[]{:S(2)}) collective-permute-start(f32[64,4,8,256]{3,2,1,0:T(8,128)} %all-to-all-done), channel_id=1, source_target_pairs={{0,96},{1,97},{2,98},{3,99},{4,100},{5,101},{6,102},{7,103},{8,104... | collective-permute-start | bytes 6291464 | tf_op jit(solution)/shard_map/ppermute | solution.py:358
  136.1 12.2 %copy-start.3 = (bf16[4,1024,256]{2,1,0:T(8,128)(2,1)S(1)}, bf16[4,1024,256]{2,1,0:T(8,128)(2,1)}, u32[]{:S(2)}) copy-start(bf16[4,1024,256]{2,1,0:T(8,128)(2,1)} %get-tuple-element.124.refs_3_.refs_2_) | copy-start | bytes 6291460
  136.1 44.5 %all-to-all-start.2 = ((f32[64,4,8,256]{3,2,1,0:T(8,128)}), f32[64,4,8,256]{3,2,1,0:T(8,128)}, u32[]{:S(2)}, u32[]{:S(2)}) async-start(f32[64,4,8,256]{3,2,1,0:T(8,128)} %get-tuple-element.93), calls=%async_computation.2 | async-start | bytes 4194304 | tf_op jit(solution)/shard_map/all_to_all | solution.py:362
  143.2 79.3 %collective-permute-start.12 = (f32[64,4,8,256]{3,2,1,0:T(8,128)}, f32[64,4,8,256]{3,2,1,0:T(8,128)}, u32[]{:S(2)}, u32[]{:S(2)}) collective-permute-start(f32[64,4,8,256]{3,2,1,0:T(8,128)} %all_to_all.15.refs_1_), channel_id=1, source_target_pairs={{0,96},{1,97},{2,98},{3,99},{4,100},{5,101},{6,102},{7,103},{8,104... | collective-permute-start | bytes 6291464 | tf_op jit(solution)/shard_map/ppermute | solution.py:358
  180.7 27.7 %copy-start.2 = (f32[1,4,32,32,256]{4,3,2,1,0:T(8,128)S(1)}, f32[1,4,32,32,256]{4,3,2,1,0:T(8,128)}, u32[]{:S(2)}) copy-start(f32[1,4,32,32,256]{4,3,2,1,0:T(8,128)} %param.15) | copy-start | bytes 12582916
  184.0 56.7 %collective-permute-start.11 = (f32[32,4,8,256]{3,2,1,0:T(8,128)}, f32[32,4,8,256]{3,2,1,0:T(8,128)}, u32[]{:S(2)}, u32[]{:S(2)}) collective-permute-start(f32[32,4,8,256]{3,2,1,0:T(8,128)} %get-tuple-element.131), channel_id=1, source_target_pairs={{0,96},{1,97},{2,98},{3,99},{4,100},{5,101},{6,102},{7,103},{8,104... | collective-permute-start | bytes 3145736 | tf_op jit(solution)/shard_map/ppermute | solution.py:358
  185.3 66.1 %collective-permute-start.10 = (f32[32,4,8,256]{3,2,1,0:T(8,128)}, f32[32,4,8,256]{3,2,1,0:T(8,128)}, u32[]{:S(2)}, u32[]{:S(2)}) collective-permute-start(f32[32,4,8,256]{3,2,1,0:T(8,128)} %get-tuple-element.132), channel_id=1, source_target_pairs={{0,96},{1,97},{2,98},{3,99},{4,100},{5,101},{6,102},{7,103},{8,104... | collective-permute-start | bytes 3145736 | tf_op jit(solution)/shard_map/ppermute | solution.py:358
  186.6 8.0 %collective-permute-start.13 = (f32[4,32,256]{2,1,0:T(8,128)}, f32[4,32,256]{2,1,0:T(8,128)S(1)}, u32[]{:S(2)}, u32[]{:S(2)}) collective-permute-start(f32[4,32,256]{2,1,0:T(8,128)} %get-tuple-element.99), channel_id=1, source_target_pairs={{0,8},{8,16},{16,24},{24,32},{32,40},{40,48},{48,56},{1,9},{9,17},... | collective-permute-start | bytes 393224 | tf_op jit(solution)/shard_map/ppermute | solution.py:346
  188.5 12.4 %collective-permute-start.14 = (f32[4,32,256]{2,1,0:T(8,128)}, f32[4,32,256]{2,1,0:T(8,128)S(1)}, u32[]{:S(2)}, u32[]{:S(2)}) collective-permute-start(f32[4,32,256]{2,1,0:T(8,128)} %get-tuple-element.100), channel_id=1, source_target_pairs={{8,0},{16,8},{24,16},{32,24},{40,32},{48,40},{56,48},{9,1},{17,9},... | collective-permute-start | bytes 393224 | tf_op jit(solution)/shard_map/ppermute | solution.py:346
  194.6 13.2 %copy-start.13 = (f32[4,32,256]{2,1,0:T(8,128)}, f32[4,32,256]{2,1,0:T(8,128)S(1)}, u32[]{:S(2)}) copy-start(f32[4,32,256]{2,1,0:T(8,128)S(1)} %collective-permute-done.13.refs_2_) | copy-start | bytes 393220
  194.6 8.5 %collective-permute-start.15 = (f32[4,32,256]{2,1,0:T(8,128)}, f32[4,32,256]{2,1,0:T(8,128)S(1)}, u32[]{:S(2)}, u32[]{:S(2)}) collective-permute-start(f32[4,32,256]{2,1,0:T(8,128)} %get-tuple-element.101), channel_id=1, source_target_pairs={{0,1},{1,2},{2,3},{3,4},{4,5},{5,6},{6,7},{8,9},{9,10},{10,11},{11... | collective-permute-start | bytes 393224 | tf_op jit(solution)/shard_map/ppermute | solution.py:346
  200.9 6.9 %collective-permute-start.16 = (f32[4,32,256]{2,1,0:T(8,128)}, f32[4,32,256]{2,1,0:T(8,128)S(1)}, u32[]{:S(2)}, u32[]{:S(2)}) collective-permute-start(f32[4,32,256]{2,1,0:T(8,128)} %get-tuple-element.102), channel_id=1, source_target_pairs={{1,0},{2,1},{3,2},{4,3},{5,4},{6,5},{7,6},{9,8},{10,9},{11,10},{12... | collective-permute-start | bytes 393224 | tf_op jit(solution)/shard_map/ppermute | solution.py:346
  222.5 18.1 %copy-start.4 = (bf16[4,1024,256]{2,1,0:T(8,128)(2,1)S(1)}, bf16[4,1024,256]{2,1,0:T(8,128)(2,1)}, u32[]{:S(2)}) copy-start(bf16[4,1024,256]{2,1,0:T(8,128)(2,1)} %get-tuple-element.123.refs_2_.refs_1_) | copy-start | bytes 6291460
  222.5 18.2 %copy-start.5 = (bf16[1024,1024]{1,0:T(8,128)(2,1)S(1)}, bf16[1024,1024]{1,0:T(8,128)(2,1)}, u32[]{:S(2)}) copy-start(bf16[1024,1024]{1,0:T(8,128)(2,1)} %get-tuple-element.90.refs_4_.refs_3_) | copy-start | bytes 6291460
  (10 other events, 58.5 us)

commit v4 on v3

--- a/solution.py
+++ b/solution.py
@@ -109,7 +109,8 @@
         w_ref = refs.pop(0)
     own_ref = refs.pop(0) if want_own else None
     if want_pack:
-        pack_one, pack_zero = refs.pop(0), refs.pop(0)
+        pack_ones = [refs.pop(0) for _ in range(2 if first_step else 1)]
+        pack_zero = refs.pop(0)
     if first_step:
         top_ref, bottom_ref, left_ref, right_ref, w_ref = refs[:5]
         refs = refs[5:]
@@ -217,16 +218,25 @@
 
         @pl.when(chunk == CR // TI - 1)
         def _():
+            def copy(slot, target, to):
+                e = jnp.maximum(ids[slot], 0)
+                i = e // (CS // BLK)
+                j = pl.multiple_of((e % (CS // BLK)) * BLK, BLK)
+                for k in range(HEL):
+                    target[to, k] = absorbed[k, i, pl.ds(j, BLK), :]
+
             def move(q, carry):
-                for slot, target in ((q ^ (SRCS // 2), pack_zero), (SRCS + (q if first_step else q ^ (SRCS // 2)), pack_one)):
-                    e = jnp.maximum(ids[slot], 0)
-                    i = e // (CS // BLK)
-                    j = pl.multiple_of((e % (CS // BLK)) * BLK, BLK)
-                    for k in range(HEL):
-                        target[q, k] = absorbed[k, i, pl.ds(j, BLK), :]
+                half = SRCS // 2
+                copy(q + half, pack_zero, q)
+                copy(q, pack_zero, q + half)
+                for n in range(2):
+                    if first_step:
+                        copy(SRCS + half * n + q, pack_ones[n], q)
+                    else:
+                        copy(SRCS + half * (1 - n) + q, pack_ones[0], half * n + q)
                 return carry
 
-            lax.fori_loop(0, SRCS, move, 0)
+            lax.fori_loop(0, SRCS // 2, move, 0)
 
 
 def step_call(first_step, want_own, want_pack, ids, helicity_start, now, halo, prev, pot, damping, switch, *weights, others=()):
@@ -239,9 +249,11 @@
         out_specs.append(rows)
         out_shape.append(jax.ShapeDtypeStruct(field, F32))
     if want_pack:
+        half = (SRCS // 2, HEL, BLK, NA)
         packed = (SRCS, HEL, BLK, NA)
-        out_specs += [whole(packed)] * 2
-        out_shape += [jax.ShapeDtypeStruct(packed, F32)] * 2
+        packs = (half, half, packed) if first_step else (packed, packed)
+        out_specs += [whole(n) for n in packs]
+        out_shape += [jax.ShapeDtypeStruct(n, F32) for n in packs]
     if first_step:
         out_specs += [whole(edge)] * 4 + [whole(stack)]
         out_shape += [jax.ShapeDtypeStruct(edge, F32)] * 4 + [jax.ShapeDtypeStruct(stack, BF16)]
@@ -284,7 +296,7 @@
     step = x_refs[0].shape[0] * BLK
     rows_in = count * step
     out_ref = refs[0]
-    terms = refs[-1]
+    terms, turned = refs[-2:]
     product_section = lax.axis_index("sec") == 1
 
     @pl.when(jnp.logical_and(product_section, pl.program_id(0) == 0))
@@ -298,13 +310,17 @@
 
     @pl.when(product_section)
     def _():
-        wide = dot(terms[...], f_high[0])
-        high, low = split(wide[:rows_in] + wide[rows_in:] + dot(terms[0:rows_in], f_low[0]))
-        for r in range(2):
-            rows = slice(r * PTS // 2, (r + 1) * PTS // 2)
+        for r in range(rows_in // 256):
+            top = slice(r * 256, (r + 1) * 256)
+            bottom = slice(rows_in + r * 256, rows_in + (r + 1) * 256)
+            framed = dot(terms[top], f_high[0]) + dot(terms[bottom], f_high[0]) + dot(terms[top], f_low[0])
+            turned[top], turned[bottom] = split(framed)
+        high, low = turned[0:rows_in], turned[rows_in : 2 * rows_in]
+        for r in range(PTS // 256):
+            rows = slice(r * 256, (r + 1) * 256)
             gain = dot(b_high[rows], high) + dot(b_low[rows], high) + dot(b_high[rows], low)
-            lines = slice(r * CR // 2, (r + 1) * CR // 2)
-            out_ref[0, lines] = acc_ref[0, lines] + gain.reshape(CR // 2, CS, NA)
+            lines = slice(r * 256 // CS, (r + 1) * 256 // CS)
+            out_ref[0, lines] = acc_ref[0, lines] + gain.reshape(256 // CS, CS, NA)
 
     @pl.when(jnp.logical_not(product_section))
     def _():
@@ -331,7 +347,7 @@
         in_specs=[whole(x.shape) for x in xs] + [column, column, weights, weights, field],
         out_specs=[field] + [edge] * count,
         out_shape=[jax.ShapeDtypeStruct((HEL, CR, CS, NA), F32)] + [jax.ShapeDtypeStruct((HEL, CR, NA), F32)] * count,
-        scratch_shapes=[pltpu.VMEM((2 * rows_in, HEL * NA), BF16)],
+        scratch_shapes=[pltpu.VMEM((2 * rows_in, HEL * NA), BF16), pltpu.VMEM((2 * rows_in, NA), BF16)],
         compiler_params=pltpu.CompilerParams(vmem_limit_bytes=56 * MIB),
         cost_estimate=pl.CostEstimate(flops=flops, transcendentals=0, bytes_accessed=1000),
         name="inflow_edges" if want_edges else "inflow",
@@ -385,12 +401,14 @@
 
     fixed = (potential[0], damping[0], switch)
 
-    own_1, one_1, zero_1, *rims, weights = step_call(
+    own_1, one_1, rest_1, zero_1, *rims, weights = step_call(
         True, True, True, ids, helicity_start, current, halo, previous, *fixed, angular[0], coriolis[0]
     )
     crossed_one_1 = cross(one_1)
     halo = exchange(*rims)
     relayed_1 = spread(zero_1)
+    rest_1, halo = lax.optimization_barrier((rest_1, halo))
+    crossed_rest_1 = cross(rest_1)
     pack_shapes = [jax.ShapeDtypeStruct((SRCS, HEL, BLK, NA), F32)] * 2
     blend_shapes = [jax.ShapeDtypeStruct((PTS, PTS), BF16)] * 2
     frame_shapes = [jax.ShapeDtypeStruct((HEL, HEL * NA, NA), BF16)] * 2
@@ -410,7 +428,8 @@
         section == 0, reactant, product, own_1, halo, weights, picks, interp_weights[0, 0], frame_map
     )
     crossed_zero_1 = cross(relayed_1)
-    shared = spread(jnp.where(section == 0, zero_2, crossed_one_1))
+    arrived_1 = jnp.concatenate([crossed_one_1, crossed_rest_1])
+    shared = spread(jnp.where(section == 0, zero_2, arrived_1))
     crossed_zero_2 = cross(shared)
     one_2, shared = lax.optimization_barrier((one_2, shared))
     relayed_2 = spread(one_2)

time: 263 us -> 266 us (1.011)
  waiting for transfers between devices: 30.4 us -> 49.7 us
  Pallas kernels: 111 us -> 92.3 us
    pallas_call x4, Pallas kernels: 71.7 us -> 53.2 us  [inflow_call(): pl.pallas_call(functools.partial(inflow_kernel, len(xs), want_edges), gri...]
    ppermute x5 -> x6, waiting for transfers between devices: 3.7 us -> 18.5 us  [cross(): return lax.ppermute(x, ALL, pairs)]
    all_to_all x2, waiting for transfers between devices: 0.01 us -> 5.81 us  [spread(): lax.all_to_all(x, ('rr', 'sr'), split_axis=0, concat_axis=0, tiled=True)]
    ppermute x5 -> x6, starting transfers between devices: 6.62 us -> 7.91 us  [cross(): return lax.ppermute(x, ALL, pairs)]
  transfers between devices with their start and end apart: 19 -> 20, of which waited for: 6 -> 8; matrix products, arithmetic and copies ran while one was open for 7% -> 7% of each run, Pallas kernels for 31% -> 24%
where the time goes in v4:
time: 266 us; the launch traced here: 264 us
  Pallas kernels  92.3 us (35%)
  starting transfers between devices  63.9 us (24%)
  waiting for transfers between devices  49.7 us (19%)
  blocking collectives  36.2 us (14%)
  local copies, waits for them, and re-layouts  15 us (6%)
  other arithmetic  5.43 us (2%)
    pallas_call x4, Pallas kernels, inflow_call(): pl.pallas_call(functools.partial(inflow_kernel, len(xs), want_edges), gri...  53.2 us
    ppermute x12, starting transfers between devices, send(): return lax.ppermute(piece, axis, pairs)  40.5 us
    all_to_all x1, blocking collectives, spread(): lax.all_to_all(x, ('rr', 'sr'), split_axis=0, concat_axis=0, tiled=True)  36.2 us
    pallas_call x2, Pallas kernels, step_call(): pl.pallas_call(functools.partial(step_kernel, first_step, want_own, want_...  32.1 us
    ppermute x12, waiting for transfers between devices, send(): return lax.ppermute(piece, axis, pairs)  25.4 us
    ppermute x6, waiting for transfers between devices, cross(): return lax.ppermute(x, ALL, pairs)  18.5 us
    all_to_all x2, starting transfers between devices, spread(): lax.all_to_all(x, ('rr', 'sr'), split_axis=0, concat_axis=0, tiled=True)  15.5 us
    ppermute x6, starting transfers between devices, cross(): return lax.ppermute(x, ALL, pairs)  7.91 us
  transfers between devices with their start and end apart: 20, of which 8 were waited for; matrix products, arithmetic and copies ran while one was open for 7% of the time, Pallas kernels for 24%

profile of v4, /device:TPU:27, one launch (start us, length us, event | category | flops | bytes accessed | tf_op | source)
XLA Modules:
  0.0 264.2 jit_solution(12907707405680324713)
XLA Ops:
  2.5 3.7 %collective-permute-start.2 = (f32[4,32,256]{2,1,0:T(8,128)S(1)}, f32[4,32,256]{2,1,0:T(8,128)S(1)}, u32[]{:S(2)}, u32[]{:S(2)}) collective-permute-start(f32[4,32,256]{2,1,0:T(8,128)S(1)} %bitcast.50), channel_id=1, source_target_pairs={{0,1},{1,2},{2,3},{3,4},{4,5},{5,6},{6,7},{8,9},{9,10},{10,11},{11... | collective-permute-start | bytes 393224 | tf_op jit(solution)/shard_map/ppermute | solution.py:362
  6.2 1.9 collective-permute-start.3
  9.1 5.8 %collective-permute-start.1 = (f32[4,32,256]{2,1,0:T(8,128)S(1)}, f32[4,32,256]{2,1,0:T(8,128)S(1)}, u32[]{:S(2)}, u32[]{:S(2)}) collective-permute-start(f32[4,32,256]{2,1,0:T(8,128)S(1)} %get-tuple-element.141), channel_id=1, source_target_pairs={{8,0},{16,8},{24,16},{32,24},{40,32},{48,40},{56,48},{9,1},{17,9},... | collective-permute-start | bytes 393224 | tf_op jit(solution)/shard_map/ppermute | solution.py:362
  15.0 1.9 collective-permute-start
  17.9 4.9 %collective-permute-done.refs_3_ = f32[4,32,256]{2,1,0:T(8,128)S(1)} collective-permute-done((f32[4,32,256]{2,1,0:T(8,128)S(1)}, f32[4,32,256]{2,1,0:T(8,128)S(1)}, u32[]{:S(2)}, u32[]{:S(2)}) %collective-permute-start) | collective-permute-done | bytes 131104 | tf_op jit(solution)/shard_map/ppermute | solution.py:362
  23.5 18.0 %step_first.1 = (f32[4,32,32,256]{3,2,1,0:T(8,128)}, f32[32,4,8,256]{3,2,1,0:T(8,128)}, f32[32,4,8,256]{3,2,1,0:T(8,128)}, f32[64,4,8,256]{3,2,1,0:T(8,128)}, f3...) custom-call(s32[128]{0:T(128)S(1)} %reshape.17.refs_0_, ...), custom_call_target="tpu_custom_call" | custom-call | flops 1000 | bytes 1000 | tf_op jit(solution)/shard_map/step_first/pallas_call | solution.py:267
  41.5 8.4 %all-to-all-start = ((f32[64,4,8,256]{3,2,1,0:T(8,128)}), f32[64,4,8,256]{3,2,1,0:T(8,128)}, u32[]{:S(2)}, u32[]{:S(2)}) async-start(f32[64,4,8,256]{3,2,1,0:T(8,128)} %get-tuple-element.83), calls=%async_computation | async-start | bytes 4194304 | tf_op jit(solution)/shard_map/all_to_all | solution.py:378
  50.0 3.1 %collective-permute-start.5 = (f32[4,32,256]{2,1,0:T(8,128)S(1)}, f32[4,32,256]{2,1,0:T(8,128)S(1)}, u32[]{:S(2)}, u32[]{:S(2)}) collective-permute-start(f32[4,32,256]{2,1,0:T(8,128)S(1)} %copy-done.22), channel_id=1, source_target_pairs={{0,8},{8,16},{16,24},{24,32},{32,40},{40,48},{48,56},{1,9},{9,17},... | collective-permute-start | bytes 393224 | tf_op jit(solution)/shard_map/ppermute | solution.py:362
  53.2 4.2 %collective-permute-start.6 = (f32[4,32,256]{2,1,0:T(8,128)S(1)}, f32[4,32,256]{2,1,0:T(8,128)S(1)}, u32[]{:S(2)}, u32[]{:S(2)}) collective-permute-start(f32[4,32,256]{2,1,0:T(8,128)S(1)} %copy-done.21), channel_id=1, source_target_pairs={{8,0},{16,8},{24,16},{32,24},{40,32},{48,40},{56,48},{9,1},{17,9},... | collective-permute-start | bytes 393224 | tf_op jit(solution)/shard_map/ppermute | solution.py:362
  57.4 3.9 %collective-permute-start.7 = (f32[4,32,256]{2,1,0:T(8,128)S(1)}, f32[4,32,256]{2,1,0:T(8,128)}, u32[]{:S(2)}, u32[]{:S(2)}) collective-permute-start(f32[4,32,256]{2,1,0:T(8,128)S(1)} %copy-done.20), channel_id=1, source_target_pairs={{0,1},{1,2},{2,3},{3,4},{4,5},{5,6},{6,7},{8,9},{9,10},{10,11},{11... | collective-permute-start | bytes 393224 | tf_op jit(solution)/shard_map/ppermute | solution.py:362
  61.4 1.9 collective-permute-start.8
  64.6 15.0 %collective-permute-done.5 = f32[4,32,256]{2,1,0:T(8,128)S(1)} collective-permute-done((f32[4,32,256]{2,1,0:T(8,128)S(1)}, f32[4,32,256]{2,1,0:T(8,128)S(1)}, u32[]{:S(2)}, u32[]{:S(2)}) %collective-permute-start.5) | collective-permute-done | bytes 131104 | tf_op jit(solution)/shard_map/ppermute | solution.py:362
  80.9 17.7 %conditional.1 = ((f32[64,4,8,256]{3,2,1,0:T(8,128)}, f32[64,4,8,256]{3,2,1,0:T(8,128)}, bf16[1024,1024]{1,0:T(8,128)(2,1)}, bf16[1024,1024]{1,0:T(8,128)(2,1)},...) conditional(s32[]{:T(128)} %convert_element_type.9, (f32[1,1,128,4,8,8]{2,5,4,3,1,0:T(8,128)S(1)}, ...), branch_computations={%region_0.1_spmd, %region_1.2_spmd} | conditional | flops 12582912 | bytes 29491256 | solution.py:427
  82.4 2.4 copy.28.tile_ref
  84.8 3.5 %fusion = (bf16[4,1024,256]{2,0,1:T(4,128)(2,1)S(1)}, bf16[4,1024,256]{2,0,1:T(4,128)(2,1)S(1)}) fusion(f32[4,256,4,256]{3,2,1,0:T(4,128)} %get-tuple-element.119), kind=kLoop, calls=%fused_computation.2 | loop fusion | flops 4194304 | bytes 8388608 | tf_op jit(solution)/shard_map/cond/branch_0_fun/convert_element_type | solution.py:53
  91.6 7.0 %blend_matrix.1 = (bf16[1024,1024]{1,0:T(8,128)(2,1)}, bf16[1024,1024]{1,0:T(8,128)(2,1)}, f32[64,4,8,256]{3,2,1,0:T(8,128)}, f32[64,4,8,256]{3,2,1,0:T(8,128)}) custom-call(s32[512]{0:T(512)S(1)} %bitcast.53, f32[128,4,8,128]{3,2,1,0:T(8,128)S(1)} %copy.28.tile_ref), custom_call_target="tpu_custom_call" | custom-call | flops 8388608 | bytes 6291456 | tf_op jit(solution)/shard_map/cond/branch_0_fun/blend_matrix/pallas_call | solution.py:86
  99.9 13.3 %collective-permute-done.10 = f32[32,4,8,256]{3,2,1,0:T(8,128)} collective-permute-done((f32[32,4,8,256]{3,2,1,0:T(8,128)}, f32[32,4,8,256]{3,2,1,0:T(8,128)}, u32[]{:S(2)}, u32[]{:S(2)}) %collective-permute-start.10) | collective-permute-done | bytes 1048608 | tf_op jit(solution)/shard_map/ppermute | solution.py:374
  113.2 1.9 maximum_select_fusion
  115.2 36.2 %all_to_all.15.refs_1_ = f32[64,4,8,256]{3,2,1,0:T(8,128)} all-to-all(f32[64,4,8,256]{3,2,1,0:T(8,128)S(1)} %maximum_select_fusion), channel_id=1, replica_groups=mesh['sec'=2,'rr'=8,'sr'=8] {'rr','sr'}, dimensions={0} | all-to-all | bytes 4194304 | tf_op jit(solution)/shard_map/all_to_all | solution.py:378
  151.4 7.0 %all-to-all-start.2 = ((f32[64,4,8,256]{3,2,1,0:T(8,128)}), f32[64,4,8,256]{3,2,1,0:T(8,128)}, u32[]{:S(2)}, u32[]{:S(2)}) async-start(f32[64,4,8,256]{3,2,1,0:T(8,128)} %get-tuple-element.105), calls=%async_computation.2 | async-start | bytes 4194304 | tf_op jit(solution)/shard_map/all_to_all | solution.py:378
  159.9 19.8 %inflow_edges.1 = (f32[4,32,32,256]{3,2,1,0:T(8,128)}, f32[4,32,256]{2,1,0:T(8,128)}, f32[4,32,256]{2,1,0:T(8,128)}, f32[4,32,256]{2,1,0:T(8,128)}, f32[4,32,256]{2,1,0:T(8,128)}) custom-call(f32[64,4,8,256]{3,2,1,0:T(8,128)} %collective-permute-done.4.refs_0_, f32[64,4,8,256]{3,2,1,0:T(8,128)} %all_to_all.15.refs_1_, ...), custom_call_target="tpu_custom_call" | custom-call | flops 42949672960 | bytes 1000 | tf_op jit(solution)/shard_map/inflow_edges/pallas_call | solution.py:344
  179.7 5.8 %all-to-all-done.2 = f32[64,4,8,256]{3,2,1,0:T(8,128)} async-done(((f32[64,4,8,256]{3,2,1,0:T(8,128)}), f32[64,4,8,256]{3,2,1,0:T(8,128)}, u32[]{:S(2)}, u32[]{:S(2)}) %all-to-all-start.2) | async-done | bytes 2097184 | tf_op jit(solution)/shard_map/all_to_all | solution.py:378
  185.6 3.3 %fusion.2 = (f32[32,4,8,256]{3,2,1,0:T(8,128)}, f32[32,4,8,256]{3,2,1,0:T(8,128)}) fusion(f32[64,4,8,256]{3,2,1,0:T(8,128)} %all-to-all-done.2), kind=kLoop, calls=%fused_computation.11 | loop fusion | bytes 4194304 | tf_op jit(solution)/shard_map/slice | solution.py:439
  191.4 1.9 collective-permute-start.14
  193.4 5.5 %collective-permute-start.15 = (f32[4,32,256]{2,1,0:T(8,128)}, f32[4,32,256]{2,1,0:T(8,128)S(1)}, u32[]{:S(2)}, u32[]{:S(2)}) collective-permute-start(f32[4,32,256]{2,1,0:T(8,128)} %get-tuple-element.112), channel_id=1, source_target_pairs={{8,0},{16,8},{24,16},{32,24},{40,32},{48,40},{56,48},{9,1},{17,9},... | collective-permute-start | bytes 393224 | tf_op jit(solution)/shard_map/ppermute | solution.py:362
  199.5 4.6 %collective-permute-start.16 = (f32[4,32,256]{2,1,0:T(8,128)}, f32[4,32,256]{2,1,0:T(8,128)S(1)}, u32[]{:S(2)}, u32[]{:S(2)}) collective-permute-start(f32[4,32,256]{2,1,0:T(8,128)} %get-tuple-element.113), channel_id=1, source_target_pairs={{0,1},{1,2},{2,3},{3,4},{4,5},{5,6},{6,7},{8,9},{9,10},{10,11},{11... | collective-permute-start | bytes 393224 | tf_op jit(solution)/shard_map/ppermute | solution.py:362
  206.3 4.7 %collective-permute-done.17.refs_5_ = f32[4,32,256]{2,1,0:T(8,128)S(1)} collective-permute-done((f32[4,32,256]{2,1,0:T(8,128)}, f32[4,32,256]{2,1,0:T(8,128)S(1)}, u32[]{:S(2)}, u32[]{:S(2)}) %collective-permute-start.17) | collective-permute-done | bytes 131104 | tf_op jit(solution)/shard_map/ppermute | solution.py:362
  211.6 14.1 %step_own.1.refs_5_ = f32[4,32,32,256]{3,2,1,0:T(8,128)} custom-call(s32[1]{0:T(128)S(6)} %copy.62.refs_1_.refs_0_, f32[4,32,32,256]{3,2,1,0:T(8,128)} %get-tuple-element.104.refs_1_, f32[4,32,256]{2,1,0:T(8,128)} %copy-done.13, f32[4,32,256]{2,1,0:T(8,128)} %copy-done.14, f32[4,32,256]{2,1,0:T(8,128)} %copy-done.15, f32[4,32,256]{2,1,0:T(8,128)} %copy-done.16, ...), custom_call_target="tpu_custom_call" | custom-call | flops 1000 | bytes 1000 | tf_op jit(solution)/shard_map/step_own/pallas_call | solution.py:267
  225.7 12.2 %inflow.3.refs_5_ = f32[4,32,32,256]{3,2,1,0:T(8,128)} custom-call(f32[64,4,8,256]{3,2,1,0:T(8,128)} %collective-permute-done.13.refs_0_, bf16[4,1024,256]{2,1,0:T(8,128)(2,1)} %get-tuple-element.135.refs_2_.refs_1_, bf16[4,1024,256]{2,1,0:T(8,128)(2,1)S(1)} %copy-done.3, bf16[1024,1024]{1,0:T(8,128)(2,1)} %get-tuple-element.102.refs_4_.refs_3_, ...), custom_call_target="tpu_custom_call" | custom-call | flops 1000 | bytes 1000 | tf_op jit(solution)/shard_map/inflow/pallas_call | solution.py:344
  237.9 10.6 %inflow.4.refs_5_ = f32[4,32,32,256]{3,2,1,0:T(8,128)} custom-call(f32[32,4,8,256]{3,2,1,0:T(8,128)} %collective-permute-done.12.refs_0_, bf16[4,1024,256]{2,1,0:T(8,128)(2,1)S(1)} %copy-done.4, bf16[4,1024,256]{2,1,0:T(8,128)(2,1)S(1)} %copy-done.3, bf16[1024,1024]{1,0:T(8,128)(2,1)S(1)} %copy-done.5, ...), custom_call_target="tpu_custom_call" | custom-call | flops 1000 | bytes 1000 | tf_op jit(solution)/shard_map/inflow/pallas_call | solution.py:344
  248.5 5.1 %collective-permute-done.11.refs_0_ = f32[32,4,8,256]{3,2,1,0:T(8,128)} collective-permute-done((f32[32,4,8,256]{3,2,1,0:T(8,128)}, f32[32,4,8,256]{3,2,1,0:T(8,128)}, u32[]{:S(2)}, u32[]{:S(2)}) %collective-permute-start.11) | collective-permute-done | bytes 1048608 | tf_op jit(solution)/shard_map/ppermute | solution.py:374
  253.7 10.6 %inflow.5 = f32[4,32,32,256]{3,2,1,0:T(8,128)} custom-call(f32[32,4,8,256]{3,2,1,0:T(8,128)} %collective-permute-done.11.refs_0_, bf16[4,1024,256]{2,1,0:T(8,128)(2,1)S(1)} %copy-done.4, bf16[4,1024,256]{2,1,0:T(8,128)(2,1)S(1)} %copy-done.3, bf16[1024,1024]{1,0:T(8,128)(2,1)S(1)} %copy-done.5, bf16[1024,1024]{1,0:T(8,128)(2,1)} %get-tuple-element.103.refs_5_.refs_4_, ...), custom_call_target="tpu_custom_call" | custom-call | flops 1000 | bytes 1000 | tf_op jit(solution)/shard_map/inflow/pallas_call | solution.py:344
  (77 shorter events, 20.1 us)
Async XLA Ops:
  0.6 16.9 %copy-start = (s32[64,64,2]{1,2,0:T(2,128)S(1)}, s32[64,64,2]{1,2,0:T(2,128)}, u32[]{:S(2)}) copy-start(s32[64,64,2]{1,2,0:T(2,128)} %param.23) | copy-start | bytes 98308
  0.6 22.8 %copy-start.6 = (f32[1,32,32,256]{3,2,1,0:T(8,128)S(1)}, f32[1,32,32,256]{3,2,1,0:T(8,128)}, u32[]{:S(2)}) copy-start(f32[1,32,32,256]{3,2,1,0:T(8,128)} %param.16) | copy-start | bytes 3145732
  2.5 15.4 %collective-permute-start.2 = (f32[4,32,256]{2,1,0:T(8,128)S(1)}, f32[4,32,256]{2,1,0:T(8,128)S(1)}, u32[]{:S(2)}, u32[]{:S(2)}) collective-permute-start(f32[4,32,256]{2,1,0:T(8,128)S(1)} %bitcast.50), channel_id=1, source_target_pairs={{0,1},{1,2},{2,3},{3,4},{4,5},{5,6},{6,7},{8,9},{9,10},{10,11},{11... | collective-permute-start | bytes 393224 | tf_op jit(solution)/shard_map/ppermute | solution.py:362
  6.2 11.7 %collective-permute-start.3 = (f32[4,32,256]{2,1,0:T(8,128)S(1)}, f32[4,32,256]{2,1,0:T(8,128)S(1)}, u32[]{:S(2)}, u32[]{:S(2)}) collective-permute-start(f32[4,32,256]{2,1,0:T(8,128)S(1)} %bitcast.51), channel_id=1, source_target_pairs={{1,0},{2,1},{3,2},{4,3},{5,4},{6,5},{7,6},{9,8},{10,9},{11,10},{12... | collective-permute-start | bytes 393224 | tf_op jit(solution)/shard_map/ppermute | solution.py:362
  9.1 8.8 %collective-permute-start.1 = (f32[4,32,256]{2,1,0:T(8,128)S(1)}, f32[4,32,256]{2,1,0:T(8,128)S(1)}, u32[]{:S(2)}, u32[]{:S(2)}) collective-permute-start(f32[4,32,256]{2,1,0:T(8,128)S(1)} %get-tuple-element.141), channel_id=1, source_target_pairs={{8,0},{16,8},{24,16},{32,24},{40,32},{48,40},{56,48},{9,1},{17,9},... | collective-permute-start | bytes 393224 | tf_op jit(solution)/shard_map/ppermute | solution.py:362
  15.0 7.8 %collective-permute-start = (f32[4,32,256]{2,1,0:T(8,128)S(1)}, f32[4,32,256]{2,1,0:T(8,128)S(1)}, u32[]{:S(2)}, u32[]{:S(2)}) collective-permute-start(f32[4,32,256]{2,1,0:T(8,128)S(1)} %get-tuple-element.142), channel_id=1, source_target_pairs={{0,8},{8,16},{16,24},{24,32},{32,40},{40,48},{48,56},{1,9},{9,17},... | collective-permute-start | bytes 393224 | tf_op jit(solution)/shard_map/ppermute | solution.py:362
  41.5 11.7 %copy-start.21 = (f32[4,32,256]{2,1,0:T(8,128)S(1)}, f32[4,32,256]{2,1,0:T(8,128)}, u32[]{:S(2)}) copy-start(f32[4,32,256]{2,1,0:T(8,128)} %get-tuple-element.87) | copy-start | bytes 393220
  41.5 15.9 %copy-start.20 = (f32[4,32,256]{2,1,0:T(8,128)S(1)}, f32[4,32,256]{2,1,0:T(8,128)}, u32[]{:S(2)}) copy-start(f32[4,32,256]{2,1,0:T(8,128)} %get-tuple-element.88) | copy-start | bytes 393220
  41.5 19.9 %copy-start.19 = (f32[4,32,256]{2,1,0:T(8,128)S(1)}, f32[4,32,256]{2,1,0:T(8,128)}, u32[]{:S(2)}) copy-start(f32[4,32,256]{2,1,0:T(8,128)} %get-tuple-element.89) | copy-start | bytes 393220
  41.5 39.4 %copy-start.7 = (f32[1,32,32]{2,1,0:T(8,128)S(1)}, f32[1,32,32]{2,1,0:T(8,128)}, u32[]{:S(2)}) copy-start(f32[1,32,32]{2,1,0:T(8,128)} %param.17) | copy-start | bytes 12292
  41.5 39.4 %copy-start.8 = (f32[32,32]{1,0:T(8,128)S(1)}, f32[32,32]{1,0:T(8,128)}, u32[]{:S(2)}) copy-start(f32[32,32]{1,0:T(8,128)} %refs_9_.1) | copy-start | bytes 12292
  41.5 39.4 %copy-start.17 = (f32[1,1,128,4,8,8]{2,5,4,3,1,0:T(8,128)S(1)}, f32[1,1,128,4,8,8]{2,5,4,3,1,0:T(8,128)}, u32[]{:S(2)}) copy-start(f32[1,1,128,4,8,8]{2,5,4,3,1,0:T(8,128)} %param.25) | copy-start | bytes 393220
  41.5 39.4 %copy-start.18 = (s32[1,1,128,4]{2,3,1,0:T(4,128)S(1)}, s32[1,1,128,4]{2,3,1,0:T(4,128)}, u32[]{:S(2)}) copy-start(s32[1,1,128,4]{2,3,1,0:T(4,128)} %param.24) | copy-start | bytes 6148
  41.5 57.1 %all-to-all-start = ((f32[64,4,8,256]{3,2,1,0:T(8,128)}), f32[64,4,8,256]{3,2,1,0:T(8,128)}, u32[]{:S(2)}, u32[]{:S(2)}) async-start(f32[64,4,8,256]{3,2,1,0:T(8,128)} %get-tuple-element.83), calls=%async_computation | async-start | bytes 4194304 | tf_op jit(solution)/shard_map/all_to_all | solution.py:378
  50.0 29.5 %collective-permute-start.5 = (f32[4,32,256]{2,1,0:T(8,128)S(1)}, f32[4,32,256]{2,1,0:T(8,128)S(1)}, u32[]{:S(2)}, u32[]{:S(2)}) collective-permute-start(f32[4,32,256]{2,1,0:T(8,128)S(1)} %copy-done.22), channel_id=1, source_target_pairs={{0,8},{8,16},{16,24},{24,32},{32,40},{40,48},{48,56},{1,9},{9,17},... | collective-permute-start | bytes 393224 | tf_op jit(solution)/shard_map/ppermute | solution.py:362
  53.2 26.4 %collective-permute-start.6 = (f32[4,32,256]{2,1,0:T(8,128)S(1)}, f32[4,32,256]{2,1,0:T(8,128)S(1)}, u32[]{:S(2)}, u32[]{:S(2)}) collective-permute-start(f32[4,32,256]{2,1,0:T(8,128)S(1)} %copy-done.21), channel_id=1, source_target_pairs={{8,0},{16,8},{24,16},{32,24},{40,32},{48,40},{56,48},{9,1},{17,9},... | collective-permute-start | bytes 393224 | tf_op jit(solution)/shard_map/ppermute | solution.py:362
  57.4 22.1 %collective-permute-start.7 = (f32[4,32,256]{2,1,0:T(8,128)S(1)}, f32[4,32,256]{2,1,0:T(8,128)}, u32[]{:S(2)}, u32[]{:S(2)}) collective-permute-start(f32[4,32,256]{2,1,0:T(8,128)S(1)} %copy-done.20), channel_id=1, source_target_pairs={{0,1},{1,2},{2,3},{3,4},{4,5},{5,6},{6,7},{8,9},{9,10},{10,11},{11... | collective-permute-start | bytes 393224 | tf_op jit(solution)/shard_map/ppermute | solution.py:362
  61.4 18.2 %collective-permute-start.8 = (f32[4,32,256]{2,1,0:T(8,128)S(1)}, f32[4,32,256]{2,1,0:T(8,128)}, u32[]{:S(2)}, u32[]{:S(2)}) collective-permute-start(f32[4,32,256]{2,1,0:T(8,128)S(1)} %copy-done.19), channel_id=1, source_target_pairs={{1,0},{2,1},{3,2},{4,3},{5,4},{6,5},{7,6},{9,8},{10,9},{11,10},{12... | collective-permute-start | bytes 393224 | tf_op jit(solution)/shard_map/ppermute | solution.py:362
  63.3 36.6 %collective-permute-start.9 = (f32[32,4,8,256]{3,2,1,0:T(8,128)}, f32[32,4,8,256]{3,2,1,0:T(8,128)}, u32[]{:S(2)}, u32[]{:S(2)}) collective-permute-start(f32[32,4,8,256]{3,2,1,0:T(8,128)} %get-tuple-element.97), channel_id=1, source_target_pairs={{0,96},{1,97},{2,98},{3,99},{4,100},{5,101},{6,102},{7,103},{8,104... | collective-permute-start | bytes 3145736 | tf_op jit(solution)/shard_map/ppermute | solution.py:374
  79.6 33.7 %collective-permute-start.10 = (f32[32,4,8,256]{3,2,1,0:T(8,128)}, f32[32,4,8,256]{3,2,1,0:T(8,128)}, u32[]{:S(2)}, u32[]{:S(2)}) collective-permute-start(f32[32,4,8,256]{3,2,1,0:T(8,128)} %get-tuple-element.98), channel_id=1, source_target_pairs={{0,96},{1,97},{2,98},{3,99},{4,100},{5,101},{6,102},{7,103},{8,104... | collective-permute-start | bytes 3145736 | tf_op jit(solution)/shard_map/ppermute | solution.py:374
  98.6 61.3 %collective-permute-start.4 = (f32[64,4,8,256]{3,2,1,0:T(8,128)}, f32[64,4,8,256]{3,2,1,0:T(8,128)}, u32[]{:S(2)}, u32[]{:S(2)}) collective-permute-start(f32[64,4,8,256]{3,2,1,0:T(8,128)} %all-to-all-done), channel_id=1, source_target_pairs={{0,96},{1,97},{2,98},{3,99},{4,100},{5,101},{6,102},{7,103},{8,104... | collective-permute-start | bytes 6291464 | tf_op jit(solution)/shard_map/ppermute | solution.py:374
  151.4 34.2 %all-to-all-start.2 = ((f32[64,4,8,256]{3,2,1,0:T(8,128)}), f32[64,4,8,256]{3,2,1,0:T(8,128)}, u32[]{:S(2)}, u32[]{:S(2)}) async-start(f32[64,4,8,256]{3,2,1,0:T(8,128)} %get-tuple-element.105), calls=%async_computation.2 | async-start | bytes 4194304 | tf_op jit(solution)/shard_map/all_to_all | solution.py:378
  158.4 67.2 %collective-permute-start.13 = (f32[64,4,8,256]{3,2,1,0:T(8,128)}, f32[64,4,8,256]{3,2,1,0:T(8,128)}, u32[]{:S(2)}, u32[]{:S(2)}) collective-permute-start(f32[64,4,8,256]{3,2,1,0:T(8,128)} %all_to_all.15.refs_1_), channel_id=1, source_target_pairs={{0,96},{1,97},{2,98},{3,99},{4,100},{5,101},{6,102},{7,103},{8,104... | collective-permute-start | bytes 6291464 | tf_op jit(solution)/shard_map/ppermute | solution.py:374
  185.6 26.1 %copy-start.2 = (f32[1,4,32,32,256]{4,3,2,1,0:T(8,128)S(1)}, f32[1,4,32,32,256]{4,3,2,1,0:T(8,128)}, u32[]{:S(2)}) copy-start(f32[1,4,32,32,256]{4,3,2,1,0:T(8,128)} %param.15) | copy-start | bytes 12582916
  188.8 49.1 %collective-permute-start.12 = (f32[32,4,8,256]{3,2,1,0:T(8,128)}, f32[32,4,8,256]{3,2,1,0:T(8,128)}, u32[]{:S(2)}, u32[]{:S(2)}) collective-permute-start(f32[32,4,8,256]{3,2,1,0:T(8,128)} %get-tuple-element.143), channel_id=1, source_target_pairs={{0,96},{1,97},{2,98},{3,99},{4,100},{5,101},{6,102},{7,103},{8,104... | collective-permute-start | bytes 3145736 | tf_op jit(solution)/shard_map/ppermute | solution.py:374
  190.1 63.5 %collective-permute-start.11 = (f32[32,4,8,256]{3,2,1,0:T(8,128)}, f32[32,4,8,256]{3,2,1,0:T(8,128)}, u32[]{:S(2)}, u32[]{:S(2)}) collective-permute-start(f32[32,4,8,256]{3,2,1,0:T(8,128)} %get-tuple-element.144), channel_id=1, source_target_pairs={{0,96},{1,97},{2,98},{3,99},{4,100},{5,101},{6,102},{7,103},{8,104... | collective-permute-start | bytes 3145736 | tf_op jit(solution)/shard_map/ppermute | solution.py:374
  191.4 8.0 %collective-permute-start.14 = (f32[4,32,256]{2,1,0:T(8,128)}, f32[4,32,256]{2,1,0:T(8,128)S(1)}, u32[]{:S(2)}, u32[]{:S(2)}) collective-permute-start(f32[4,32,256]{2,1,0:T(8,128)} %get-tuple-element.111), channel_id=1, source_target_pairs={{0,8},{8,16},{16,24},{24,32},{32,40},{40,48},{48,56},{1,9},{9,17},... | collective-permute-start | bytes 393224 | tf_op jit(solution)/shard_map/ppermute | solution.py:362
  193.4 10.7 %collective-permute-start.15 = (f32[4,32,256]{2,1,0:T(8,128)}, f32[4,32,256]{2,1,0:T(8,128)S(1)}, u32[]{:S(2)}, u32[]{:S(2)}) collective-permute-start(f32[4,32,256]{2,1,0:T(8,128)} %get-tuple-element.112), channel_id=1, source_target_pairs={{8,0},{16,8},{24,16},{32,24},{40,32},{48,40},{56,48},{9,1},{17,9},... | collective-permute-start | bytes 393224 | tf_op jit(solution)/shard_map/ppermute | solution.py:362
  199.5 6.8 %collective-permute-start.16 = (f32[4,32,256]{2,1,0:T(8,128)}, f32[4,32,256]{2,1,0:T(8,128)S(1)}, u32[]{:S(2)}, u32[]{:S(2)}) collective-permute-start(f32[4,32,256]{2,1,0:T(8,128)} %get-tuple-element.113), channel_id=1, source_target_pairs={{0,1},{1,2},{2,3},{3,4},{4,5},{5,6},{6,7},{8,9},{9,10},{10,11},{11... | collective-permute-start | bytes 393224 | tf_op jit(solution)/shard_map/ppermute | solution.py:362
  204.1 6.9 %collective-permute-start.17 = (f32[4,32,256]{2,1,0:T(8,128)}, f32[4,32,256]{2,1,0:T(8,128)S(1)}, u32[]{:S(2)}, u32[]{:S(2)}) collective-permute-start(f32[4,32,256]{2,1,0:T(8,128)} %get-tuple-element.114), channel_id=1, source_target_pairs={{1,0},{2,1},{3,2},{4,3},{5,4},{6,5},{7,6},{9,8},{10,9},{11,10},{12... | collective-permute-start | bytes 393224 | tf_op jit(solution)/shard_map/ppermute | solution.py:362
  225.7 12.2 %copy-start.4 = (bf16[4,1024,256]{2,1,0:T(8,128)(2,1)S(1)}, bf16[4,1024,256]{2,1,0:T(8,128)(2,1)}, u32[]{:S(2)}) copy-start(bf16[4,1024,256]{2,1,0:T(8,128)(2,1)} %get-tuple-element.135.refs_2_.refs_1_) | copy-start | bytes 6291460
  225.7 12.2 %copy-start.5 = (bf16[1024,1024]{1,0:T(8,128)(2,1)S(1)}, bf16[1024,1024]{1,0:T(8,128)(2,1)}, u32[]{:S(2)}) copy-start(bf16[1024,1024]{1,0:T(8,128)(2,1)} %get-tuple-element.102.refs_4_.refs_3_) | copy-start | bytes 6291460
  (11 other events, 66.8 us)

commit v5 on v4

--- a/solution.py
+++ b/solution.py
@@ -109,8 +109,7 @@
         w_ref = refs.pop(0)
     own_ref = refs.pop(0) if want_own else None
     if want_pack:
-        pack_ones = [refs.pop(0) for _ in range(2 if first_step else 1)]
-        pack_zero = refs.pop(0)
+        pack_one, pack_zero = refs.pop(0), refs.pop(0)
     if first_step:
         top_ref, bottom_ref, left_ref, right_ref, w_ref = refs[:5]
         refs = refs[5:]
@@ -126,10 +125,7 @@
         @pl.when(chunk == 0)
         def _():
             def put(n, w):
-                high, low = split(w)
-                w_ref[n, 0:NA] = high
-                w_ref[n, NA : 2 * NA] = high
-                w_ref[n, 2 * NA : 3 * NA] = low
+                w_ref[n, 0], w_ref[n, 1] = split(w)
 
             for k in range(HEL):
                 put(k, angular[k].T)
@@ -140,17 +136,18 @@
                 put(ABOVE[k], scaled.T)
                 put(BELOW[k], scaled)
 
-    parts = []
+    parts = [split(now[k, pl.ds(first, TI)].reshape(ROWS, NA)) for k in range(HEL)]
+
+    def product(k, n):
+        high, low = parts[k]
+        return dot(high, w_ref[n, 0]) + dot(low, w_ref[n, 0]) + dot(high, w_ref[n, 1])
+
     for k in range(HEL):
-        high, low = split(now[k, pl.ds(first, TI)].reshape(ROWS, NA))
-        parts.append(jnp.concatenate([high, low, high], axis=1))
-    for k in range(HEL):
-        rot[k] = dot(parts[k], w_ref[k])
-    mix[0] = dot(parts[1], w_ref[ABOVE[0]])
+        rot[k] = product(k, k)
+    mix[0] = product(1, ABOVE[0])
     for k in (1, 2):
-        both = jnp.concatenate([parts[k + 1], parts[k - 1]], axis=1)
-        mix[k] = dot(both, w_ref[ABOVE[k] : ABOVE[k] + 2].reshape(6 * NA, NA))
-    mix[3] = dot(parts[2], w_ref[BELOW[2]])
+        mix[k] = product(k + 1, ABOVE[k]) + product(k - 1, BELOW[k - 1])
+    mix[3] = product(2, BELOW[2])
 
     bond = lax.broadcasted_iota(jnp.int32, (CS, NA), 0)
     diagonal = lax.broadcasted_iota(jnp.int32, (CS, CS), 0) == lax.broadcasted_iota(jnp.int32, (CS, CS), 1)
@@ -171,10 +168,10 @@
         line = jnp.broadcast_to(ref[pl.ds(i, 1), :], (CS, CS))
         return jnp.sum(jnp.where(diagonal, line, 0.0), axis=1, keepdims=True)
 
-    def row(t, carry):
+    def row(t):
         i = first + t
         u = factor(jnp.full((CS, NA), radial_start + t, jnp.int32), radial_cells)
-        start = pl.multiple_of(t * CS, CS)
+        start = t * CS
         damp = jnp.broadcast_to(column(damping, i), (CS, NA))
         share = jnp.broadcast_to(column(switch, i) * live, (CS, NA))
         spin = rotor_scale * (u + bond_factor)
@@ -188,8 +185,8 @@
             applied = (
                 (well + u * centre[k]) * v
                 - kinetic * ((before + after) + (lower + upper))
-                + spin * rot[k, pl.ds(start, CS), :]
-                + u * mix[k, pl.ds(start, CS), :]
+                + spin * rot[k, start : start + CS]
+                + u * mix[k, start : start + CS]
             )
             renewed = damp * (2.0 * applied - damp * prev[k, t])
             taken = share * renewed
@@ -197,9 +194,9 @@
                 own_ref[k, t] = renewed - taken
             if want_pack:
                 absorbed[k, i] = taken
-        return carry
-
-    lax.fori_loop(0, TI, row, 0)
+
+    for t in range(TI):
+        row(t)
 
     if first_step:
         for k in range(HEL):
@@ -230,10 +227,7 @@
                 copy(q + half, pack_zero, q)
                 copy(q, pack_zero, q + half)
                 for n in range(2):
-                    if first_step:
-                        copy(SRCS + half * n + q, pack_ones[n], q)
-                    else:
-                        copy(SRCS + half * (1 - n) + q, pack_ones[0], half * n + q)
+                    copy(SRCS + half * (n if first_step else 1 - n) + q, pack_one, half * n + q)
                 return carry
 
             lax.fori_loop(0, SRCS // 2, move, 0)
@@ -242,18 +236,16 @@
 def step_call(first_step, want_own, want_pack, ids, helicity_start, now, halo, prev, pot, damping, switch, *weights, others=()):
     field = (HEL, CR, CS, NA)
     edge = (HEL, CR, NA)
-    stack = (10, 3 * NA, NA)
+    stack = (10, 2, NA, NA)
     rows = pl.BlockSpec((HEL, TI, CS, NA), lambda c: (0, c, 0, 0))
     out_specs, out_shape, scratch = [], [], []
     if want_own:
         out_specs.append(rows)
         out_shape.append(jax.ShapeDtypeStruct(field, F32))
     if want_pack:
-        half = (SRCS // 2, HEL, BLK, NA)
         packed = (SRCS, HEL, BLK, NA)
-        packs = (half, half, packed) if first_step else (packed, packed)
-        out_specs += [whole(n) for n in packs]
-        out_shape += [jax.ShapeDtypeStruct(n, F32) for n in packs]
+        out_specs += [whole(packed)] * 2
+        out_shape += [jax.ShapeDtypeStruct(packed, F32)] * 2
     if first_step:
         out_specs += [whole(edge)] * 4 + [whole(stack)]
         out_shape += [jax.ShapeDtypeStruct(edge, F32)] * 4 + [jax.ShapeDtypeStruct(stack, BF16)]
@@ -401,14 +393,12 @@
 
     fixed = (potential[0], damping[0], switch)
 
-    own_1, one_1, rest_1, zero_1, *rims, weights = step_call(
+    own_1, one_1, zero_1, *rims, weights = step_call(
         True, True, True, ids, helicity_start, current, halo, previous, *fixed, angular[0], coriolis[0]
     )
     crossed_one_1 = cross(one_1)
     halo = exchange(*rims)
     relayed_1 = spread(zero_1)
-    rest_1, halo = lax.optimization_barrier((rest_1, halo))
-    crossed_rest_1 = cross(rest_1)
     pack_shapes = [jax.ShapeDtypeStruct((SRCS, HEL, BLK, NA), F32)] * 2
     blend_shapes = [jax.ShapeDtypeStruct((PTS, PTS), BF16)] * 2
     frame_shapes = [jax.ShapeDtypeStruct((HEL, HEL * NA, NA), BF16)] * 2
@@ -428,8 +418,7 @@
         section == 0, reactant, product, own_1, halo, weights, picks, interp_weights[0, 0], frame_map
     )
     crossed_zero_1 = cross(relayed_1)
-    arrived_1 = jnp.concatenate([crossed_one_1, crossed_rest_1])
-    shared = spread(jnp.where(section == 0, zero_2, arrived_1))
+    shared = spread(jnp.where(section == 0, zero_2, crossed_one_1))
     crossed_zero_2 = cross(shared)
     one_2, shared = lax.optimization_barrier((one_2, shared))
     relayed_2 = spread(one_2)

time: 266 us -> 248 us (0.932)
  waiting for transfers between devices: 49.7 us -> 41.7 us
  Pallas kernels: 92.3 us -> 86 us
    pallas_call x2, Pallas kernels: 32.1 us -> 26 us  [step_call(): pl.pallas_call(functools.partial(step_kernel, first_step, want_own, want_...]
    ppermute x6 -> x5, waiting for transfers between devices: 18.5 us -> 12.8 us  [cross(): return lax.ppermute(x, ALL, pairs)]
    all_to_all x2, waiting for transfers between devices: 5.81 us -> 2.14 us  [spread(): lax.all_to_all(x, ('rr', 'sr'), split_axis=0, concat_axis=0, tiled=True)]
    ppermute x6 -> x5, starting transfers between devices: 7.91 us -> 6.62 us  [cross(): return lax.ppermute(x, ALL, pairs)]
  transfers between devices with their start and end apart: 20 -> 19, of which waited for: 8 -> 8; matrix products, arithmetic and copies ran while one was open for 7% -> 7% of each run, Pallas kernels for 24% -> 25%
where the time goes in v5:
time: 248 us; the launch traced here: 247 us
  Pallas kernels  86 us (35%)
  starting transfers between devices  62.6 us (25%)
  waiting for transfers between devices  41.7 us (17%)
  blocking collectives  34 us (14%)
  local copies, waits for them, and re-layouts  14.9 us (6%)
  other arithmetic  5.55 us (2%)
    pallas_call x4, Pallas kernels, inflow_call(): pl.pallas_call(functools.partial(inflow_kernel, len(xs), want_edges), gri...  53.1 us
    ppermute x12, starting transfers between devices, send(): return lax.ppermute(piece, axis, pairs)  40.5 us
    all_to_all x1, blocking collectives, spread(): lax.all_to_all(x, ('rr', 'sr'), split_axis=0, concat_axis=0, tiled=True)  34 us
    ppermute x12, waiting for transfers between devices, send(): return lax.ppermute(piece, axis, pairs)  26.7 us
    pallas_call x2, Pallas kernels, step_call(): pl.pallas_call(functools.partial(step_kernel, first_step, want_own, want_...  26 us
    all_to_all x2, starting transfers between devices, spread(): lax.all_to_all(x, ('rr', 'sr'), split_axis=0, concat_axis=0, tiled=True)  15.5 us
    ppermute x5, waiting for transfers between devices, cross(): return lax.ppermute(x, ALL, pairs)  12.8 us
    pallas_call x1, Pallas kernels, blend_call(): pl.pallas_call(blend_kernel, in_specs=[smem(), pl.BlockSpec(memory_space=...  6.93 us
  transfers between devices with their start and end apart: 19, of which 8 were waited for; matrix products, arithmetic and copies ran while one was open for 7% of the time, Pallas kernels for 25%

profile of v5, /device:TPU:27, one launch (start us, length us, event | category | flops | bytes accessed | tf_op | source)
XLA Modules:
  0.0 246.5 jit_solution(6448792514933611369)
XLA Ops:
  2.5 3.7 %collective-permute-start.2 = (f32[4,32,256]{2,1,0:T(8,128)S(1)}, f32[4,32,256]{2,1,0:T(8,128)S(1)}, u32[]{:S(2)}, u32[]{:S(2)}) collective-permute-start(f32[4,32,256]{2,1,0:T(8,128)S(1)} %bitcast.50), channel_id=1, source_target_pairs={{0,1},{1,2},{2,3},{3,4},{4,5},{5,6},{6,7},{8,9},{9,10},{10,11},{11... | collective-permute-start | bytes 393224 | tf_op jit(solution)/shard_map/ppermute | solution.py:354
  6.2 1.9 collective-permute-start.3
  9.1 5.8 %collective-permute-start.1 = (f32[4,32,256]{2,1,0:T(8,128)S(1)}, f32[4,32,256]{2,1,0:T(8,128)S(1)}, u32[]{:S(2)}, u32[]{:S(2)}) collective-permute-start(f32[4,32,256]{2,1,0:T(8,128)S(1)} %get-tuple-element.129), channel_id=1, source_target_pairs={{8,0},{16,8},{24,16},{32,24},{40,32},{48,40},{56,48},{9,1},{17,9},... | collective-permute-start | bytes 393224 | tf_op jit(solution)/shard_map/ppermute | solution.py:354
  15.0 1.9 collective-permute-start
  17.9 4.9 %collective-permute-done.refs_3_ = f32[4,32,256]{2,1,0:T(8,128)S(1)} collective-permute-done((f32[4,32,256]{2,1,0:T(8,128)S(1)}, f32[4,32,256]{2,1,0:T(8,128)S(1)}, u32[]{:S(2)}, u32[]{:S(2)}) %collective-permute-start) | collective-permute-done | bytes 131104 | tf_op jit(solution)/shard_map/ppermute | solution.py:354
  23.5 14.9 %step_first.1 = (f32[4,32,32,256]{3,2,1,0:T(8,128)}, f32[64,4,8,256]{3,2,1,0:T(8,128)}, f32[64,4,8,256]{3,2,1,0:T(8,128)}, f32[4,32,256]{2,1,0:T(8,128)}, f32[4,...) custom-call(s32[128]{0:T(128)S(1)} %reshape.17.refs_0_, ...), custom_call_target="tpu_custom_call" | custom-call | flops 1000 | bytes 1000 | tf_op jit(solution)/shard_map/step_first/pallas_call | solution.py:259
  39.8 8.4 %all-to-all-start = ((f32[64,4,8,256]{3,2,1,0:T(8,128)}), f32[64,4,8,256]{3,2,1,0:T(8,128)}, u32[]{:S(2)}, u32[]{:S(2)}) async-start(f32[64,4,8,256]{3,2,1,0:T(8,128)} %get-tuple-element.77), calls=%async_computation | async-start | bytes 4194304 | tf_op jit(solution)/shard_map/all_to_all | solution.py:370
  48.2 3.1 %collective-permute-start.5 = (f32[4,32,256]{2,1,0:T(8,128)S(1)}, f32[4,32,256]{2,1,0:T(8,128)S(1)}, u32[]{:S(2)}, u32[]{:S(2)}) collective-permute-start(f32[4,32,256]{2,1,0:T(8,128)S(1)} %copy-done.22), channel_id=1, source_target_pairs={{0,8},{8,16},{16,24},{24,32},{32,40},{40,48},{48,56},{1,9},{9,17},... | collective-permute-start | bytes 393224 | tf_op jit(solution)/shard_map/ppermute | solution.py:354
  51.4 4.2 %collective-permute-start.6 = (f32[4,32,256]{2,1,0:T(8,128)S(1)}, f32[4,32,256]{2,1,0:T(8,128)S(1)}, u32[]{:S(2)}, u32[]{:S(2)}) collective-permute-start(f32[4,32,256]{2,1,0:T(8,128)S(1)} %copy-done.21), channel_id=1, source_target_pairs={{8,0},{16,8},{24,16},{32,24},{40,32},{48,40},{56,48},{9,1},{17,9},... | collective-permute-start | bytes 393224 | tf_op jit(solution)/shard_map/ppermute | solution.py:354
  55.7 3.9 %collective-permute-start.7 = (f32[4,32,256]{2,1,0:T(8,128)S(1)}, f32[4,32,256]{2,1,0:T(8,128)S(1)}, u32[]{:S(2)}, u32[]{:S(2)}) collective-permute-start(f32[4,32,256]{2,1,0:T(8,128)S(1)} %copy-done.20), channel_id=1, source_target_pairs={{0,1},{1,2},{2,3},{3,4},{4,5},{5,6},{6,7},{8,9},{9,10},{10,11},{11... | collective-permute-start | bytes 393224 | tf_op jit(solution)/shard_map/ppermute | solution.py:354
  59.6 1.9 collective-permute-start.8
  61.5 16.2 %collective-permute-done.5 = f32[4,32,256]{2,1,0:T(8,128)S(1)} collective-permute-done((f32[4,32,256]{2,1,0:T(8,128)S(1)}, f32[4,32,256]{2,1,0:T(8,128)S(1)}, u32[]{:S(2)}, u32[]{:S(2)}) %collective-permute-start.5) | collective-permute-done | bytes 131104 | tf_op jit(solution)/shard_map/ppermute | solution.py:354
  77.8 17.5 %conditional.1 = ((f32[64,4,8,256]{3,2,1,0:T(8,128)}, f32[64,4,8,256]{3,2,1,0:T(8,128)}, bf16[1024,1024]{1,0:T(8,128)(2,1)}, bf16[1024,1024]{1,0:T(8,128)(2,1)},...) conditional(s32[]{:T(128)} %convert_element_type.9, (f32[1,1,128,4,8,8]{2,5,4,3,1,0:T(8,128)S(1)}, ...), branch_computations={%region_0.1_spmd, %region_1.2_spmd} | conditional | flops 12582912 | bytes 29491256 | solution.py:417
  79.3 2.4 copy.28.tile_ref
  81.7 3.5 %fusion = (bf16[4,1024,256]{2,0,1:T(4,128)(2,1)S(1)}, bf16[4,1024,256]{2,0,1:T(4,128)(2,1)S(1)}) fusion(f32[4,256,4,256]{3,2,1,0:T(4,128)} %get-tuple-element.107), kind=kLoop, calls=%fused_computation.2 | loop fusion | flops 4194304 | bytes 8388608 | tf_op jit(solution)/shard_map/cond/branch_0_fun/convert_element_type | solution.py:53
  88.4 6.9 %blend_matrix.1 = (bf16[1024,1024]{1,0:T(8,128)(2,1)}, bf16[1024,1024]{1,0:T(8,128)(2,1)}, f32[64,4,8,256]{3,2,1,0:T(8,128)}, f32[64,4,8,256]{3,2,1,0:T(8,128)}) custom-call(s32[512]{0:T(512)S(1)} %bitcast.53, f32[128,4,8,128]{3,2,1,0:T(8,128)S(1)} %copy.28.tile_ref), custom_call_target="tpu_custom_call" | custom-call | flops 8388608 | bytes 6291456 | tf_op jit(solution)/shard_map/cond/branch_0_fun/blend_matrix/pallas_call | solution.py:86
  96.6 2.1 broadcast_select_fusion
  98.7 34.0 %all_to_all.15.refs_1_ = f32[64,4,8,256]{3,2,1,0:T(8,128)} all-to-all(f32[64,4,8,256]{3,2,1,0:T(8,128)S(1)} %broadcast_select_fusion), channel_id=1, replica_groups=mesh['sec'=2,'rr'=8,'sr'=8] {'rr','sr'}, dimensions={0} | all-to-all | bytes 4194304 | tf_op jit(solution)/shard_map/all_to_all | solution.py:370
  132.7 7.0 %all-to-all-start.2 = ((f32[64,4,8,256]{3,2,1,0:T(8,128)}), f32[64,4,8,256]{3,2,1,0:T(8,128)}, u32[]{:S(2)}, u32[]{:S(2)}) async-start(f32[64,4,8,256]{3,2,1,0:T(8,128)} %get-tuple-element.93), calls=%async_computation.2 | async-start | bytes 4194304 | tf_op jit(solution)/shard_map/all_to_all | solution.py:370
  141.3 3.7 %collective-permute-done.4.refs_0_ = f32[64,4,8,256]{3,2,1,0:T(8,128)} collective-permute-done((f32[64,4,8,256]{3,2,1,0:T(8,128)}, f32[64,4,8,256]{3,2,1,0:T(8,128)}, u32[]{:S(2)}, u32[]{:S(2)}) %collective-permute-start.4) | collective-permute-done | bytes 2097184 | tf_op jit(solution)/shard_map/ppermute | solution.py:366
  145.0 19.8 %inflow_edges.1 = (f32[4,32,32,256]{3,2,1,0:T(8,128)}, f32[4,32,256]{2,1,0:T(8,128)}, f32[4,32,256]{2,1,0:T(8,128)}, f32[4,32,256]{2,1,0:T(8,128)}, f32[4,32,256]{2,1,0:T(8,128)}) custom-call(f32[64,4,8,256]{3,2,1,0:T(8,128)} %collective-permute-done.4.refs_0_, f32[64,4,8,256]{3,2,1,0:T(8,128)} %all_to_all.15.refs_1_, ...), custom_call_target="tpu_custom_call" | custom-call | flops 42949672960 | bytes 1000 | tf_op jit(solution)/shard_map/inflow_edges/pallas_call | solution.py:336
  164.8 2.1 all-to-all-done.2
  166.9 3.3 %fusion.2 = (f32[32,4,8,256]{3,2,1,0:T(8,128)}, f32[32,4,8,256]{3,2,1,0:T(8,128)}) fusion(f32[64,4,8,256]{3,2,1,0:T(8,128)} %all-to-all-done.2), kind=kLoop, calls=%fused_computation.11 | loop fusion | bytes 4194304 | tf_op jit(solution)/shard_map/slice | solution.py:428
  172.8 1.9 collective-permute-start.13
  174.7 5.5 %collective-permute-start.14 = (f32[4,32,256]{2,1,0:T(8,128)}, f32[4,32,256]{2,1,0:T(8,128)S(1)}, u32[]{:S(2)}, u32[]{:S(2)}) collective-permute-start(f32[4,32,256]{2,1,0:T(8,128)} %get-tuple-element.100), channel_id=1, source_target_pairs={{8,0},{16,8},{24,16},{32,24},{40,32},{48,40},{56,48},{9,1},{17,9},... | collective-permute-start | bytes 393224 | tf_op jit(solution)/shard_map/ppermute | solution.py:354
  180.8 4.6 %collective-permute-start.15 = (f32[4,32,256]{2,1,0:T(8,128)}, f32[4,32,256]{2,1,0:T(8,128)S(1)}, u32[]{:S(2)}, u32[]{:S(2)}) collective-permute-start(f32[4,32,256]{2,1,0:T(8,128)} %get-tuple-element.101), channel_id=1, source_target_pairs={{0,1},{1,2},{2,3},{3,4},{4,5},{5,6},{6,7},{8,9},{9,10},{10,11},{11... | collective-permute-start | bytes 393224 | tf_op jit(solution)/shard_map/ppermute | solution.py:354
  187.6 4.7 %collective-permute-done.16.refs_5_ = f32[4,32,256]{2,1,0:T(8,128)S(1)} collective-permute-done((f32[4,32,256]{2,1,0:T(8,128)}, f32[4,32,256]{2,1,0:T(8,128)S(1)}, u32[]{:S(2)}, u32[]{:S(2)}) %collective-permute-start.16) | collective-permute-done | bytes 131104 | tf_op jit(solution)/shard_map/ppermute | solution.py:354
  193.0 11.1 %step_own.1.refs_5_ = f32[4,32,32,256]{3,2,1,0:T(8,128)} custom-call(s32[1]{0:T(128)S(6)} %copy.62.refs_1_.refs_0_, f32[4,32,32,256]{3,2,1,0:T(8,128)} %get-tuple-element.92.refs_1_, f32[4,32,256]{2,1,0:T(8,128)} %copy-done.13, f32[4,32,256]{2,1,0:T(8,128)} %copy-done.14, f32[4,32,256]{2,1,0:T(8,128)} %copy-done.15, f32[4,32,256]{2,1,0:T(8,128)} %copy-done.16, ...), custom_call_target="tpu_custom_call" | custom-call | flops 1000 | bytes 1000 | tf_op jit(solution)/shard_map/step_own/pallas_call | solution.py:259
  204.0 12.1 %inflow.3.refs_5_ = f32[4,32,32,256]{3,2,1,0:T(8,128)} custom-call(f32[64,4,8,256]{3,2,1,0:T(8,128)} %collective-permute-done.12.refs_0_, bf16[4,1024,256]{2,1,0:T(8,128)(2,1)} %get-tuple-element.123.refs_2_.refs_1_, bf16[4,1024,256]{2,1,0:T(8,128)(2,1)S(1)} %copy-done.3, bf16[1024,1024]{1,0:T(8,128)(2,1)} %get-tuple-element.90.refs_4_.refs_3_, ...), custom_call_target="tpu_custom_call" | custom-call | flops 1000 | bytes 1000 | tf_op jit(solution)/shard_map/inflow/pallas_call | solution.py:336
  216.2 10.7 %inflow.4.refs_5_ = f32[4,32,32,256]{3,2,1,0:T(8,128)} custom-call(f32[32,4,8,256]{3,2,1,0:T(8,128)} %collective-permute-done.11.refs_0_, bf16[4,1024,256]{2,1,0:T(8,128)(2,1)S(1)} %copy-done.4, bf16[4,1024,256]{2,1,0:T(8,128)(2,1)S(1)} %copy-done.3, bf16[1024,1024]{1,0:T(8,128)(2,1)S(1)} %copy-done.5, bf16[1024,1024]{1,0:T(8,128)(2,1)} %get-tuple-element.91.refs_5_.refs_4_, ...), custom_call_target="tpu_custom_call" | custom-call | flops 1000 | bytes 1000 | tf_op jit(solution)/shard_map/inflow/pallas_call | solution.py:336
  226.8 9.1 %collective-permute-done.10.refs_0_ = f32[32,4,8,256]{3,2,1,0:T(8,128)} collective-permute-done((f32[32,4,8,256]{3,2,1,0:T(8,128)}, f32[32,4,8,256]{3,2,1,0:T(8,128)}, u32[]{:S(2)}, u32[]{:S(2)}) %collective-permute-start.10) | collective-permute-done | bytes 1048608 | tf_op jit(solution)/shard_map/ppermute | solution.py:366
  235.9 10.6 %inflow.5 = f32[4,32,32,256]{3,2,1,0:T(8,128)} custom-call(f32[32,4,8,256]{3,2,1,0:T(8,128)} %collective-permute-done.10.refs_0_, bf16[4,1024,256]{2,1,0:T(8,128)(2,1)S(1)} %copy-done.4, bf16[4,1024,256]{2,1,0:T(8,128)(2,1)S(1)} %copy-done.3, bf16[1024,1024]{1,0:T(8,128)(2,1)S(1)} %copy-done.5, bf16[1024,1024]{1,0:T(8,128)(2,1)} %get-tuple-element.91.refs_5_.refs_4_, ...), custom_call_target="tpu_custom_call" | custom-call | flops 1000 | bytes 1000 | tf_op jit(solution)/shard_map/inflow/pallas_call | solution.py:336
  (75 shorter events, 18.7 us)
Async XLA Ops:
  0.6 16.9 %copy-start = (s32[64,64,2]{1,2,0:T(2,128)S(1)}, s32[64,64,2]{1,2,0:T(2,128)}, u32[]{:S(2)}) copy-start(s32[64,64,2]{1,2,0:T(2,128)} %param.23) | copy-start | bytes 98308
  0.6 22.8 %copy-start.6 = (f32[1,32,32,256]{3,2,1,0:T(8,128)S(1)}, f32[1,32,32,256]{3,2,1,0:T(8,128)}, u32[]{:S(2)}) copy-start(f32[1,32,32,256]{3,2,1,0:T(8,128)} %param.16) | copy-start | bytes 3145732
  2.5 15.4 %collective-permute-start.2 = (f32[4,32,256]{2,1,0:T(8,128)S(1)}, f32[4,32,256]{2,1,0:T(8,128)S(1)}, u32[]{:S(2)}, u32[]{:S(2)}) collective-permute-start(f32[4,32,256]{2,1,0:T(8,128)S(1)} %bitcast.50), channel_id=1, source_target_pairs={{0,1},{1,2},{2,3},{3,4},{4,5},{5,6},{6,7},{8,9},{9,10},{10,11},{11... | collective-permute-start | bytes 393224 | tf_op jit(solution)/shard_map/ppermute | solution.py:354
  6.2 11.7 %collective-permute-start.3 = (f32[4,32,256]{2,1,0:T(8,128)S(1)}, f32[4,32,256]{2,1,0:T(8,128)S(1)}, u32[]{:S(2)}, u32[]{:S(2)}) collective-permute-start(f32[4,32,256]{2,1,0:T(8,128)S(1)} %bitcast.51), channel_id=1, source_target_pairs={{1,0},{2,1},{3,2},{4,3},{5,4},{6,5},{7,6},{9,8},{10,9},{11,10},{12... | collective-permute-start | bytes 393224 | tf_op jit(solution)/shard_map/ppermute | solution.py:354
  9.1 8.8 %collective-permute-start.1 = (f32[4,32,256]{2,1,0:T(8,128)S(1)}, f32[4,32,256]{2,1,0:T(8,128)S(1)}, u32[]{:S(2)}, u32[]{:S(2)}) collective-permute-start(f32[4,32,256]{2,1,0:T(8,128)S(1)} %get-tuple-element.129), channel_id=1, source_target_pairs={{8,0},{16,8},{24,16},{32,24},{40,32},{48,40},{56,48},{9,1},{17,9},... | collective-permute-start | bytes 393224 | tf_op jit(solution)/shard_map/ppermute | solution.py:354
  15.0 7.8 %collective-permute-start = (f32[4,32,256]{2,1,0:T(8,128)S(1)}, f32[4,32,256]{2,1,0:T(8,128)S(1)}, u32[]{:S(2)}, u32[]{:S(2)}) collective-permute-start(f32[4,32,256]{2,1,0:T(8,128)S(1)} %get-tuple-element.130), channel_id=1, source_target_pairs={{0,8},{8,16},{16,24},{24,32},{32,40},{40,48},{48,56},{1,9},{9,17},... | collective-permute-start | bytes 393224 | tf_op jit(solution)/shard_map/ppermute | solution.py:354
  38.4 58.3 %collective-permute-start.9 = (f32[64,4,8,256]{3,2,1,0:T(8,128)}, f32[64,4,8,256]{3,2,1,0:T(8,128)}, u32[]{:S(2)}, u32[]{:S(2)}) collective-permute-start(f32[64,4,8,256]{3,2,1,0:T(8,128)} %get-tuple-element.86), channel_id=1, source_target_pairs={{0,96},{1,97},{2,98},{3,99},{4,100},{5,101},{6,102},{7,103},{8,104... | collective-permute-start | bytes 6291464 | tf_op jit(solution)/shard_map/ppermute | solution.py:366
  39.7 11.7 %copy-start.21 = (f32[4,32,256]{2,1,0:T(8,128)S(1)}, f32[4,32,256]{2,1,0:T(8,128)}, u32[]{:S(2)}) copy-start(f32[4,32,256]{2,1,0:T(8,128)} %get-tuple-element.80) | copy-start | bytes 393220
  39.7 15.9 %copy-start.20 = (f32[4,32,256]{2,1,0:T(8,128)S(1)}, f32[4,32,256]{2,1,0:T(8,128)}, u32[]{:S(2)}) copy-start(f32[4,32,256]{2,1,0:T(8,128)} %get-tuple-element.81) | copy-start | bytes 393220
  39.7 19.9 %copy-start.19 = (f32[4,32,256]{2,1,0:T(8,128)S(1)}, f32[4,32,256]{2,1,0:T(8,128)}, u32[]{:S(2)}) copy-start(f32[4,32,256]{2,1,0:T(8,128)} %get-tuple-element.82) | copy-start | bytes 393220
  39.7 38.1 %copy-start.7 = (f32[1,32,32]{2,1,0:T(8,128)S(1)}, f32[1,32,32]{2,1,0:T(8,128)}, u32[]{:S(2)}) copy-start(f32[1,32,32]{2,1,0:T(8,128)} %param.17) | copy-start | bytes 12292
  39.7 38.1 %copy-start.8 = (f32[32,32]{1,0:T(8,128)S(1)}, f32[32,32]{1,0:T(8,128)}, u32[]{:S(2)}) copy-start(f32[32,32]{1,0:T(8,128)} %refs_9_.1) | copy-start | bytes 12292
  39.7 38.1 %copy-start.17 = (f32[1,1,128,4,8,8]{2,5,4,3,1,0:T(8,128)S(1)}, f32[1,1,128,4,8,8]{2,5,4,3,1,0:T(8,128)}, u32[]{:S(2)}) copy-start(f32[1,1,128,4,8,8]{2,5,4,3,1,0:T(8,128)} %param.25) | copy-start | bytes 393220
  39.8 38.1 %copy-start.18 = (s32[1,1,128,4]{2,3,1,0:T(4,128)S(1)}, s32[1,1,128,4]{2,3,1,0:T(4,128)}, u32[]{:S(2)}) copy-start(s32[1,1,128,4]{2,3,1,0:T(4,128)} %param.24) | copy-start | bytes 6148
  39.8 55.6 %all-to-all-start = ((f32[64,4,8,256]{3,2,1,0:T(8,128)}), f32[64,4,8,256]{3,2,1,0:T(8,128)}, u32[]{:S(2)}, u32[]{:S(2)}) async-start(f32[64,4,8,256]{3,2,1,0:T(8,128)} %get-tuple-element.77), calls=%async_computation | async-start | bytes 4194304 | tf_op jit(solution)/shard_map/all_to_all | solution.py:370
  48.2 29.5 %collective-permute-start.5 = (f32[4,32,256]{2,1,0:T(8,128)S(1)}, f32[4,32,256]{2,1,0:T(8,128)S(1)}, u32[]{:S(2)}, u32[]{:S(2)}) collective-permute-start(f32[4,32,256]{2,1,0:T(8,128)S(1)} %copy-done.22), channel_id=1, source_target_pairs={{0,8},{8,16},{16,24},{24,32},{32,40},{40,48},{48,56},{1,9},{9,17},... | collective-permute-start | bytes 393224 | tf_op jit(solution)/shard_map/ppermute | solution.py:354
  51.4 26.4 %collective-permute-start.6 = (f32[4,32,256]{2,1,0:T(8,128)S(1)}, f32[4,32,256]{2,1,0:T(8,128)S(1)}, u32[]{:S(2)}, u32[]{:S(2)}) collective-permute-start(f32[4,32,256]{2,1,0:T(8,128)S(1)} %copy-done.21), channel_id=1, source_target_pairs={{8,0},{16,8},{24,16},{32,24},{40,32},{48,40},{56,48},{9,1},{17,9},... | collective-permute-start | bytes 393224 | tf_op jit(solution)/shard_map/ppermute | solution.py:354
  55.7 22.1 %collective-permute-start.7 = (f32[4,32,256]{2,1,0:T(8,128)S(1)}, f32[4,32,256]{2,1,0:T(8,128)S(1)}, u32[]{:S(2)}, u32[]{:S(2)}) collective-permute-start(f32[4,32,256]{2,1,0:T(8,128)S(1)} %copy-done.20), channel_id=1, source_target_pairs={{0,1},{1,2},{2,3},{3,4},{4,5},{5,6},{6,7},{8,9},{9,10},{10,11},{11... | collective-permute-start | bytes 393224 | tf_op jit(solution)/shard_map/ppermute | solution.py:354
  59.6 18.2 %collective-permute-start.8 = (f32[4,32,256]{2,1,0:T(8,128)S(1)}, f32[4,32,256]{2,1,0:T(8,128)S(1)}, u32[]{:S(2)}, u32[]{:S(2)}) collective-permute-start(f32[4,32,256]{2,1,0:T(8,128)S(1)} %copy-done.19), channel_id=1, source_target_pairs={{1,0},{2,1},{3,2},{4,3},{5,4},{6,5},{7,6},{9,8},{10,9},{11,10},{12... | collective-permute-start | bytes 393224 | tf_op jit(solution)/shard_map/ppermute | solution.py:354
  95.3 49.6 %collective-permute-start.4 = (f32[64,4,8,256]{3,2,1,0:T(8,128)}, f32[64,4,8,256]{3,2,1,0:T(8,128)}, u32[]{:S(2)}, u32[]{:S(2)}) collective-permute-start(f32[64,4,8,256]{3,2,1,0:T(8,128)} %all-to-all-done), channel_id=1, source_target_pairs={{0,96},{1,97},{2,98},{3,99},{4,100},{5,101},{6,102},{7,103},{8,104... | collective-permute-start | bytes 6291464 | tf_op jit(solution)/shard_map/ppermute | solution.py:366
  132.7 12.2 %copy-start.3 = (bf16[4,1024,256]{2,1,0:T(8,128)(2,1)S(1)}, bf16[4,1024,256]{2,1,0:T(8,128)(2,1)}, u32[]{:S(2)}) copy-start(bf16[4,1024,256]{2,1,0:T(8,128)(2,1)} %get-tuple-element.124.refs_3_.refs_2_) | copy-start | bytes 6291460
  132.7 34.2 %all-to-all-start.2 = ((f32[64,4,8,256]{3,2,1,0:T(8,128)}), f32[64,4,8,256]{3,2,1,0:T(8,128)}, u32[]{:S(2)}, u32[]{:S(2)}) async-start(f32[64,4,8,256]{3,2,1,0:T(8,128)} %get-tuple-element.93), calls=%async_computation.2 | async-start | bytes 4194304 | tf_op jit(solution)/shard_map/all_to_all | solution.py:370
  139.8 64.3 %collective-permute-start.12 = (f32[64,4,8,256]{3,2,1,0:T(8,128)}, f32[64,4,8,256]{3,2,1,0:T(8,128)}, u32[]{:S(2)}, u32[]{:S(2)}) collective-permute-start(f32[64,4,8,256]{3,2,1,0:T(8,128)} %all_to_all.15.refs_1_), channel_id=1, source_target_pairs={{0,96},{1,97},{2,98},{3,99},{4,100},{5,101},{6,102},{7,103},{8,104... | collective-permute-start | bytes 6291464 | tf_op jit(solution)/shard_map/ppermute | solution.py:366
  166.9 26.1 %copy-start.2 = (f32[1,4,32,32,256]{4,3,2,1,0:T(8,128)S(1)}, f32[1,4,32,32,256]{4,3,2,1,0:T(8,128)}, u32[]{:S(2)}) copy-start(f32[1,4,32,32,256]{4,3,2,1,0:T(8,128)} %param.15) | copy-start | bytes 12582916
  170.2 45.9 %collective-permute-start.11 = (f32[32,4,8,256]{3,2,1,0:T(8,128)}, f32[32,4,8,256]{3,2,1,0:T(8,128)}, u32[]{:S(2)}, u32[]{:S(2)}) collective-permute-start(f32[32,4,8,256]{3,2,1,0:T(8,128)} %get-tuple-element.131), channel_id=1, source_target_pairs={{0,96},{1,97},{2,98},{3,99},{4,100},{5,101},{6,102},{7,103},{8,104... | collective-permute-start | bytes 3145736 | tf_op jit(solution)/shard_map/ppermute | solution.py:366
  171.5 64.4 %collective-permute-start.10 = (f32[32,4,8,256]{3,2,1,0:T(8,128)}, f32[32,4,8,256]{3,2,1,0:T(8,128)}, u32[]{:S(2)}, u32[]{:S(2)}) collective-permute-start(f32[32,4,8,256]{3,2,1,0:T(8,128)} %get-tuple-element.132), channel_id=1, source_target_pairs={{0,96},{1,97},{2,98},{3,99},{4,100},{5,101},{6,102},{7,103},{8,104... | collective-permute-start | bytes 3145736 | tf_op jit(solution)/shard_map/ppermute | solution.py:366
  172.8 8.0 %collective-permute-start.13 = (f32[4,32,256]{2,1,0:T(8,128)}, f32[4,32,256]{2,1,0:T(8,128)S(1)}, u32[]{:S(2)}, u32[]{:S(2)}) collective-permute-start(f32[4,32,256]{2,1,0:T(8,128)} %get-tuple-element.99), channel_id=1, source_target_pairs={{0,8},{8,16},{16,24},{24,32},{32,40},{40,48},{48,56},{1,9},{9,17},... | collective-permute-start | bytes 393224 | tf_op jit(solution)/shard_map/ppermute | solution.py:354
  174.7 10.7 %collective-permute-start.14 = (f32[4,32,256]{2,1,0:T(8,128)}, f32[4,32,256]{2,1,0:T(8,128)S(1)}, u32[]{:S(2)}, u32[]{:S(2)}) collective-permute-start(f32[4,32,256]{2,1,0:T(8,128)} %get-tuple-element.100), channel_id=1, source_target_pairs={{8,0},{16,8},{24,16},{32,24},{40,32},{48,40},{56,48},{9,1},{17,9},... | collective-permute-start | bytes 393224 | tf_op jit(solution)/shard_map/ppermute | solution.py:354
  180.8 6.8 %collective-permute-start.15 = (f32[4,32,256]{2,1,0:T(8,128)}, f32[4,32,256]{2,1,0:T(8,128)S(1)}, u32[]{:S(2)}, u32[]{:S(2)}) collective-permute-start(f32[4,32,256]{2,1,0:T(8,128)} %get-tuple-element.101), channel_id=1, source_target_pairs={{0,1},{1,2},{2,3},{3,4},{4,5},{5,6},{6,7},{8,9},{9,10},{10,11},{11... | collective-permute-start | bytes 393224 | tf_op jit(solution)/shard_map/ppermute | solution.py:354
  185.4 6.9 %collective-permute-start.16 = (f32[4,32,256]{2,1,0:T(8,128)}, f32[4,32,256]{2,1,0:T(8,128)S(1)}, u32[]{:S(2)}, u32[]{:S(2)}) collective-permute-start(f32[4,32,256]{2,1,0:T(8,128)} %get-tuple-element.102), channel_id=1, source_target_pairs={{1,0},{2,1},{3,2},{4,3},{5,4},{6,5},{7,6},{9,8},{10,9},{11,10},{12... | collective-permute-start | bytes 393224 | tf_op jit(solution)/shard_map/ppermute | solution.py:354
  204.0 12.1 %copy-start.4 = (bf16[4,1024,256]{2,1,0:T(8,128)(2,1)S(1)}, bf16[4,1024,256]{2,1,0:T(8,128)(2,1)}, u32[]{:S(2)}) copy-start(bf16[4,1024,256]{2,1,0:T(8,128)(2,1)} %get-tuple-element.123.refs_2_.refs_1_) | copy-start | bytes 6291460
  204.0 12.1 %copy-start.5 = (bf16[1024,1024]{1,0:T(8,128)(2,1)S(1)}, bf16[1024,1024]{1,0:T(8,128)(2,1)}, u32[]{:S(2)}) copy-start(bf16[1024,1024]{1,0:T(8,128)(2,1)} %get-tuple-element.90.refs_4_.refs_3_) | copy-start | bytes 6291460
  (10 other events, 58.3 us)

commit v6 on v5

--- a/solution.py
+++ b/solution.py
@@ -101,8 +101,8 @@
 def step_kernel(first_step, want_own, want_pack, *refs):
     refs = list(refs)
     ids = refs.pop(0) if want_pack else None
-    start_ref, now, up, down, left, right, prev, pot, damping, switch = refs[:10]
-    refs = refs[10:]
+    start_ref, now, above, below, up, down, left, right, prev, pot, damping, switch = refs[:12]
+    refs = refs[12:]
     if first_step:
         angular, coriolis = refs.pop(0), refs.pop(0)
     else:
@@ -136,7 +136,7 @@
                 put(ABOVE[k], scaled.T)
                 put(BELOW[k], scaled)
 
-    parts = [split(now[k, pl.ds(first, TI)].reshape(ROWS, NA)) for k in range(HEL)]
+    parts = [split(now[k].reshape(ROWS, NA)) for k in range(HEL)]
 
     def product(k, n):
         high, low = parts[k]
@@ -177,9 +177,9 @@
         spin = rotor_scale * (u + bond_factor)
         well = pot[t] + 4.0 * kinetic
         for k in range(HEL):
-            v = now[k, i]
-            before = jnp.where(i == 0, up[k], now[k, jnp.maximum(i - 1, 0)])
-            after = jnp.where(i == CR - 1, down[k], now[k, jnp.minimum(i + 1, CR - 1)])
+            v = now[k, t]
+            before = now[k, t - 1] if t > 0 else jnp.where(chunk == 0, up[k], above[k, 0])
+            after = now[k, t + 1] if t < TI - 1 else jnp.where(chunk == CR // TI - 1, down[k], below[k, 0])
             lower = jnp.where(bond == 0, left[k, pl.ds(i, 1), :], pltpu.roll(v, 1, 0))
             upper = jnp.where(bond == CS - 1, right[k, pl.ds(i, 1), :], pltpu.roll(v, CS - 1, 0))
             applied = (
@@ -262,7 +262,9 @@
         in_specs=([smem()] if want_pack else [])
         + [
             smem(),
-            whole(field),
+            rows,
+            pl.BlockSpec((HEL, 1, CS, NA), lambda c: (0, jnp.maximum(c * TI - 1, 0), 0, 0)),
+            pl.BlockSpec((HEL, 1, CS, NA), lambda c: (0, jnp.minimum(c * TI + TI, CR - 1), 0, 0)),
             whole(edge),
             whole(edge),
             whole(edge),
@@ -279,7 +281,7 @@
         compiler_params=pltpu.CompilerParams(vmem_limit_bytes=56 * MIB),
         cost_estimate=pl.CostEstimate(flops=1000, transcendentals=0, bytes_accessed=1000),
         name="step_first" if first_step else "step_own" if want_own else "step_pack",
-    )(*((ids,) if want_pack else ()), helicity_start, now, *halo, prev, pot, damping, switch, *weights)
+    )(*((ids,) if want_pack else ()), helicity_start, now, now, now, *halo, prev, pot, damping, switch, *weights)
 
 
 def inflow_kernel(count, want_edges, *refs):

time: 248 us -> 247 us (level)
  transfers between devices with their start and end apart: 19 -> 19, of which waited for: 8 -> 8; matrix products, arithmetic and copies ran while one was open for 7% -> 7% of each run, Pallas kernels for 25% -> 24%
where the time goes in v6:
time: 247 us; the launch traced here: 246 us
  Pallas kernels  83.9 us (34%)
  starting transfers between devices  62.6 us (25%)
  waiting for transfers between devices  43 us (17%)
  blocking collectives  34 us (14%)
  local copies, waits for them, and re-layouts  14.9 us (6%)
  other arithmetic  5.55 us (2%)
    pallas_call x4, Pallas kernels, inflow_call(): pl.pallas_call(functools.partial(inflow_kernel, len(xs), want_edges), gri...  53.1 us
    ppermute x12, starting transfers between devices, send(): return lax.ppermute(piece, axis, pairs)  40.5 us
    all_to_all x1, blocking collectives, spread(): lax.all_to_all(x, ('rr', 'sr'), split_axis=0, concat_axis=0, tiled=True)  34 us
    ppermute x12, waiting for transfers between devices, send(): return lax.ppermute(piece, axis, pairs)  26.7 us
    pallas_call x2, Pallas kernels, step_call(): pl.pallas_call(functools.partial(step_kernel, first_step, want_own, want_...  23.9 us
    all_to_all x2, starting transfers between devices, spread(): lax.all_to_all(x, ('rr', 'sr'), split_axis=0, concat_axis=0, tiled=True)  15.5 us
    ppermute x5, waiting for transfers between devices, cross(): return lax.ppermute(x, ALL, pairs)  14.1 us
    pallas_call x1, Pallas kernels, blend_call(): pl.pallas_call(blend_kernel, in_specs=[smem(), pl.BlockSpec(memory_space=...  6.93 us
  transfers between devices with their start and end apart: 19, of which 8 were waited for; matrix products, arithmetic and copies ran while one was open for 7% of the time, Pallas kernels for 24%

profile of v6, /device:TPU:27, one launch (start us, length us, event | category | flops | bytes accessed | tf_op | source)
XLA Modules:
  0.0 245.7 jit_solution(11818339137679559124)
XLA Ops:
  2.5 3.7 %collective-permute-start.2 = (f32[4,32,256]{2,1,0:T(8,128)S(1)}, f32[4,32,256]{2,1,0:T(8,128)S(1)}, u32[]{:S(2)}, u32[]{:S(2)}) collective-permute-start(f32[4,32,256]{2,1,0:T(8,128)S(1)} %bitcast.52), channel_id=1, source_target_pairs={{0,1},{1,2},{2,3},{3,4},{4,5},{5,6},{6,7},{8,9},{9,10},{10,11},{11... | collective-permute-start | bytes 393224 | tf_op jit(solution)/shard_map/ppermute | solution.py:356
  6.2 1.9 collective-permute-start.3
  9.1 5.8 %collective-permute-start.1 = (f32[4,32,256]{2,1,0:T(8,128)S(1)}, f32[4,32,256]{2,1,0:T(8,128)S(1)}, u32[]{:S(2)}, u32[]{:S(2)}) collective-permute-start(f32[4,32,256]{2,1,0:T(8,128)S(1)} %get-tuple-element.129), channel_id=1, source_target_pairs={{8,0},{16,8},{24,16},{32,24},{40,32},{48,40},{56,48},{9,1},{17,9},... | collective-permute-start | bytes 393224 | tf_op jit(solution)/shard_map/ppermute | solution.py:356
  15.0 1.9 collective-permute-start
  17.9 4.9 %collective-permute-done.refs_5_ = f32[4,32,256]{2,1,0:T(8,128)S(1)} collective-permute-done((f32[4,32,256]{2,1,0:T(8,128)S(1)}, f32[4,32,256]{2,1,0:T(8,128)S(1)}, u32[]{:S(2)}, u32[]{:S(2)}) %collective-permute-start) | collective-permute-done | bytes 131104 | tf_op jit(solution)/shard_map/ppermute | solution.py:356
  23.5 14.1 %step_first.1 = (f32[4,32,32,256]{3,2,1,0:T(8,128)}, f32[64,4,8,256]{3,2,1,0:T(8,128)}, f32[64,4,8,256]{3,2,1,0:T(8,128)}, f32[4,32,256]{2,1,0:T(8,128)}, f32[4,...) custom-call(s32[128]{0:T(128)S(1)} %reshape.17.refs_0_, ...), custom_call_target="tpu_custom_call" | custom-call | flops 1000 | bytes 1000 | tf_op jit(solution)/shard_map/step_first/pallas_call | solution.py:259
  39.0 8.4 %all-to-all-start = ((f32[64,4,8,256]{3,2,1,0:T(8,128)}), f32[64,4,8,256]{3,2,1,0:T(8,128)}, u32[]{:S(2)}, u32[]{:S(2)}) async-start(f32[64,4,8,256]{3,2,1,0:T(8,128)} %get-tuple-element.77), calls=%async_computation | async-start | bytes 4194304 | tf_op jit(solution)/shard_map/all_to_all | solution.py:372
  47.4 3.1 %collective-permute-start.5 = (f32[4,32,256]{2,1,0:T(8,128)S(1)}, f32[4,32,256]{2,1,0:T(8,128)S(1)}, u32[]{:S(2)}, u32[]{:S(2)}) collective-permute-start(f32[4,32,256]{2,1,0:T(8,128)S(1)} %copy-done.22), channel_id=1, source_target_pairs={{0,8},{8,16},{16,24},{24,32},{32,40},{40,48},{48,56},{1,9},{9,17},... | collective-permute-start | bytes 393224 | tf_op jit(solution)/shard_map/ppermute | solution.py:356
  50.6 4.2 %collective-permute-start.6 = (f32[4,32,256]{2,1,0:T(8,128)S(1)}, f32[4,32,256]{2,1,0:T(8,128)S(1)}, u32[]{:S(2)}, u32[]{:S(2)}) collective-permute-start(f32[4,32,256]{2,1,0:T(8,128)S(1)} %copy-done.21), channel_id=1, source_target_pairs={{8,0},{16,8},{24,16},{32,24},{40,32},{48,40},{56,48},{9,1},{17,9},... | collective-permute-start | bytes 393224 | tf_op jit(solution)/shard_map/ppermute | solution.py:356
  54.9 3.9 %collective-permute-start.7 = (f32[4,32,256]{2,1,0:T(8,128)S(1)}, f32[4,32,256]{2,1,0:T(8,128)S(1)}, u32[]{:S(2)}, u32[]{:S(2)}) collective-permute-start(f32[4,32,256]{2,1,0:T(8,128)S(1)} %copy-done.20), channel_id=1, source_target_pairs={{0,1},{1,2},{2,3},{3,4},{4,5},{5,6},{6,7},{8,9},{9,10},{10,11},{11... | collective-permute-start | bytes 393224 | tf_op jit(solution)/shard_map/ppermute | solution.py:356
  58.8 1.9 collective-permute-start.8
  60.7 16.2 %collective-permute-done.5 = f32[4,32,256]{2,1,0:T(8,128)S(1)} collective-permute-done((f32[4,32,256]{2,1,0:T(8,128)S(1)}, f32[4,32,256]{2,1,0:T(8,128)S(1)}, u32[]{:S(2)}, u32[]{:S(2)}) %collective-permute-start.5) | collective-permute-done | bytes 131104 | tf_op jit(solution)/shard_map/ppermute | solution.py:356
  77.0 17.5 %conditional.1 = ((f32[64,4,8,256]{3,2,1,0:T(8,128)}, f32[64,4,8,256]{3,2,1,0:T(8,128)}, bf16[1024,1024]{1,0:T(8,128)(2,1)}, bf16[1024,1024]{1,0:T(8,128)(2,1)},...) conditional(s32[]{:T(128)} %convert_element_type.9, (f32[1,1,128,4,8,8]{2,5,4,3,1,0:T(8,128)S(1)}, ...), branch_computations={%region_0.1_spmd, %region_1.2_spmd} | conditional | flops 12582912 | bytes 29491256 | solution.py:419
  78.5 2.4 copy.28.tile_ref
  80.9 3.5 %fusion = (bf16[4,1024,256]{2,0,1:T(4,128)(2,1)S(1)}, bf16[4,1024,256]{2,0,1:T(4,128)(2,1)S(1)}) fusion(f32[4,256,4,256]{3,2,1,0:T(4,128)} %get-tuple-element.107), kind=kLoop, calls=%fused_computation.2 | loop fusion | flops 4194304 | bytes 8388608 | tf_op jit(solution)/shard_map/cond/branch_0_fun/convert_element_type | solution.py:53
  87.6 6.9 %blend_matrix.1 = (bf16[1024,1024]{1,0:T(8,128)(2,1)}, bf16[1024,1024]{1,0:T(8,128)(2,1)}, f32[64,4,8,256]{3,2,1,0:T(8,128)}, f32[64,4,8,256]{3,2,1,0:T(8,128)}) custom-call(s32[512]{0:T(512)S(1)} %bitcast.55, f32[128,4,8,128]{3,2,1,0:T(8,128)S(1)} %copy.28.tile_ref), custom_call_target="tpu_custom_call" | custom-call | flops 8388608 | bytes 6291456 | tf_op jit(solution)/shard_map/cond/branch_0_fun/blend_matrix/pallas_call | solution.py:86
  95.9 2.1 broadcast_select_fusion
  97.9 34.0 %all_to_all.15.refs_1_ = f32[64,4,8,256]{3,2,1,0:T(8,128)} all-to-all(f32[64,4,8,256]{3,2,1,0:T(8,128)S(1)} %broadcast_select_fusion), channel_id=1, replica_groups=mesh['sec'=2,'rr'=8,'sr'=8] {'rr','sr'}, dimensions={0} | all-to-all | bytes 4194304 | tf_op jit(solution)/shard_map/all_to_all | solution.py:372
  131.9 7.0 %all-to-all-start.2 = ((f32[64,4,8,256]{3,2,1,0:T(8,128)}), f32[64,4,8,256]{3,2,1,0:T(8,128)}, u32[]{:S(2)}, u32[]{:S(2)}) async-start(f32[64,4,8,256]{3,2,1,0:T(8,128)} %get-tuple-element.93), calls=%async_computation.2 | async-start | bytes 4194304 | tf_op jit(solution)/shard_map/all_to_all | solution.py:372
  140.5 3.7 %collective-permute-done.4.refs_0_ = f32[64,4,8,256]{3,2,1,0:T(8,128)} collective-permute-done((f32[64,4,8,256]{3,2,1,0:T(8,128)}, f32[64,4,8,256]{3,2,1,0:T(8,128)}, u32[]{:S(2)}, u32[]{:S(2)}) %collective-permute-start.4) | collective-permute-done | bytes 2097184 | tf_op jit(solution)/shard_map/ppermute | solution.py:368
  144.2 19.8 %inflow_edges.1 = (f32[4,32,32,256]{3,2,1,0:T(8,128)}, f32[4,32,256]{2,1,0:T(8,128)}, f32[4,32,256]{2,1,0:T(8,128)}, f32[4,32,256]{2,1,0:T(8,128)}, f32[4,32,256]{2,1,0:T(8,128)}) custom-call(f32[64,4,8,256]{3,2,1,0:T(8,128)} %collective-permute-done.4.refs_0_, f32[64,4,8,256]{3,2,1,0:T(8,128)} %all_to_all.15.refs_1_, ...), custom_call_target="tpu_custom_call" | custom-call | flops 42949672960 | bytes 1000 | tf_op jit(solution)/shard_map/inflow_edges/pallas_call | solution.py:338
  164.0 2.1 all-to-all-done.2
  166.1 3.3 %fusion.2 = (f32[32,4,8,256]{3,2,1,0:T(8,128)}, f32[32,4,8,256]{3,2,1,0:T(8,128)}) fusion(f32[64,4,8,256]{3,2,1,0:T(8,128)} %all-to-all-done.2), kind=kLoop, calls=%fused_computation.11 | loop fusion | bytes 4194304 | tf_op jit(solution)/shard_map/slice | solution.py:430
  172.0 1.9 collective-permute-start.13
  173.9 5.5 %collective-permute-start.14 = (f32[4,32,256]{2,1,0:T(8,128)}, f32[4,32,256]{2,1,0:T(8,128)S(1)}, u32[]{:S(2)}, u32[]{:S(2)}) collective-permute-start(f32[4,32,256]{2,1,0:T(8,128)} %get-tuple-element.100), channel_id=1, source_target_pairs={{8,0},{16,8},{24,16},{32,24},{40,32},{48,40},{56,48},{9,1},{17,9},... | collective-permute-start | bytes 393224 | tf_op jit(solution)/shard_map/ppermute | solution.py:356
  180.0 4.6 %collective-permute-start.15 = (f32[4,32,256]{2,1,0:T(8,128)}, f32[4,32,256]{2,1,0:T(8,128)S(1)}, u32[]{:S(2)}, u32[]{:S(2)}) collective-permute-start(f32[4,32,256]{2,1,0:T(8,128)} %get-tuple-element.101), channel_id=1, source_target_pairs={{0,1},{1,2},{2,3},{3,4},{4,5},{5,6},{6,7},{8,9},{9,10},{10,11},{11... | collective-permute-start | bytes 393224 | tf_op jit(solution)/shard_map/ppermute | solution.py:356
  186.9 4.7 %collective-permute-done.16.refs_7_ = f32[4,32,256]{2,1,0:T(8,128)S(1)} collective-permute-done((f32[4,32,256]{2,1,0:T(8,128)}, f32[4,32,256]{2,1,0:T(8,128)S(1)}, u32[]{:S(2)}, u32[]{:S(2)}) %collective-permute-start.16) | collective-permute-done | bytes 131104 | tf_op jit(solution)/shard_map/ppermute | solution.py:356
  192.2 9.7 %step_own.1.refs_5_ = f32[4,32,32,256]{3,2,1,0:T(8,128)} custom-call(s32[1]{0:T(128)S(6)} %copy.62.refs_1_.refs_0_, f32[4,32,32,256]{3,2,1,0:T(8,128)} %get-tuple-element.92.refs_1_.refs_2_.refs_3_, f32[4,32,32,256]{3,2,1,0:T(8,128)} %get-tuple-element.92.refs_1_.refs_2_.refs_3_, f32[4,32,32,256]{3,2,1,0:T(8,128)} %get-tuple-element.92.refs_1_.refs_2_.refs_3_, ...), custom_call_target="tpu_custom_call" | custom-call | flops 1000 | bytes 1000 | tf_op jit(solution)/shard_map/step_own/pallas_call | solution.py:259
  201.9 12.1 %inflow.3.refs_5_ = f32[4,32,32,256]{3,2,1,0:T(8,128)} custom-call(f32[64,4,8,256]{3,2,1,0:T(8,128)} %collective-permute-done.12.refs_0_, bf16[4,1024,256]{2,1,0:T(8,128)(2,1)} %get-tuple-element.123.refs_2_.refs_1_, bf16[4,1024,256]{2,1,0:T(8,128)(2,1)S(1)} %copy-done.3, bf16[1024,1024]{1,0:T(8,128)(2,1)} %get-tuple-element.90.refs_4_.refs_3_, ...), custom_call_target="tpu_custom_call" | custom-call | flops 1000 | bytes 1000 | tf_op jit(solution)/shard_map/inflow/pallas_call | solution.py:338
  214.0 10.7 %inflow.4.refs_5_ = f32[4,32,32,256]{3,2,1,0:T(8,128)} custom-call(f32[32,4,8,256]{3,2,1,0:T(8,128)} %collective-permute-done.11.refs_0_, bf16[4,1024,256]{2,1,0:T(8,128)(2,1)S(1)} %copy-done.4, bf16[4,1024,256]{2,1,0:T(8,128)(2,1)S(1)} %copy-done.3, bf16[1024,1024]{1,0:T(8,128)(2,1)S(1)} %copy-done.5, bf16[1024,1024]{1,0:T(8,128)(2,1)} %get-tuple-element.91.refs_5_.refs_4_, ...), custom_call_target="tpu_custom_call" | custom-call | flops 1000 | bytes 1000 | tf_op jit(solution)/shard_map/inflow/pallas_call | solution.py:338
  224.7 10.4 %collective-permute-done.10.refs_0_ = f32[32,4,8,256]{3,2,1,0:T(8,128)} collective-permute-done((f32[32,4,8,256]{3,2,1,0:T(8,128)}, f32[32,4,8,256]{3,2,1,0:T(8,128)}, u32[]{:S(2)}, u32[]{:S(2)}) %collective-permute-start.10) | collective-permute-done | bytes 1048608 | tf_op jit(solution)/shard_map/ppermute | solution.py:368
  235.1 10.6 %inflow.5 = f32[4,32,32,256]{3,2,1,0:T(8,128)} custom-call(f32[32,4,8,256]{3,2,1,0:T(8,128)} %collective-permute-done.10.refs_0_, bf16[4,1024,256]{2,1,0:T(8,128)(2,1)S(1)} %copy-done.4, bf16[4,1024,256]{2,1,0:T(8,128)(2,1)S(1)} %copy-done.3, bf16[1024,1024]{1,0:T(8,128)(2,1)S(1)} %copy-done.5, bf16[1024,1024]{1,0:T(8,128)(2,1)} %get-tuple-element.91.refs_5_.refs_4_, ...), custom_call_target="tpu_custom_call" | custom-call | flops 1000 | bytes 1000 | tf_op jit(solution)/shard_map/inflow/pallas_call | solution.py:338
  (75 shorter events, 18.7 us)
Async XLA Ops:
  0.6 16.9 %copy-start = (s32[64,64,2]{1,2,0:T(2,128)S(1)}, s32[64,64,2]{1,2,0:T(2,128)}, u32[]{:S(2)}) copy-start(s32[64,64,2]{1,2,0:T(2,128)} %param.23) | copy-start | bytes 98308
  0.6 22.8 %copy-start.6 = (f32[1,32,32,256]{3,2,1,0:T(8,128)S(1)}, f32[1,32,32,256]{3,2,1,0:T(8,128)}, u32[]{:S(2)}) copy-start(f32[1,32,32,256]{3,2,1,0:T(8,128)} %param.16) | copy-start | bytes 3145732
  2.5 15.4 %collective-permute-start.2 = (f32[4,32,256]{2,1,0:T(8,128)S(1)}, f32[4,32,256]{2,1,0:T(8,128)S(1)}, u32[]{:S(2)}, u32[]{:S(2)}) collective-permute-start(f32[4,32,256]{2,1,0:T(8,128)S(1)} %bitcast.52), channel_id=1, source_target_pairs={{0,1},{1,2},{2,3},{3,4},{4,5},{5,6},{6,7},{8,9},{9,10},{10,11},{11... | collective-permute-start | bytes 393224 | tf_op jit(solution)/shard_map/ppermute | solution.py:356
  6.2 11.7 %collective-permute-start.3 = (f32[4,32,256]{2,1,0:T(8,128)S(1)}, f32[4,32,256]{2,1,0:T(8,128)S(1)}, u32[]{:S(2)}, u32[]{:S(2)}) collective-permute-start(f32[4,32,256]{2,1,0:T(8,128)S(1)} %bitcast.53), channel_id=1, source_target_pairs={{1,0},{2,1},{3,2},{4,3},{5,4},{6,5},{7,6},{9,8},{10,9},{11,10},{12... | collective-permute-start | bytes 393224 | tf_op jit(solution)/shard_map/ppermute | solution.py:356
  9.1 8.8 %collective-permute-start.1 = (f32[4,32,256]{2,1,0:T(8,128)S(1)}, f32[4,32,256]{2,1,0:T(8,128)S(1)}, u32[]{:S(2)}, u32[]{:S(2)}) collective-permute-start(f32[4,32,256]{2,1,0:T(8,128)S(1)} %get-tuple-element.129), channel_id=1, source_target_pairs={{8,0},{16,8},{24,16},{32,24},{40,32},{48,40},{56,48},{9,1},{17,9},... | collective-permute-start | bytes 393224 | tf_op jit(solution)/shard_map/ppermute | solution.py:356
  15.0 7.8 %collective-permute-start = (f32[4,32,256]{2,1,0:T(8,128)S(1)}, f32[4,32,256]{2,1,0:T(8,128)S(1)}, u32[]{:S(2)}, u32[]{:S(2)}) collective-permute-start(f32[4,32,256]{2,1,0:T(8,128)S(1)} %get-tuple-element.130), channel_id=1, source_target_pairs={{0,8},{8,16},{16,24},{24,32},{32,40},{40,48},{48,56},{1,9},{9,17},... | collective-permute-start | bytes 393224 | tf_op jit(solution)/shard_map/ppermute | solution.py:356
  37.6 58.2 %collective-permute-start.9 = (f32[64,4,8,256]{3,2,1,0:T(8,128)}, f32[64,4,8,256]{3,2,1,0:T(8,128)}, u32[]{:S(2)}, u32[]{:S(2)}) collective-permute-start(f32[64,4,8,256]{3,2,1,0:T(8,128)} %get-tuple-element.86), channel_id=1, source_target_pairs={{0,96},{1,97},{2,98},{3,99},{4,100},{5,101},{6,102},{7,103},{8,104... | collective-permute-start | bytes 6291464 | tf_op jit(solution)/shard_map/ppermute | solution.py:368
  38.9 11.7 %copy-start.21 = (f32[4,32,256]{2,1,0:T(8,128)S(1)}, f32[4,32,256]{2,1,0:T(8,128)}, u32[]{:S(2)}) copy-start(f32[4,32,256]{2,1,0:T(8,128)} %get-tuple-element.80) | copy-start | bytes 393220
  38.9 15.9 %copy-start.20 = (f32[4,32,256]{2,1,0:T(8,128)S(1)}, f32[4,32,256]{2,1,0:T(8,128)}, u32[]{:S(2)}) copy-start(f32[4,32,256]{2,1,0:T(8,128)} %get-tuple-element.81) | copy-start | bytes 393220
  38.9 19.9 %copy-start.19 = (f32[4,32,256]{2,1,0:T(8,128)S(1)}, f32[4,32,256]{2,1,0:T(8,128)}, u32[]{:S(2)}) copy-start(f32[4,32,256]{2,1,0:T(8,128)} %get-tuple-element.82) | copy-start | bytes 393220
  39.0 38.1 %copy-start.7 = (f32[1,32,32]{2,1,0:T(8,128)S(1)}, f32[1,32,32]{2,1,0:T(8,128)}, u32[]{:S(2)}) copy-start(f32[1,32,32]{2,1,0:T(8,128)} %param.17) | copy-start | bytes 12292
  39.0 38.0 %copy-start.8 = (f32[32,32]{1,0:T(8,128)S(1)}, f32[32,32]{1,0:T(8,128)}, u32[]{:S(2)}) copy-start(f32[32,32]{1,0:T(8,128)} %refs_11_.1) | copy-start | bytes 12292
  39.0 38.0 %copy-start.17 = (f32[1,1,128,4,8,8]{2,5,4,3,1,0:T(8,128)S(1)}, f32[1,1,128,4,8,8]{2,5,4,3,1,0:T(8,128)}, u32[]{:S(2)}) copy-start(f32[1,1,128,4,8,8]{2,5,4,3,1,0:T(8,128)} %param.25) | copy-start | bytes 393220
  39.0 38.0 %copy-start.18 = (s32[1,1,128,4]{2,3,1,0:T(4,128)S(1)}, s32[1,1,128,4]{2,3,1,0:T(4,128)}, u32[]{:S(2)}) copy-start(s32[1,1,128,4]{2,3,1,0:T(4,128)} %param.24) | copy-start | bytes 6148
  39.0 55.6 %all-to-all-start = ((f32[64,4,8,256]{3,2,1,0:T(8,128)}), f32[64,4,8,256]{3,2,1,0:T(8,128)}, u32[]{:S(2)}, u32[]{:S(2)}) async-start(f32[64,4,8,256]{3,2,1,0:T(8,128)} %get-tuple-element.77), calls=%async_computation | async-start | bytes 4194304 | tf_op jit(solution)/shard_map/all_to_all | solution.py:372
  47.4 29.5 %collective-permute-start.5 = (f32[4,32,256]{2,1,0:T(8,128)S(1)}, f32[4,32,256]{2,1,0:T(8,128)S(1)}, u32[]{:S(2)}, u32[]{:S(2)}) collective-permute-start(f32[4,32,256]{2,1,0:T(8,128)S(1)} %copy-done.22), channel_id=1, source_target_pairs={{0,8},{8,16},{16,24},{24,32},{32,40},{40,48},{48,56},{1,9},{9,17},... | collective-permute-start | bytes 393224 | tf_op jit(solution)/shard_map/ppermute | solution.py:356
  50.6 26.4 %collective-permute-start.6 = (f32[4,32,256]{2,1,0:T(8,128)S(1)}, f32[4,32,256]{2,1,0:T(8,128)S(1)}, u32[]{:S(2)}, u32[]{:S(2)}) collective-permute-start(f32[4,32,256]{2,1,0:T(8,128)S(1)} %copy-done.21), channel_id=1, source_target_pairs={{8,0},{16,8},{24,16},{32,24},{40,32},{48,40},{56,48},{9,1},{17,9},... | collective-permute-start | bytes 393224 | tf_op jit(solution)/shard_map/ppermute | solution.py:356
  54.9 22.1 %collective-permute-start.7 = (f32[4,32,256]{2,1,0:T(8,128)S(1)}, f32[4,32,256]{2,1,0:T(8,128)S(1)}, u32[]{:S(2)}, u32[]{:S(2)}) collective-permute-start(f32[4,32,256]{2,1,0:T(8,128)S(1)} %copy-done.20), channel_id=1, source_target_pairs={{0,1},{1,2},{2,3},{3,4},{4,5},{5,6},{6,7},{8,9},{9,10},{10,11},{11... | collective-permute-start | bytes 393224 | tf_op jit(solution)/shard_map/ppermute | solution.py:356
  58.8 18.2 %collective-permute-start.8 = (f32[4,32,256]{2,1,0:T(8,128)S(1)}, f32[4,32,256]{2,1,0:T(8,128)S(1)}, u32[]{:S(2)}, u32[]{:S(2)}) collective-permute-start(f32[4,32,256]{2,1,0:T(8,128)S(1)} %copy-done.19), channel_id=1, source_target_pairs={{1,0},{2,1},{3,2},{4,3},{5,4},{6,5},{7,6},{9,8},{10,9},{11,10},{12... | collective-permute-start | bytes 393224 | tf_op jit(solution)/shard_map/ppermute | solution.py:356
  94.6 49.6 %collective-permute-start.4 = (f32[64,4,8,256]{3,2,1,0:T(8,128)}, f32[64,4,8,256]{3,2,1,0:T(8,128)}, u32[]{:S(2)}, u32[]{:S(2)}) collective-permute-start(f32[64,4,8,256]{3,2,1,0:T(8,128)} %all-to-all-done), channel_id=1, source_target_pairs={{0,96},{1,97},{2,98},{3,99},{4,100},{5,101},{6,102},{7,103},{8,104... | collective-permute-start | bytes 6291464 | tf_op jit(solution)/shard_map/ppermute | solution.py:368
  131.9 12.2 %copy-start.3 = (bf16[4,1024,256]{2,1,0:T(8,128)(2,1)S(1)}, bf16[4,1024,256]{2,1,0:T(8,128)(2,1)}, u32[]{:S(2)}) copy-start(bf16[4,1024,256]{2,1,0:T(8,128)(2,1)} %get-tuple-element.124.refs_3_.refs_2_) | copy-start | bytes 6291460
  131.9 34.2 %all-to-all-start.2 = ((f32[64,4,8,256]{3,2,1,0:T(8,128)}), f32[64,4,8,256]{3,2,1,0:T(8,128)}, u32[]{:S(2)}, u32[]{:S(2)}) async-start(f32[64,4,8,256]{3,2,1,0:T(8,128)} %get-tuple-element.93), calls=%async_computation.2 | async-start | bytes 4194304 | tf_op jit(solution)/shard_map/all_to_all | solution.py:372
  139.0 62.9 %collective-permute-start.12 = (f32[64,4,8,256]{3,2,1,0:T(8,128)}, f32[64,4,8,256]{3,2,1,0:T(8,128)}, u32[]{:S(2)}, u32[]{:S(2)}) collective-permute-start(f32[64,4,8,256]{3,2,1,0:T(8,128)} %all_to_all.15.refs_1_), channel_id=1, source_target_pairs={{0,96},{1,97},{2,98},{3,99},{4,100},{5,101},{6,102},{7,103},{8,104... | collective-permute-start | bytes 6291464 | tf_op jit(solution)/shard_map/ppermute | solution.py:368
  166.1 26.1 %copy-start.2 = (f32[1,4,32,32,256]{4,3,2,1,0:T(8,128)S(1)}, f32[1,4,32,32,256]{4,3,2,1,0:T(8,128)}, u32[]{:S(2)}) copy-start(f32[1,4,32,32,256]{4,3,2,1,0:T(8,128)} %param.15) | copy-start | bytes 12582916
  169.4 44.6 %collective-permute-start.11 = (f32[32,4,8,256]{3,2,1,0:T(8,128)}, f32[32,4,8,256]{3,2,1,0:T(8,128)}, u32[]{:S(2)}, u32[]{:S(2)}) collective-permute-start(f32[32,4,8,256]{3,2,1,0:T(8,128)} %get-tuple-element.131), channel_id=1, source_target_pairs={{0,96},{1,97},{2,98},{3,99},{4,100},{5,101},{6,102},{7,103},{8,104... | collective-permute-start | bytes 3145736 | tf_op jit(solution)/shard_map/ppermute | solution.py:368
  170.7 64.4 %collective-permute-start.10 = (f32[32,4,8,256]{3,2,1,0:T(8,128)}, f32[32,4,8,256]{3,2,1,0:T(8,128)}, u32[]{:S(2)}, u32[]{:S(2)}) collective-permute-start(f32[32,4,8,256]{3,2,1,0:T(8,128)} %get-tuple-element.132), channel_id=1, source_target_pairs={{0,96},{1,97},{2,98},{3,99},{4,100},{5,101},{6,102},{7,103},{8,104... | collective-permute-start | bytes 3145736 | tf_op jit(solution)/shard_map/ppermute | solution.py:368
  172.0 8.0 %collective-permute-start.13 = (f32[4,32,256]{2,1,0:T(8,128)}, f32[4,32,256]{2,1,0:T(8,128)S(1)}, u32[]{:S(2)}, u32[]{:S(2)}) collective-permute-start(f32[4,32,256]{2,1,0:T(8,128)} %get-tuple-element.99), channel_id=1, source_target_pairs={{0,8},{8,16},{16,24},{24,32},{32,40},{40,48},{48,56},{1,9},{9,17},... | collective-permute-start | bytes 393224 | tf_op jit(solution)/shard_map/ppermute | solution.py:356
  173.9 10.7 %collective-permute-start.14 = (f32[4,32,256]{2,1,0:T(8,128)}, f32[4,32,256]{2,1,0:T(8,128)S(1)}, u32[]{:S(2)}, u32[]{:S(2)}) collective-permute-start(f32[4,32,256]{2,1,0:T(8,128)} %get-tuple-element.100), channel_id=1, source_target_pairs={{8,0},{16,8},{24,16},{32,24},{40,32},{48,40},{56,48},{9,1},{17,9},... | collective-permute-start | bytes 393224 | tf_op jit(solution)/shard_map/ppermute | solution.py:356
  180.0 6.8 %collective-permute-start.15 = (f32[4,32,256]{2,1,0:T(8,128)}, f32[4,32,256]{2,1,0:T(8,128)S(1)}, u32[]{:S(2)}, u32[]{:S(2)}) collective-permute-start(f32[4,32,256]{2,1,0:T(8,128)} %get-tuple-element.101), channel_id=1, source_target_pairs={{0,1},{1,2},{2,3},{3,4},{4,5},{5,6},{6,7},{8,9},{9,10},{10,11},{11... | collective-permute-start | bytes 393224 | tf_op jit(solution)/shard_map/ppermute | solution.py:356
  184.6 6.9 %collective-permute-start.16 = (f32[4,32,256]{2,1,0:T(8,128)}, f32[4,32,256]{2,1,0:T(8,128)S(1)}, u32[]{:S(2)}, u32[]{:S(2)}) collective-permute-start(f32[4,32,256]{2,1,0:T(8,128)} %get-tuple-element.102), channel_id=1, source_target_pairs={{1,0},{2,1},{3,2},{4,3},{5,4},{6,5},{7,6},{9,8},{10,9},{11,10},{12... | collective-permute-start | bytes 393224 | tf_op jit(solution)/shard_map/ppermute | solution.py:356
  201.9 12.1 %copy-start.4 = (bf16[4,1024,256]{2,1,0:T(8,128)(2,1)S(1)}, bf16[4,1024,256]{2,1,0:T(8,128)(2,1)}, u32[]{:S(2)}) copy-start(bf16[4,1024,256]{2,1,0:T(8,128)(2,1)} %get-tuple-element.123.refs_2_.refs_1_) | copy-start | bytes 6291460
  201.9 12.1 %copy-start.5 = (bf16[1024,1024]{1,0:T(8,128)(2,1)S(1)}, bf16[1024,1024]{1,0:T(8,128)(2,1)}, u32[]{:S(2)}) copy-start(bf16[1024,1024]{1,0:T(8,128)(2,1)} %get-tuple-element.90.refs_4_.refs_3_) | copy-start | bytes 6291460
  (10 other events, 58.3 us)

commit v7 on v6

--- a/solution.py
+++ b/solution.py
@@ -403,22 +403,22 @@
     relayed_1 = spread(zero_1)
     pack_shapes = [jax.ShapeDtypeStruct((SRCS, HEL, BLK, NA), F32)] * 2
     blend_shapes = [jax.ShapeDtypeStruct((PTS, PTS), BF16)] * 2
-    frame_shapes = [jax.ShapeDtypeStruct((HEL, HEL * NA, NA), BF16)] * 2
 
     def reactant(own, halo, weights, *_):
         one, zero, *rest = step_call(
-            False, False, True, ids, helicity_start, own, halo, current, *fixed, weights, others=blend_shapes + frame_shapes
+            False, False, True, ids, helicity_start, own, halo, current, *fixed, weights, others=blend_shapes
         )
-        return one, zero, tuple(rest[:2]), tuple(rest[2:])
-
-    def product(own, halo, weights, picks, tiles, frame_map):
-        high, low, one, zero = blend_call(picks, jnp.tile(tiles, (1, 1, 1, 128 // BLK)), pack_shapes)
-        return one, zero, (high, low), frame_terms(frame_map)
-
+        return one, zero, tuple(rest)
+
+    def product(own, halo, weights, picks, tiles):
+        high, low, one, zero = blend_call(picks, tiles, pack_shapes)
+        return one, zero, (high, low)
+
+    late_map, late_weights, own_1 = lax.optimization_barrier((frame_map, interp_weights[0, 0], own_1))
+    frame, tiles = frame_terms(late_map), jnp.tile(late_weights, (1, 1, 1, 128 // BLK))
+    own_1, frame, tiles = lax.optimization_barrier((own_1, frame, tiles))
     picks = pick_slots[0, 0].T.reshape(MSLOT * NBLK)
-    one_2, zero_2, blend, frame = lax.cond(
-        section == 0, reactant, product, own_1, halo, weights, picks, interp_weights[0, 0], frame_map
-    )
+    one_2, zero_2, blend = lax.cond(section == 0, reactant, product, own_1, halo, weights, picks, tiles)
     crossed_zero_1 = cross(relayed_1)
     shared = spread(jnp.where(section == 0, zero_2, crossed_one_1))
     crossed_zero_2 = cross(shared)

time: 247 us -> 244 us (0.988)
  waiting for transfers between devices: 43 us -> 39 us
    ppermute x12, waiting for transfers between devices: 26.7 us -> 18.5 us  [send(): return lax.ppermute(piece, axis, pairs)]
    ppermute x5, waiting for transfers between devices: 14.1 us -> 20.3 us  [cross(): return lax.ppermute(x, ALL, pairs)]
    cond x2 -> x0, local copies, waits for them, and re-layouts: 3.26 us -> none  [per_device(): lax.cond(section == 0, reactant, product, own_1, halo, weights, picks, in...]
    transpose x0 -> x1, local copies, waits for them, and re-layouts: none -> 3 us  [frame_terms(): turned = frame_map.transpose(2, 0, 1, 3).reshape(HEL, HEL * NA, NA)]
  transfers between devices with their start and end apart: 19 -> 19, of which waited for: 8 -> 9; matrix products, arithmetic and copies ran while one was open for 7% -> 7% of each run, Pallas kernels for 24% -> 24%
where the time goes in v7:
time: 244 us; the launch traced here: 242 us
  Pallas kernels  84 us (34%)
  starting transfers between devices  62.7 us (26%)
  waiting for transfers between devices  39 us (16%)
  blocking collectives  34.2 us (14%)
  local copies, waits for them, and re-layouts  15.4 us (6%)
  other arithmetic  5 us (2%)
    pallas_call x4, Pallas kernels, inflow_call(): pl.pallas_call(functools.partial(inflow_kernel, len(xs), want_edges), gri...  53.1 us
    ppermute x12, starting transfers between devices, send(): return lax.ppermute(piece, axis, pairs)  40.6 us
    all_to_all x1, blocking collectives, spread(): lax.all_to_all(x, ('rr', 'sr'), split_axis=0, concat_axis=0, tiled=True)  34.2 us
    pallas_call x2, Pallas kernels, step_call(): pl.pallas_call(functools.partial(step_kernel, first_step, want_own, want_...  23.9 us
    ppermute x5, waiting for transfers between devices, cross(): return lax.ppermute(x, ALL, pairs)  20.3 us
    ppermute x12, waiting for transfers between devices, send(): return lax.ppermute(piece, axis, pairs)  18.5 us
    all_to_all x2, starting transfers between devices, spread(): lax.all_to_all(x, ('rr', 'sr'), split_axis=0, concat_axis=0, tiled=True)  15.5 us
    pallas_call x1, Pallas kernels, blend_call(): pl.pallas_call(blend_kernel, in_specs=[smem(), pl.BlockSpec(memory_space=...  7.04 us
  transfers between devices with their start and end apart: 19, of which 9 were waited for; matrix products, arithmetic and copies ran while one was open for 7% of the time, Pallas kernels for 24%

profile of v7, /device:TPU:27, one launch (start us, length us, event | category | flops | bytes accessed | tf_op | source)
XLA Modules:
  0.0 242.1 jit_solution(11064070644089923037)
XLA Ops:
  2.5 3.7 %collective-permute-start.2 = (f32[4,32,256]{2,1,0:T(8,128)S(1)}, f32[4,32,256]{2,1,0:T(8,128)S(1)}, u32[]{:S(2)}, u32[]{:S(2)}) collective-permute-start(f32[4,32,256]{2,1,0:T(8,128)S(1)} %bitcast.52), channel_id=1, source_target_pairs={{0,1},{1,2},{2,3},{3,4},{4,5},{5,6},{6,7},{8,9},{9,10},{10,11},{11... | collective-permute-start | bytes 393224 | tf_op jit(solution)/shard_map/ppermute | solution.py:356
  6.2 1.9 collective-permute-start.3
  9.1 5.8 %collective-permute-start.1 = (f32[4,32,256]{2,1,0:T(8,128)S(1)}, f32[4,32,256]{2,1,0:T(8,128)S(1)}, u32[]{:S(2)}, u32[]{:S(2)}) collective-permute-start(f32[4,32,256]{2,1,0:T(8,128)S(1)} %get-tuple-element.117), channel_id=1, source_target_pairs={{8,0},{16,8},{24,16},{32,24},{40,32},{48,40},{56,48},{9,1},{17,9},... | collective-permute-start | bytes 393224 | tf_op jit(solution)/shard_map/ppermute | solution.py:356
  18.8 4.0 %collective-permute-done.refs_5_ = f32[4,32,256]{2,1,0:T(8,128)S(1)} collective-permute-done((f32[4,32,256]{2,1,0:T(8,128)S(1)}, f32[4,32,256]{2,1,0:T(8,128)S(1)}, u32[]{:S(2)}, u32[]{:S(2)}) %collective-permute-start) | collective-permute-done | bytes 131104 | tf_op jit(solution)/shard_map/ppermute | solution.py:356
  23.5 14.1 %step_first.1 = (f32[4,32,32,256]{3,2,1,0:T(8,128)}, f32[64,4,8,256]{3,2,1,0:T(8,128)}, f32[64,4,8,256]{3,2,1,0:T(8,128)}, f32[4,32,256]{2,1,0:T(8,128)}, f32[4,...) custom-call(s32[128]{0:T(128)S(1)} %reshape.18.refs_0_, ...), custom_call_target="tpu_custom_call" | custom-call | flops 1000 | bytes 1000 | tf_op jit(solution)/shard_map/step_first/pallas_call | solution.py:259
  39.0 8.4 %all-to-all-start = ((f32[64,4,8,256]{3,2,1,0:T(8,128)}), f32[64,4,8,256]{3,2,1,0:T(8,128)}, u32[]{:S(2)}, u32[]{:S(2)}) async-start(f32[64,4,8,256]{3,2,1,0:T(8,128)} %get-tuple-element.80), calls=%async_computation | async-start | bytes 4194304 | tf_op jit(solution)/shard_map/all_to_all | solution.py:372
  47.4 3.1 %collective-permute-start.5 = (f32[4,32,256]{2,1,0:T(8,128)S(1)}, f32[4,32,256]{2,1,0:T(8,128)S(1)}, u32[]{:S(2)}, u32[]{:S(2)}) collective-permute-start(f32[4,32,256]{2,1,0:T(8,128)S(1)} %copy-done.20), channel_id=1, source_target_pairs={{0,8},{8,16},{16,24},{24,32},{32,40},{40,48},{48,56},{1,9},{9,17},... | collective-permute-start | bytes 393224 | tf_op jit(solution)/shard_map/ppermute | solution.py:356
  50.6 4.2 %collective-permute-start.6 = (f32[4,32,256]{2,1,0:T(8,128)S(1)}, f32[4,32,256]{2,1,0:T(8,128)}, u32[]{:S(2)}, u32[]{:S(2)}) collective-permute-start(f32[4,32,256]{2,1,0:T(8,128)S(1)} %copy-done.19), channel_id=1, source_target_pairs={{8,0},{16,8},{24,16},{32,24},{40,32},{48,40},{56,48},{9,1},{17,9},... | collective-permute-start | bytes 393224 | tf_op jit(solution)/shard_map/ppermute | solution.py:356
  54.9 3.9 %collective-permute-start.7 = (f32[4,32,256]{2,1,0:T(8,128)S(1)}, f32[4,32,256]{2,1,0:T(8,128)}, u32[]{:S(2)}, u32[]{:S(2)}) collective-permute-start(f32[4,32,256]{2,1,0:T(8,128)S(1)} %copy-done.18), channel_id=1, source_target_pairs={{0,1},{1,2},{2,3},{3,4},{4,5},{5,6},{6,7},{8,9},{9,10},{10,11},{11... | collective-permute-start | bytes 393224 | tf_op jit(solution)/shard_map/ppermute | solution.py:356
  58.8 1.9 collective-permute-start.8
  60.7 3.0 %copy.18 = f32[4,4,256,256]{3,2,1,0:T(8,128)S(1)} copy(f32[4,4,256,256]{3,0,2,1:T(4,128)} %bitcast.46) | data formatting | bytes 8388608 | tf_op jit(solution)/shard_map/transpose | solution.py:51
  63.7 2.9 %fusion = (bf16[4,1024,256]{2,1,0:T(8,128)(2,1)}, bf16[4,1024,256]{2,1,0:T(8,128)(2,1)}) fusion(f32[4,4,256,256]{3,2,1,0:T(8,128)S(1)} %copy.18), kind=kLoop, calls=%fused_computation.2 | loop fusion | flops 4194304 | bytes 8388608 | tf_op jit(solution)/shard_map/convert_element_type | solution.py:53
  68.1 8.8 %collective-permute-done.5 = f32[4,32,256]{2,1,0:T(8,128)S(1)} collective-permute-done((f32[4,32,256]{2,1,0:T(8,128)S(1)}, f32[4,32,256]{2,1,0:T(8,128)S(1)}, u32[]{:S(2)}, u32[]{:S(2)}) %collective-permute-start.5) | collective-permute-done | bytes 131104 | tf_op jit(solution)/shard_map/ppermute | solution.py:356
  77.0 9.4 %conditional.1 = ((f32[64,4,8,256]{3,2,1,0:T(8,128)}, f32[64,4,8,256]{3,2,1,0:T(8,128)}, bf16[1024,1024]{1,0:T(8,128)(2,1)}, bf16[1024,1024]{1,0:T(8,128)(2,1)})) conditional(s32[]{:T(128)} %convert_element_type.9, (s32[4,128]{1,0:T(4,128)S(1)}, f32[128,4,8,128]{0,3,2,1:T(8,128)}) %tuple.39, (s32[128]{0:T(128)S(1)}, s32[1]{0:T(128)}, ...), branch_computations={%region_0.1_spmd, %region_1.2_spmd} | conditional | flops 8388608 | bytes 10485800 | solution.py:421
  77.0 2.4 copy.19.tile_ref
  79.4 7.0 %blend_matrix.1 = (bf16[1024,1024]{1,0:T(8,128)(2,1)}, bf16[1024,1024]{1,0:T(8,128)(2,1)}, f32[64,4,8,256]{3,2,1,0:T(8,128)}, f32[64,4,8,256]{3,2,1,0:T(8,128)}) custom-call(s32[512]{0:T(512)S(1)} %bitcast.55, f32[128,4,8,128]{3,2,1,0:T(8,128)S(1)} %copy.19.tile_ref), custom_call_target="tpu_custom_call" | custom-call | flops 8388608 | bytes 6291456 | tf_op jit(solution)/shard_map/cond/branch_0_fun/blend_matrix/pallas_call | solution.py:86
  87.7 2.1 broadcast_select_fusion
  89.8 34.2 %all_to_all.15.refs_1_ = f32[64,4,8,256]{3,2,1,0:T(8,128)} all-to-all(f32[64,4,8,256]{3,2,1,0:T(8,128)S(1)} %broadcast_select_fusion), channel_id=1, replica_groups=mesh['sec'=2,'rr'=8,'sr'=8] {'rr','sr'}, dimensions={0} | all-to-all | bytes 4194304 | tf_op jit(solution)/shard_map/all_to_all | solution.py:372
  124.0 7.0 %all-to-all-start.2 = ((f32[64,4,8,256]{3,2,1,0:T(8,128)}), f32[64,4,8,256]{3,2,1,0:T(8,128)}, u32[]{:S(2)}, u32[]{:S(2)}) async-start(f32[64,4,8,256]{3,2,1,0:T(8,128)} %get-tuple-element.101), calls=%async_computation.2 | async-start | bytes 4194304 | tf_op jit(solution)/shard_map/all_to_all | solution.py:372
  132.5 5.9 %collective-permute-done.4.refs_0_ = f32[64,4,8,256]{3,2,1,0:T(8,128)} collective-permute-done((f32[64,4,8,256]{3,2,1,0:T(8,128)}, f32[64,4,8,256]{3,2,1,0:T(8,128)}, u32[]{:S(2)}, u32[]{:S(2)}) %collective-permute-start.4) | collective-permute-done | bytes 2097184 | tf_op jit(solution)/shard_map/ppermute | solution.py:368
  138.4 19.5 %inflow_edges.1 = (f32[4,32,32,256]{3,2,1,0:T(8,128)}, f32[4,32,256]{2,1,0:T(8,128)}, f32[4,32,256]{2,1,0:T(8,128)}, f32[4,32,256]{2,1,0:T(8,128)}, f32[4,32,256]{2,1,0:T(8,128)}) custom-call(f32[64,4,8,256]{3,2,1,0:T(8,128)} %collective-permute-done.4.refs_0_, f32[64,4,8,256]{3,2,1,0:T(8,128)} %all_to_all.15.refs_1_, ...), custom_call_target="tpu_custom_call" | custom-call | flops 42949672960 | bytes 1000 | tf_op jit(solution)/shard_map/inflow_edges/pallas_call | solution.py:338
  158.1 3.2 %fusion.2 = (f32[32,4,8,256]{3,2,1,0:T(8,128)}, f32[32,4,8,256]{3,2,1,0:T(8,128)}) fusion(f32[64,4,8,256]{3,2,1,0:T(8,128)} %all-to-all-done.2), kind=kLoop, calls=%fused_computation.11 | loop fusion | bytes 4194304 | tf_op jit(solution)/shard_map/slice | solution.py:430
  164.0 3.1 %collective-permute-start.13 = (f32[4,32,256]{2,1,0:T(8,128)}, f32[4,32,256]{2,1,0:T(8,128)S(1)}, u32[]{:S(2)}, u32[]{:S(2)}) collective-permute-start(f32[4,32,256]{2,1,0:T(8,128)} %get-tuple-element.107), channel_id=1, source_target_pairs={{0,8},{8,16},{16,24},{24,32},{32,40},{40,48},{48,56},{1,9},{9,17},... | collective-permute-start | bytes 393224 | tf_op jit(solution)/shard_map/ppermute | solution.py:356
  167.0 4.3 %collective-permute-start.14 = (f32[4,32,256]{2,1,0:T(8,128)}, f32[4,32,256]{2,1,0:T(8,128)S(1)}, u32[]{:S(2)}, u32[]{:S(2)}) collective-permute-start(f32[4,32,256]{2,1,0:T(8,128)} %get-tuple-element.108), channel_id=1, source_target_pairs={{8,0},{16,8},{24,16},{32,24},{40,32},{48,40},{56,48},{9,1},{17,9},... | collective-permute-start | bytes 393224 | tf_op jit(solution)/shard_map/ppermute | solution.py:356
  172.0 4.7 %collective-permute-start.15 = (f32[4,32,256]{2,1,0:T(8,128)}, f32[4,32,256]{2,1,0:T(8,128)S(1)}, u32[]{:S(2)}, u32[]{:S(2)}) collective-permute-start(f32[4,32,256]{2,1,0:T(8,128)} %get-tuple-element.109), channel_id=1, source_target_pairs={{0,1},{1,2},{2,3},{3,4},{4,5},{5,6},{6,7},{8,9},{9,10},{10,11},{11... | collective-permute-start | bytes 393224 | tf_op jit(solution)/shard_map/ppermute | solution.py:356
  179.0 4.7 %collective-permute-done.16.refs_7_ = f32[4,32,256]{2,1,0:T(8,128)S(1)} collective-permute-done((f32[4,32,256]{2,1,0:T(8,128)}, f32[4,32,256]{2,1,0:T(8,128)S(1)}, u32[]{:S(2)}, u32[]{:S(2)}) %collective-permute-start.16) | collective-permute-done | bytes 131104 | tf_op jit(solution)/shard_map/ppermute | solution.py:356
  184.3 9.7 %step_own.1.refs_5_ = f32[4,32,32,256]{3,2,1,0:T(8,128)} custom-call(s32[1]{0:T(128)S(6)} %copy.34.refs_1_.refs_0_, f32[4,32,32,256]{3,2,1,0:T(8,128)} %get-tuple-element.100.refs_1_.refs_2_.refs_3_, f32[4,32,32,256]{3,2,1,0:T(8,128)} %get-tuple-element.100.refs_1_.refs_2_.refs_3_, f32[4,32,32,256]{3,2,1,0:T(8,128)} %get-tuple-element.100.refs_1_.refs_2_.refs_3_, ...), custom_call_target="tpu_custom_call" | custom-call | flops 1000 | bytes 1000 | tf_op jit(solution)/shard_map/step_own/pallas_call | solution.py:259
  194.1 12.0 %inflow.3.refs_5_ = f32[4,32,32,256]{3,2,1,0:T(8,128)} custom-call(f32[64,4,8,256]{3,2,1,0:T(8,128)} %collective-permute-done.12.refs_0_, bf16[4,1024,256]{2,1,0:T(8,128)(2,1)} %get-tuple-element.96.refs_2_.refs_1_, bf16[4,1024,256]{2,1,0:T(8,128)(2,1)} %get-tuple-element.97.refs_3_.refs_2_, bf16[1024,1024]{1,0:T(8,128)(2,1)S(1)} %copy-done.3, ...), custom_call_target="tpu_custom_call" | custom-call | flops 1000 | bytes 1000 | tf_op jit(solution)/shard_map/inflow/pallas_call | solution.py:338
  206.0 2.8 %collective-permute-done.11.refs_0_ = f32[32,4,8,256]{3,2,1,0:T(8,128)} collective-permute-done((f32[32,4,8,256]{3,2,1,0:T(8,128)}, f32[32,4,8,256]{3,2,1,0:T(8,128)}, u32[]{:S(2)}, u32[]{:S(2)}) %collective-permute-start.11) | collective-permute-done | bytes 1048608 | tf_op jit(solution)/shard_map/ppermute | solution.py:368
  208.8 10.8 %inflow.4.refs_5_ = f32[4,32,32,256]{3,2,1,0:T(8,128)} custom-call(f32[32,4,8,256]{3,2,1,0:T(8,128)} %collective-permute-done.11.refs_0_, bf16[4,1024,256]{2,1,0:T(8,128)(2,1)} %get-tuple-element.96.refs_2_.refs_1_, bf16[4,1024,256]{2,1,0:T(8,128)(2,1)} %get-tuple-element.97.refs_3_.refs_2_, bf16[1024,1024]{1,0:T(8,128)(2,1)S(1)} %copy-done.3, ...), custom_call_target="tpu_custom_call" | custom-call | flops 1000 | bytes 1000 | tf_op jit(solution)/shard_map/inflow/pallas_call | solution.py:338
  219.6 11.7 %collective-permute-done.10.refs_0_ = f32[32,4,8,256]{3,2,1,0:T(8,128)} collective-permute-done((f32[32,4,8,256]{3,2,1,0:T(8,128)}, f32[32,4,8,256]{3,2,1,0:T(8,128)}, u32[]{:S(2)}, u32[]{:S(2)}) %collective-permute-start.10) | collective-permute-done | bytes 1048608 | tf_op jit(solution)/shard_map/ppermute | solution.py:368
  231.3 10.8 %inflow.5 = f32[4,32,32,256]{3,2,1,0:T(8,128)} custom-call(f32[32,4,8,256]{3,2,1,0:T(8,128)} %collective-permute-done.10.refs_0_, bf16[4,1024,256]{2,1,0:T(8,128)(2,1)} %get-tuple-element.96.refs_2_.refs_1_, bf16[4,1024,256]{2,1,0:T(8,128)(2,1)} %get-tuple-element.97.refs_3_.refs_2_, bf16[1024,1024]{1,0:T(8,128)(2,1)S(1)} %copy-done.3, ...), custom_call_target="tpu_custom_call" | custom-call | flops 1000 | bytes 1000 | tf_op jit(solution)/shard_map/inflow/pallas_call | solution.py:338
  (70 shorter events, 18.4 us)
Async XLA Ops:
  0.6 46.8 %copy-start = (f32[1,1,128,4,8,8]{2,5,4,3,1,0:T(8,128)S(1)}, f32[1,1,128,4,8,8]{2,5,4,3,1,0:T(8,128)}, u32[]{:S(2)}) copy-start(f32[1,1,128,4,8,8]{2,5,4,3,1,0:T(8,128)} %param.25) | copy-start | bytes 393220
  0.6 22.8 %copy-start.5 = (f32[1,32,32,256]{3,2,1,0:T(8,128)S(1)}, f32[1,32,32,256]{3,2,1,0:T(8,128)}, u32[]{:S(2)}) copy-start(f32[1,32,32,256]{3,2,1,0:T(8,128)} %param.16) | copy-start | bytes 3145732
  2.5 16.2 %collective-permute-start.2 = (f32[4,32,256]{2,1,0:T(8,128)S(1)}, f32[4,32,256]{2,1,0:T(8,128)S(1)}, u32[]{:S(2)}, u32[]{:S(2)}) collective-permute-start(f32[4,32,256]{2,1,0:T(8,128)S(1)} %bitcast.52), channel_id=1, source_target_pairs={{0,1},{1,2},{2,3},{3,4},{4,5},{5,6},{6,7},{8,9},{9,10},{10,11},{11... | collective-permute-start | bytes 393224 | tf_op jit(solution)/shard_map/ppermute | solution.py:356
  6.2 12.5 %collective-permute-start.3 = (f32[4,32,256]{2,1,0:T(8,128)S(1)}, f32[4,32,256]{2,1,0:T(8,128)S(1)}, u32[]{:S(2)}, u32[]{:S(2)}) collective-permute-start(f32[4,32,256]{2,1,0:T(8,128)S(1)} %bitcast.53), channel_id=1, source_target_pairs={{1,0},{2,1},{3,2},{4,3},{5,4},{6,5},{7,6},{9,8},{10,9},{11,10},{12... | collective-permute-start | bytes 393224 | tf_op jit(solution)/shard_map/ppermute | solution.py:356
  9.1 9.6 %collective-permute-start.1 = (f32[4,32,256]{2,1,0:T(8,128)S(1)}, f32[4,32,256]{2,1,0:T(8,128)S(1)}, u32[]{:S(2)}, u32[]{:S(2)}) collective-permute-start(f32[4,32,256]{2,1,0:T(8,128)S(1)} %get-tuple-element.117), channel_id=1, source_target_pairs={{8,0},{16,8},{24,16},{32,24},{40,32},{48,40},{56,48},{9,1},{17,9},... | collective-permute-start | bytes 393224 | tf_op jit(solution)/shard_map/ppermute | solution.py:356
  15.0 7.8 %collective-permute-start = (f32[4,32,256]{2,1,0:T(8,128)S(1)}, f32[4,32,256]{2,1,0:T(8,128)S(1)}, u32[]{:S(2)}, u32[]{:S(2)}) collective-permute-start(f32[4,32,256]{2,1,0:T(8,128)S(1)} %get-tuple-element.118), channel_id=1, source_target_pairs={{0,8},{8,16},{16,24},{24,32},{32,40},{40,48},{48,56},{1,9},{9,17},... | collective-permute-start | bytes 393224 | tf_op jit(solution)/shard_map/ppermute | solution.py:356
  37.6 50.1 %collective-permute-start.9 = (f32[64,4,8,256]{3,2,1,0:T(8,128)}, f32[64,4,8,256]{3,2,1,0:T(8,128)}, u32[]{:S(2)}, u32[]{:S(2)}) collective-permute-start(f32[64,4,8,256]{3,2,1,0:T(8,128)} %get-tuple-element.94), channel_id=1, source_target_pairs={{0,96},{1,97},{2,98},{3,99},{4,100},{5,101},{6,102},{7,103},{8,104... | collective-permute-start | bytes 6291464 | tf_op jit(solution)/shard_map/ppermute | solution.py:368
  38.9 11.7 %copy-start.19 = (f32[4,32,256]{2,1,0:T(8,128)S(1)}, f32[4,32,256]{2,1,0:T(8,128)}, u32[]{:S(2)}) copy-start(f32[4,32,256]{2,1,0:T(8,128)} %get-tuple-element.88) | copy-start | bytes 393220
  38.9 15.9 %copy-start.18 = (f32[4,32,256]{2,1,0:T(8,128)S(1)}, f32[4,32,256]{2,1,0:T(8,128)}, u32[]{:S(2)}) copy-start(f32[4,32,256]{2,1,0:T(8,128)} %get-tuple-element.89) | copy-start | bytes 393220
  39.0 19.8 %copy-start.17 = (f32[4,32,256]{2,1,0:T(8,128)S(1)}, f32[4,32,256]{2,1,0:T(8,128)}, u32[]{:S(2)}) copy-start(f32[4,32,256]{2,1,0:T(8,128)} %get-tuple-element.90) | copy-start | bytes 393220
  39.0 47.5 %all-to-all-start = ((f32[64,4,8,256]{3,2,1,0:T(8,128)}), f32[64,4,8,256]{3,2,1,0:T(8,128)}, u32[]{:S(2)}, u32[]{:S(2)}) async-start(f32[64,4,8,256]{3,2,1,0:T(8,128)} %get-tuple-element.80), calls=%async_computation | async-start | bytes 4194304 | tf_op jit(solution)/shard_map/all_to_all | solution.py:372
  47.4 29.5 %collective-permute-start.5 = (f32[4,32,256]{2,1,0:T(8,128)S(1)}, f32[4,32,256]{2,1,0:T(8,128)S(1)}, u32[]{:S(2)}, u32[]{:S(2)}) collective-permute-start(f32[4,32,256]{2,1,0:T(8,128)S(1)} %copy-done.20), channel_id=1, source_target_pairs={{0,8},{8,16},{16,24},{24,32},{32,40},{40,48},{48,56},{1,9},{9,17},... | collective-permute-start | bytes 393224 | tf_op jit(solution)/shard_map/ppermute | solution.py:356
  50.6 26.4 %collective-permute-start.6 = (f32[4,32,256]{2,1,0:T(8,128)S(1)}, f32[4,32,256]{2,1,0:T(8,128)}, u32[]{:S(2)}, u32[]{:S(2)}) collective-permute-start(f32[4,32,256]{2,1,0:T(8,128)S(1)} %copy-done.19), channel_id=1, source_target_pairs={{8,0},{16,8},{24,16},{32,24},{40,32},{48,40},{56,48},{9,1},{17,9},... | collective-permute-start | bytes 393224 | tf_op jit(solution)/shard_map/ppermute | solution.py:356
  54.9 22.1 %collective-permute-start.7 = (f32[4,32,256]{2,1,0:T(8,128)S(1)}, f32[4,32,256]{2,1,0:T(8,128)}, u32[]{:S(2)}, u32[]{:S(2)}) collective-permute-start(f32[4,32,256]{2,1,0:T(8,128)S(1)} %copy-done.18), channel_id=1, source_target_pairs={{0,1},{1,2},{2,3},{3,4},{4,5},{5,6},{6,7},{8,9},{9,10},{10,11},{11... | collective-permute-start | bytes 393224 | tf_op jit(solution)/shard_map/ppermute | solution.py:356
  58.8 18.2 %collective-permute-start.8 = (f32[4,32,256]{2,1,0:T(8,128)S(1)}, f32[4,32,256]{2,1,0:T(8,128)}, u32[]{:S(2)}, u32[]{:S(2)}) collective-permute-start(f32[4,32,256]{2,1,0:T(8,128)S(1)} %copy-done.17), channel_id=1, source_target_pairs={{1,0},{2,1},{3,2},{4,3},{5,4},{6,5},{7,6},{9,8},{10,9},{11,10},{12... | collective-permute-start | bytes 393224 | tf_op jit(solution)/shard_map/ppermute | solution.py:356
  66.7 10.3 %copy-start.6 = (f32[1,32,32]{2,1,0:T(8,128)S(1)}, f32[1,32,32]{2,1,0:T(8,128)}, u32[]{:S(2)}) copy-start(f32[1,32,32]{2,1,0:T(8,128)} %param.17) | copy-start | bytes 12292
  66.7 10.3 %copy-start.7 = (f32[32,32]{1,0:T(8,128)S(1)}, f32[32,32]{1,0:T(8,128)}, u32[]{:S(2)}) copy-start(f32[32,32]{1,0:T(8,128)} %refs_11_.1) | copy-start | bytes 12292
  66.7 10.3 %copy-start.16 = (s32[1,1,128,4]{2,3,1,0:T(4,128)S(1)}, s32[1,1,128,4]{2,3,1,0:T(4,128)}, u32[]{:S(2)}) copy-start(s32[1,1,128,4]{2,3,1,0:T(4,128)} %param.24) | copy-start | bytes 6148
  86.4 51.9 %collective-permute-start.4 = (f32[64,4,8,256]{3,2,1,0:T(8,128)}, f32[64,4,8,256]{3,2,1,0:T(8,128)}, u32[]{:S(2)}, u32[]{:S(2)}) collective-permute-start(f32[64,4,8,256]{3,2,1,0:T(8,128)} %all-to-all-done), channel_id=1, source_target_pairs={{0,96},{1,97},{2,98},{3,99},{4,100},{5,101},{6,102},{7,103},{8,104... | collective-permute-start | bytes 6291464 | tf_op jit(solution)/shard_map/ppermute | solution.py:368
  124.0 14.4 %copy-start.3 = (bf16[1024,1024]{1,0:T(8,128)(2,1)S(1)}, bf16[1024,1024]{1,0:T(8,128)(2,1)}, u32[]{:S(2)}) copy-start(bf16[1024,1024]{1,0:T(8,128)(2,1)} %get-tuple-element.98.refs_4_.refs_3_) | copy-start | bytes 6291460
  124.0 34.2 %all-to-all-start.2 = ((f32[64,4,8,256]{3,2,1,0:T(8,128)}), f32[64,4,8,256]{3,2,1,0:T(8,128)}, u32[]{:S(2)}, u32[]{:S(2)}) async-start(f32[64,4,8,256]{3,2,1,0:T(8,128)} %get-tuple-element.101), calls=%async_computation.2 | async-start | bytes 4194304 | tf_op jit(solution)/shard_map/all_to_all | solution.py:372
  131.0 63.0 %collective-permute-start.12 = (f32[64,4,8,256]{3,2,1,0:T(8,128)}, f32[64,4,8,256]{3,2,1,0:T(8,128)}, u32[]{:S(2)}, u32[]{:S(2)}) collective-permute-start(f32[64,4,8,256]{3,2,1,0:T(8,128)} %all_to_all.15.refs_1_), channel_id=1, source_target_pairs={{0,96},{1,97},{2,98},{3,99},{4,100},{5,101},{6,102},{7,103},{8,104... | collective-permute-start | bytes 6291464 | tf_op jit(solution)/shard_map/ppermute | solution.py:368
  158.1 26.2 %copy-start.2 = (f32[1,4,32,32,256]{4,3,2,1,0:T(8,128)S(1)}, f32[1,4,32,32,256]{4,3,2,1,0:T(8,128)}, u32[]{:S(2)}) copy-start(f32[1,4,32,32,256]{4,3,2,1,0:T(8,128)} %param.15) | copy-start | bytes 12582916
  161.4 47.4 %collective-permute-start.11 = (f32[32,4,8,256]{3,2,1,0:T(8,128)}, f32[32,4,8,256]{3,2,1,0:T(8,128)}, u32[]{:S(2)}, u32[]{:S(2)}) collective-permute-start(f32[32,4,8,256]{3,2,1,0:T(8,128)} %get-tuple-element.119), channel_id=1, source_target_pairs={{0,96},{1,97},{2,98},{3,99},{4,100},{5,101},{6,102},{7,103},{8,104... | collective-permute-start | bytes 3145736 | tf_op jit(solution)/shard_map/ppermute | solution.py:368
  162.7 68.6 %collective-permute-start.10 = (f32[32,4,8,256]{3,2,1,0:T(8,128)}, f32[32,4,8,256]{3,2,1,0:T(8,128)}, u32[]{:S(2)}, u32[]{:S(2)}) collective-permute-start(f32[32,4,8,256]{3,2,1,0:T(8,128)} %get-tuple-element.120), channel_id=1, source_target_pairs={{0,96},{1,97},{2,98},{3,99},{4,100},{5,101},{6,102},{7,103},{8,104... | collective-permute-start | bytes 3145736 | tf_op jit(solution)/shard_map/ppermute | solution.py:368
  164.0 8.0 %collective-permute-start.13 = (f32[4,32,256]{2,1,0:T(8,128)}, f32[4,32,256]{2,1,0:T(8,128)S(1)}, u32[]{:S(2)}, u32[]{:S(2)}) collective-permute-start(f32[4,32,256]{2,1,0:T(8,128)} %get-tuple-element.107), channel_id=1, source_target_pairs={{0,8},{8,16},{16,24},{24,32},{32,40},{40,48},{48,56},{1,9},{9,17},... | collective-permute-start | bytes 393224 | tf_op jit(solution)/shard_map/ppermute | solution.py:356
  167.0 9.7 %collective-permute-start.14 = (f32[4,32,256]{2,1,0:T(8,128)}, f32[4,32,256]{2,1,0:T(8,128)S(1)}, u32[]{:S(2)}, u32[]{:S(2)}) collective-permute-start(f32[4,32,256]{2,1,0:T(8,128)} %get-tuple-element.108), channel_id=1, source_target_pairs={{8,0},{16,8},{24,16},{32,24},{40,32},{48,40},{56,48},{9,1},{17,9},... | collective-permute-start | bytes 393224 | tf_op jit(solution)/shard_map/ppermute | solution.py:356
  172.0 11.7 %copy-start.12 = (f32[4,32,256]{2,1,0:T(8,128)}, f32[4,32,256]{2,1,0:T(8,128)S(1)}, u32[]{:S(2)}) copy-start(f32[4,32,256]{2,1,0:T(8,128)S(1)} %collective-permute-done.13.refs_4_) | copy-start | bytes 393220
  172.0 7.0 %collective-permute-start.15 = (f32[4,32,256]{2,1,0:T(8,128)}, f32[4,32,256]{2,1,0:T(8,128)S(1)}, u32[]{:S(2)}, u32[]{:S(2)}) collective-permute-start(f32[4,32,256]{2,1,0:T(8,128)} %get-tuple-element.109), channel_id=1, source_target_pairs={{0,1},{1,2},{2,3},{3,4},{4,5},{5,6},{6,7},{8,9},{9,10},{10,11},{11... | collective-permute-start | bytes 393224 | tf_op jit(solution)/shard_map/ppermute | solution.py:356
  176.8 6.9 %collective-permute-start.16 = (f32[4,32,256]{2,1,0:T(8,128)}, f32[4,32,256]{2,1,0:T(8,128)S(1)}, u32[]{:S(2)}, u32[]{:S(2)}) collective-permute-start(f32[4,32,256]{2,1,0:T(8,128)} %get-tuple-element.110), channel_id=1, source_target_pairs={{1,0},{2,1},{3,2},{4,3},{5,4},{6,5},{7,6},{9,8},{10,9},{11,10},{12... | collective-permute-start | bytes 393224 | tf_op jit(solution)/shard_map/ppermute | solution.py:356
  194.1 14.7 %copy-start.4 = (bf16[1024,1024]{1,0:T(8,128)(2,1)S(1)}, bf16[1024,1024]{1,0:T(8,128)(2,1)}, u32[]{:S(2)}) copy-start(bf16[1024,1024]{1,0:T(8,128)(2,1)} %get-tuple-element.99.refs_5_.refs_4_) | copy-start | bytes 6291460
  231.3 10.8 %copy-start.1 = (f32[1,1,128,4,8,8]{2,5,4,3,1,0:T(8,128)S(1)}, f32[1,1,128,4,8,8]{2,5,4,3,1,0:T(8,128)}, u32[]{:S(2)}) copy-start(f32[1,1,128,4,8,8]{2,5,4,3,1,0:T(8,128)} %param.25) | copy-start | bytes 393220
  (8 other events, 33.6 us)

commit v8 on v7

--- a/solution.py
+++ b/solution.py
@@ -416,10 +416,10 @@
 
     late_map, late_weights, own_1 = lax.optimization_barrier((frame_map, interp_weights[0, 0], own_1))
     frame, tiles = frame_terms(late_map), jnp.tile(late_weights, (1, 1, 1, 128 // BLK))
-    own_1, frame, tiles = lax.optimization_barrier((own_1, frame, tiles))
+    own_1, frame, tiles, relayed_1 = lax.optimization_barrier((own_1, frame, tiles, relayed_1))
+    crossed_zero_1 = cross(relayed_1)
     picks = pick_slots[0, 0].T.reshape(MSLOT * NBLK)
     one_2, zero_2, blend = lax.cond(section == 0, reactant, product, own_1, halo, weights, picks, tiles)
-    crossed_zero_1 = cross(relayed_1)
     shared = spread(jnp.where(section == 0, zero_2, crossed_one_1))
     crossed_zero_2 = cross(shared)
     one_2, shared = lax.optimization_barrier((one_2, shared))

time: 244 us -> 244 us (level)
  blocking collectives: 34.2 us -> 37.1 us
  waiting for transfers between devices: 39 us -> 36.1 us
    all_to_all x2, waiting for transfers between devices: 0.24 us -> 12.6 us  [spread(): lax.all_to_all(x, ('rr', 'sr'), split_axis=0, concat_axis=0, tiled=True)]
    ppermute x5, waiting for transfers between devices: 20.3 us -> 11.4 us  [cross(): return lax.ppermute(x, ALL, pairs)]
    ppermute x12, waiting for transfers between devices: 18.5 us -> 12 us  [send(): return lax.ppermute(piece, axis, pairs)]
    all_to_all x1, blocking collectives: 34.2 us -> 37.1 us  [spread(): lax.all_to_all(x, ('rr', 'sr'), split_axis=0, concat_axis=0, tiled=True)]
  transfers between devices with their start and end apart: 19 -> 19, of which waited for: 9 -> 8; matrix products, arithmetic and copies ran while one was open for 7% -> 7% of each run, Pallas kernels for 24% -> 24%
where the time goes in v8:
time: 244 us; the launch traced here: 242 us
  Pallas kernels  84 us (34%)
  starting transfers between devices  62.6 us (26%)
  blocking collectives  37.1 us (15%)
  waiting for transfers between devices  36.1 us (15%)
  local copies, waits for them, and re-layouts  15.4 us (6%)
  other arithmetic  4.92 us (2%)
    pallas_call x4, Pallas kernels, inflow_call(): pl.pallas_call(functools.partial(inflow_kernel, len(xs), want_edges), gri...  53.1 us
    ppermute x12, starting transfers between devices, send(): return lax.ppermute(piece, axis, pairs)  40.5 us
    all_to_all x1, blocking collectives, spread(): lax.all_to_all(x, ('rr', 'sr'), split_axis=0, concat_axis=0, tiled=True)  37.1 us
    pallas_call x2, Pallas kernels, step_call(): pl.pallas_call(functools.partial(step_kernel, first_step, want_own, want_...  23.9 us
    all_to_all x2, starting transfers between devices, spread(): lax.all_to_all(x, ('rr', 'sr'), split_axis=0, concat_axis=0, tiled=True)  15.5 us
    all_to_all x2, waiting for transfers between devices, spread(): lax.all_to_all(x, ('rr', 'sr'), split_axis=0, concat_axis=0, tiled=True)  12.6 us
    ppermute x12, waiting for transfers between devices, send(): return lax.ppermute(piece, axis, pairs)  12 us
    ppermute x5, waiting for transfers between devices, cross(): return lax.ppermute(x, ALL, pairs)  11.4 us
  transfers between devices with their start and end apart: 19, of which 8 were waited for; matrix products, arithmetic and copies ran while one was open for 7% of the time, Pallas kernels for 24%

profile of v8, /device:TPU:27, one launch (start us, length us, event | category | flops | bytes accessed | tf_op | source)
XLA Modules:
  0.0 241.9 jit_solution(5987886883505720338)
XLA Ops:
  2.5 3.7 %collective-permute-start.2 = (f32[4,32,256]{2,1,0:T(8,128)S(1)}, f32[4,32,256]{2,1,0:T(8,128)S(1)}, u32[]{:S(2)}, u32[]{:S(2)}) collective-permute-start(f32[4,32,256]{2,1,0:T(8,128)S(1)} %bitcast.52), channel_id=1, source_target_pairs={{0,1},{1,2},{2,3},{3,4},{4,5},{5,6},{6,7},{8,9},{9,10},{10,11},{11... | collective-permute-start | bytes 393224 | tf_op jit(solution)/shard_map/ppermute | solution.py:356
  6.2 1.9 collective-permute-start.3
  9.1 5.8 %collective-permute-start.1 = (f32[4,32,256]{2,1,0:T(8,128)S(1)}, f32[4,32,256]{2,1,0:T(8,128)S(1)}, u32[]{:S(2)}, u32[]{:S(2)}) collective-permute-start(f32[4,32,256]{2,1,0:T(8,128)S(1)} %get-tuple-element.119), channel_id=1, source_target_pairs={{8,0},{16,8},{24,16},{32,24},{40,32},{48,40},{56,48},{9,1},{17,9},... | collective-permute-start | bytes 393224 | tf_op jit(solution)/shard_map/ppermute | solution.py:356
  15.0 1.9 collective-permute-start
  18.8 4.0 %collective-permute-done.refs_5_ = f32[4,32,256]{2,1,0:T(8,128)S(1)} collective-permute-done((f32[4,32,256]{2,1,0:T(8,128)S(1)}, f32[4,32,256]{2,1,0:T(8,128)S(1)}, u32[]{:S(2)}, u32[]{:S(2)}) %collective-permute-start) | collective-permute-done | bytes 131104 | tf_op jit(solution)/shard_map/ppermute | solution.py:356
  23.5 14.1 %step_first.1 = (f32[4,32,32,256]{3,2,1,0:T(8,128)}, f32[64,4,8,256]{3,2,1,0:T(8,128)}, f32[64,4,8,256]{3,2,1,0:T(8,128)}, f32[4,32,256]{2,1,0:T(8,128)}, f32[4,...) custom-call(s32[128]{0:T(128)S(1)} %reshape.18.refs_0_, ...), custom_call_target="tpu_custom_call" | custom-call | flops 1000 | bytes 1000 | tf_op jit(solution)/shard_map/step_first/pallas_call | solution.py:259
  39.0 8.4 %all-to-all-start = ((f32[64,4,8,256]{3,2,1,0:T(8,128)}), f32[64,4,8,256]{3,2,1,0:T(8,128)}, u32[]{:S(2)}, u32[]{:S(2)}) async-start(f32[64,4,8,256]{3,2,1,0:T(8,128)} %get-tuple-element.85), calls=%async_computation | async-start | bytes 4194304 | tf_op jit(solution)/shard_map/all_to_all | solution.py:372
  47.4 3.1 %collective-permute-start.5 = (f32[4,32,256]{2,1,0:T(8,128)S(1)}, f32[4,32,256]{2,1,0:T(8,128)S(1)}, u32[]{:S(2)}, u32[]{:S(2)}) collective-permute-start(f32[4,32,256]{2,1,0:T(8,128)S(1)} %copy-done.20), channel_id=1, source_target_pairs={{0,8},{8,16},{16,24},{24,32},{32,40},{40,48},{48,56},{1,9},{9,17},... | collective-permute-start | bytes 393224 | tf_op jit(solution)/shard_map/ppermute | solution.py:356
  50.6 4.2 %collective-permute-start.6 = (f32[4,32,256]{2,1,0:T(8,128)S(1)}, f32[4,32,256]{2,1,0:T(8,128)S(1)}, u32[]{:S(2)}, u32[]{:S(2)}) collective-permute-start(f32[4,32,256]{2,1,0:T(8,128)S(1)} %copy-done.19), channel_id=1, source_target_pairs={{8,0},{16,8},{24,16},{32,24},{40,32},{48,40},{56,48},{9,1},{17,9},... | collective-permute-start | bytes 393224 | tf_op jit(solution)/shard_map/ppermute | solution.py:356
  54.9 3.9 %collective-permute-start.7 = (f32[4,32,256]{2,1,0:T(8,128)S(1)}, f32[4,32,256]{2,1,0:T(8,128)S(1)}, u32[]{:S(2)}, u32[]{:S(2)}) collective-permute-start(f32[4,32,256]{2,1,0:T(8,128)S(1)} %copy-done.18), channel_id=1, source_target_pairs={{0,1},{1,2},{2,3},{3,4},{4,5},{5,6},{6,7},{8,9},{9,10},{10,11},{11... | collective-permute-start | bytes 393224 | tf_op jit(solution)/shard_map/ppermute | solution.py:356
  58.8 1.9 collective-permute-start.8
  60.7 3.0 %copy.18 = f32[4,4,256,256]{3,2,1,0:T(8,128)S(1)} copy(f32[4,4,256,256]{3,0,2,1:T(4,128)} %bitcast.46) | data formatting | bytes 8388608 | tf_op jit(solution)/shard_map/transpose | solution.py:51
  63.7 2.9 %fusion = (bf16[4,1024,256]{2,1,0:T(8,128)(2,1)}, bf16[4,1024,256]{2,1,0:T(8,128)(2,1)}) fusion(f32[4,4,256,256]{3,2,1,0:T(8,128)S(1)} %copy.18), kind=kLoop, calls=%fused_computation.2 | loop fusion | flops 4194304 | bytes 8388608 | tf_op jit(solution)/shard_map/convert_element_type | solution.py:53
  68.1 6.5 %all-to-all-done = f32[64,4,8,256]{3,2,1,0:T(8,128)} async-done(((f32[64,4,8,256]{3,2,1,0:T(8,128)}), f32[64,4,8,256]{3,2,1,0:T(8,128)}, u32[]{:S(2)}, u32[]{:S(2)}) %all-to-all-start) | async-done | bytes 2097184 | tf_op jit(solution)/shard_map/all_to_all | solution.py:372
  74.6 2.4 collective-permute-done.5
  78.3 9.4 %conditional.1 = ((f32[64,4,8,256]{3,2,1,0:T(8,128)}, f32[64,4,8,256]{3,2,1,0:T(8,128)}, bf16[1024,1024]{1,0:T(8,128)(2,1)}, bf16[1024,1024]{1,0:T(8,128)(2,1)})) conditional(s32[]{:T(128)} %convert_element_type.11, (s32[4,128]{1,0:T(4,128)S(1)}, f32[128,4,8,128]{0,3,2,1:T(8,128)}) %tuple.39, (s32[128]{0:T(128)S(1)}, s32[1]{0:T(128)}, ...), branch_computations={%region_0.1_spmd, %region_1.2_spmd} | conditional | flops 8388608 | bytes 10485800 | solution.py:422
  78.3 2.4 copy.19.tile_ref
  80.7 7.0 %blend_matrix.1 = (bf16[1024,1024]{1,0:T(8,128)(2,1)}, bf16[1024,1024]{1,0:T(8,128)(2,1)}, f32[64,4,8,256]{3,2,1,0:T(8,128)}, f32[64,4,8,256]{3,2,1,0:T(8,128)}) custom-call(s32[512]{0:T(512)S(1)} %bitcast.55, f32[128,4,8,128]{3,2,1,0:T(8,128)S(1)} %copy.19.tile_ref), custom_call_target="tpu_custom_call" | custom-call | flops 8388608 | bytes 6291456 | tf_op jit(solution)/shard_map/cond/branch_0_fun/blend_matrix/pallas_call | solution.py:86
  87.7 2.0 broadcast_select_fusion
  89.8 37.1 %all_to_all.15.refs_1_ = f32[64,4,8,256]{3,2,1,0:T(8,128)} all-to-all(f32[64,4,8,256]{3,2,1,0:T(8,128)S(1)} %broadcast_select_fusion), channel_id=1, replica_groups=mesh['sec'=2,'rr'=8,'sr'=8] {'rr','sr'}, dimensions={0} | all-to-all | bytes 4194304 | tf_op jit(solution)/shard_map/all_to_all | solution.py:372
  126.9 7.0 %all-to-all-start.2 = ((f32[64,4,8,256]{3,2,1,0:T(8,128)}), f32[64,4,8,256]{3,2,1,0:T(8,128)}, u32[]{:S(2)}, u32[]{:S(2)}) async-start(f32[64,4,8,256]{3,2,1,0:T(8,128)} %get-tuple-element.103), calls=%async_computation.2 | async-start | bytes 4194304 | tf_op jit(solution)/shard_map/all_to_all | solution.py:372
  135.4 19.5 %inflow_edges.1 = (f32[4,32,32,256]{3,2,1,0:T(8,128)}, f32[4,32,256]{2,1,0:T(8,128)}, f32[4,32,256]{2,1,0:T(8,128)}, f32[4,32,256]{2,1,0:T(8,128)}, f32[4,32,256]{2,1,0:T(8,128)}) custom-call(f32[64,4,8,256]{3,2,1,0:T(8,128)} %collective-permute-done.4.refs_0_, f32[64,4,8,256]{3,2,1,0:T(8,128)} %all_to_all.15.refs_1_, ...), custom_call_target="tpu_custom_call" | custom-call | flops 42949672960 | bytes 1000 | tf_op jit(solution)/shard_map/inflow_edges/pallas_call | solution.py:338
  154.9 6.1 %all-to-all-done.2 = f32[64,4,8,256]{3,2,1,0:T(8,128)} async-done(((f32[64,4,8,256]{3,2,1,0:T(8,128)}), f32[64,4,8,256]{3,2,1,0:T(8,128)}, u32[]{:S(2)}, u32[]{:S(2)}) %all-to-all-start.2) | async-done | bytes 2097184 | tf_op jit(solution)/shard_map/all_to_all | solution.py:372
  161.0 3.3 %fusion.2 = (f32[32,4,8,256]{3,2,1,0:T(8,128)}, f32[32,4,8,256]{3,2,1,0:T(8,128)}) fusion(f32[64,4,8,256]{3,2,1,0:T(8,128)} %all-to-all-done.2), kind=kLoop, calls=%fused_computation.11 | loop fusion | bytes 4194304 | tf_op jit(solution)/shard_map/slice | solution.py:430
  168.8 5.5 %collective-permute-start.14 = (f32[4,32,256]{2,1,0:T(8,128)}, f32[4,32,256]{2,1,0:T(8,128)S(1)}, u32[]{:S(2)}, u32[]{:S(2)}) collective-permute-start(f32[4,32,256]{2,1,0:T(8,128)} %get-tuple-element.110), channel_id=1, source_target_pairs={{8,0},{16,8},{24,16},{32,24},{40,32},{48,40},{56,48},{9,1},{17,9},... | collective-permute-start | bytes 393224 | tf_op jit(solution)/shard_map/ppermute | solution.py:356
  174.9 4.6 %collective-permute-start.15 = (f32[4,32,256]{2,1,0:T(8,128)}, f32[4,32,256]{2,1,0:T(8,128)S(1)}, u32[]{:S(2)}, u32[]{:S(2)}) collective-permute-start(f32[4,32,256]{2,1,0:T(8,128)} %get-tuple-element.111), channel_id=1, source_target_pairs={{0,1},{1,2},{2,3},{3,4},{4,5},{5,6},{6,7},{8,9},{9,10},{10,11},{11... | collective-permute-start | bytes 393224 | tf_op jit(solution)/shard_map/ppermute | solution.py:356
  181.7 4.7 %collective-permute-done.16.refs_7_ = f32[4,32,256]{2,1,0:T(8,128)S(1)} collective-permute-done((f32[4,32,256]{2,1,0:T(8,128)}, f32[4,32,256]{2,1,0:T(8,128)S(1)}, u32[]{:S(2)}, u32[]{:S(2)}) %collective-permute-start.16) | collective-permute-done | bytes 131104 | tf_op jit(solution)/shard_map/ppermute | solution.py:356
  187.1 9.7 %step_own.1.refs_5_ = f32[4,32,32,256]{3,2,1,0:T(8,128)} custom-call(s32[1]{0:T(128)S(6)} %copy.34.refs_1_.refs_0_, f32[4,32,32,256]{3,2,1,0:T(8,128)} %get-tuple-element.102.refs_1_.refs_2_.refs_3_, f32[4,32,32,256]{3,2,1,0:T(8,128)} %get-tuple-element.102.refs_1_.refs_2_.refs_3_, f32[4,32,32,256]{3,2,1,0:T(8,128)} %get-tuple-element.102.refs_1_.refs_2_.refs_3_, ...), custom_call_target="tpu_custom_call" | custom-call | flops 1000 | bytes 1000 | tf_op jit(solution)/shard_map/step_own/pallas_call | solution.py:259
  196.8 12.0 %inflow.3.refs_5_ = f32[4,32,32,256]{3,2,1,0:T(8,128)} custom-call(f32[64,4,8,256]{3,2,1,0:T(8,128)} %collective-permute-done.12.refs_0_, bf16[4,1024,256]{2,1,0:T(8,128)(2,1)} %get-tuple-element.98.refs_2_.refs_1_, bf16[4,1024,256]{2,1,0:T(8,128)(2,1)} %get-tuple-element.99.refs_3_.refs_2_, bf16[1024,1024]{1,0:T(8,128)(2,1)S(1)} %copy-done.3, ...), custom_call_target="tpu_custom_call" | custom-call | flops 1000 | bytes 1000 | tf_op jit(solution)/shard_map/inflow/pallas_call | solution.py:338
  208.8 10.8 %inflow.4.refs_5_ = f32[4,32,32,256]{3,2,1,0:T(8,128)} custom-call(f32[32,4,8,256]{3,2,1,0:T(8,128)} %collective-permute-done.11.refs_0_, bf16[4,1024,256]{2,1,0:T(8,128)(2,1)} %get-tuple-element.98.refs_2_.refs_1_, bf16[4,1024,256]{2,1,0:T(8,128)(2,1)} %get-tuple-element.99.refs_3_.refs_2_, bf16[1024,1024]{1,0:T(8,128)(2,1)S(1)} %copy-done.3, ...), custom_call_target="tpu_custom_call" | custom-call | flops 1000 | bytes 1000 | tf_op jit(solution)/shard_map/inflow/pallas_call | solution.py:338
  219.6 11.4 %collective-permute-done.10.refs_0_ = f32[32,4,8,256]{3,2,1,0:T(8,128)} collective-permute-done((f32[32,4,8,256]{3,2,1,0:T(8,128)}, f32[32,4,8,256]{3,2,1,0:T(8,128)}, u32[]{:S(2)}, u32[]{:S(2)}) %collective-permute-start.10) | collective-permute-done | bytes 1048608 | tf_op jit(solution)/shard_map/ppermute | solution.py:368
  231.1 10.8 %inflow.5 = f32[4,32,32,256]{3,2,1,0:T(8,128)} custom-call(f32[32,4,8,256]{3,2,1,0:T(8,128)} %collective-permute-done.10.refs_0_, bf16[4,1024,256]{2,1,0:T(8,128)(2,1)} %get-tuple-element.98.refs_2_.refs_1_, bf16[4,1024,256]{2,1,0:T(8,128)(2,1)} %get-tuple-element.99.refs_3_.refs_2_, bf16[1024,1024]{1,0:T(8,128)(2,1)S(1)} %copy-done.3, ...), custom_call_target="tpu_custom_call" | custom-call | flops 1000 | bytes 1000 | tf_op jit(solution)/shard_map/inflow/pallas_call | solution.py:338
  (70 shorter events, 18.2 us)
Async XLA Ops:
  0.6 46.8 %copy-start = (f32[1,1,128,4,8,8]{2,5,4,3,1,0:T(8,128)S(1)}, f32[1,1,128,4,8,8]{2,5,4,3,1,0:T(8,128)}, u32[]{:S(2)}) copy-start(f32[1,1,128,4,8,8]{2,5,4,3,1,0:T(8,128)} %param.25) | copy-start | bytes 393220
  0.6 22.8 %copy-start.5 = (f32[1,32,32,256]{3,2,1,0:T(8,128)S(1)}, f32[1,32,32,256]{3,2,1,0:T(8,128)}, u32[]{:S(2)}) copy-start(f32[1,32,32,256]{3,2,1,0:T(8,128)} %param.16) | copy-start | bytes 3145732
  2.5 16.2 %collective-permute-start.2 = (f32[4,32,256]{2,1,0:T(8,128)S(1)}, f32[4,32,256]{2,1,0:T(8,128)S(1)}, u32[]{:S(2)}, u32[]{:S(2)}) collective-permute-start(f32[4,32,256]{2,1,0:T(8,128)S(1)} %bitcast.52), channel_id=1, source_target_pairs={{0,1},{1,2},{2,3},{3,4},{4,5},{5,6},{6,7},{8,9},{9,10},{10,11},{11... | collective-permute-start | bytes 393224 | tf_op jit(solution)/shard_map/ppermute | solution.py:356
  6.2 12.5 %collective-permute-start.3 = (f32[4,32,256]{2,1,0:T(8,128)S(1)}, f32[4,32,256]{2,1,0:T(8,128)S(1)}, u32[]{:S(2)}, u32[]{:S(2)}) collective-permute-start(f32[4,32,256]{2,1,0:T(8,128)S(1)} %bitcast.53), channel_id=1, source_target_pairs={{1,0},{2,1},{3,2},{4,3},{5,4},{6,5},{7,6},{9,8},{10,9},{11,10},{12... | collective-permute-start | bytes 393224 | tf_op jit(solution)/shard_map/ppermute | solution.py:356
  9.1 9.6 %collective-permute-start.1 = (f32[4,32,256]{2,1,0:T(8,128)S(1)}, f32[4,32,256]{2,1,0:T(8,128)S(1)}, u32[]{:S(2)}, u32[]{:S(2)}) collective-permute-start(f32[4,32,256]{2,1,0:T(8,128)S(1)} %get-tuple-element.119), channel_id=1, source_target_pairs={{8,0},{16,8},{24,16},{32,24},{40,32},{48,40},{56,48},{9,1},{17,9},... | collective-permute-start | bytes 393224 | tf_op jit(solution)/shard_map/ppermute | solution.py:356
  15.0 7.8 %collective-permute-start = (f32[4,32,256]{2,1,0:T(8,128)S(1)}, f32[4,32,256]{2,1,0:T(8,128)S(1)}, u32[]{:S(2)}, u32[]{:S(2)}) collective-permute-start(f32[4,32,256]{2,1,0:T(8,128)S(1)} %get-tuple-element.120), channel_id=1, source_target_pairs={{0,8},{8,16},{16,24},{24,32},{32,40},{40,48},{48,56},{1,9},{9,17},... | collective-permute-start | bytes 393224 | tf_op jit(solution)/shard_map/ppermute | solution.py:356
  37.6 50.1 %collective-permute-start.9 = (f32[64,4,8,256]{3,2,1,0:T(8,128)}, f32[64,4,8,256]{3,2,1,0:T(8,128)}, u32[]{:S(2)}, u32[]{:S(2)}) collective-permute-start(f32[64,4,8,256]{3,2,1,0:T(8,128)} %get-tuple-element.96), channel_id=1, source_target_pairs={{0,96},{1,97},{2,98},{3,99},{4,100},{5,101},{6,102},{7,103},{8,104... | collective-permute-start | bytes 6291464 | tf_op jit(solution)/shard_map/ppermute | solution.py:368
  38.9 11.7 %copy-start.19 = (f32[4,32,256]{2,1,0:T(8,128)S(1)}, f32[4,32,256]{2,1,0:T(8,128)}, u32[]{:S(2)}) copy-start(f32[4,32,256]{2,1,0:T(8,128)} %get-tuple-element.90) | copy-start | bytes 393220
  38.9 15.9 %copy-start.18 = (f32[4,32,256]{2,1,0:T(8,128)S(1)}, f32[4,32,256]{2,1,0:T(8,128)}, u32[]{:S(2)}) copy-start(f32[4,32,256]{2,1,0:T(8,128)} %get-tuple-element.91) | copy-start | bytes 393220
  38.9 19.8 %copy-start.17 = (f32[4,32,256]{2,1,0:T(8,128)S(1)}, f32[4,32,256]{2,1,0:T(8,128)}, u32[]{:S(2)}) copy-start(f32[4,32,256]{2,1,0:T(8,128)} %get-tuple-element.92) | copy-start | bytes 393220
  39.0 35.6 %all-to-all-start = ((f32[64,4,8,256]{3,2,1,0:T(8,128)}), f32[64,4,8,256]{3,2,1,0:T(8,128)}, u32[]{:S(2)}, u32[]{:S(2)}) async-start(f32[64,4,8,256]{3,2,1,0:T(8,128)} %get-tuple-element.85), calls=%async_computation | async-start | bytes 4194304 | tf_op jit(solution)/shard_map/all_to_all | solution.py:372
  47.4 29.5 %collective-permute-start.5 = (f32[4,32,256]{2,1,0:T(8,128)S(1)}, f32[4,32,256]{2,1,0:T(8,128)S(1)}, u32[]{:S(2)}, u32[]{:S(2)}) collective-permute-start(f32[4,32,256]{2,1,0:T(8,128)S(1)} %copy-done.20), channel_id=1, source_target_pairs={{0,8},{8,16},{16,24},{24,32},{32,40},{40,48},{48,56},{1,9},{9,17},... | collective-permute-start | bytes 393224 | tf_op jit(solution)/shard_map/ppermute | solution.py:356
  50.6 27.7 %collective-permute-start.6 = (f32[4,32,256]{2,1,0:T(8,128)S(1)}, f32[4,32,256]{2,1,0:T(8,128)S(1)}, u32[]{:S(2)}, u32[]{:S(2)}) collective-permute-start(f32[4,32,256]{2,1,0:T(8,128)S(1)} %copy-done.19), channel_id=1, source_target_pairs={{8,0},{16,8},{24,16},{32,24},{40,32},{48,40},{56,48},{9,1},{17,9},... | collective-permute-start | bytes 393224 | tf_op jit(solution)/shard_map/ppermute | solution.py:356
  54.9 23.4 %collective-permute-start.7 = (f32[4,32,256]{2,1,0:T(8,128)S(1)}, f32[4,32,256]{2,1,0:T(8,128)S(1)}, u32[]{:S(2)}, u32[]{:S(2)}) collective-permute-start(f32[4,32,256]{2,1,0:T(8,128)S(1)} %copy-done.18), channel_id=1, source_target_pairs={{0,1},{1,2},{2,3},{3,4},{4,5},{5,6},{6,7},{8,9},{9,10},{10,11},{11... | collective-permute-start | bytes 393224 | tf_op jit(solution)/shard_map/ppermute | solution.py:356
  58.8 19.5 %collective-permute-start.8 = (f32[4,32,256]{2,1,0:T(8,128)S(1)}, f32[4,32,256]{2,1,0:T(8,128)S(1)}, u32[]{:S(2)}, u32[]{:S(2)}) collective-permute-start(f32[4,32,256]{2,1,0:T(8,128)S(1)} %copy-done.17), channel_id=1, source_target_pairs={{1,0},{2,1},{3,2},{4,3},{5,4},{6,5},{7,6},{9,8},{10,9},{11,10},{12... | collective-permute-start | bytes 393224 | tf_op jit(solution)/shard_map/ppermute | solution.py:356
  66.6 11.7 %copy-start.6 = (f32[1,32,32]{2,1,0:T(8,128)S(1)}, f32[1,32,32]{2,1,0:T(8,128)}, u32[]{:S(2)}) copy-start(f32[1,32,32]{2,1,0:T(8,128)} %param.17) | copy-start | bytes 12292
  66.6 11.7 %copy-start.7 = (f32[32,32]{1,0:T(8,128)S(1)}, f32[32,32]{1,0:T(8,128)}, u32[]{:S(2)}) copy-start(f32[32,32]{1,0:T(8,128)} %refs_11_.1) | copy-start | bytes 12292
  66.6 11.7 %copy-start.16 = (s32[1,1,128,4]{2,3,1,0:T(4,128)S(1)}, s32[1,1,128,4]{2,3,1,0:T(4,128)}, u32[]{:S(2)}) copy-start(s32[1,1,128,4]{2,3,1,0:T(4,128)} %param.24) | copy-start | bytes 6148
  77.0 58.4 %collective-permute-start.4 = (f32[64,4,8,256]{3,2,1,0:T(8,128)}, f32[64,4,8,256]{3,2,1,0:T(8,128)}, u32[]{:S(2)}, u32[]{:S(2)}) collective-permute-start(f32[64,4,8,256]{3,2,1,0:T(8,128)} %all-to-all-done), channel_id=1, source_target_pairs={{0,96},{1,97},{2,98},{3,99},{4,100},{5,101},{6,102},{7,103},{8,104... | collective-permute-start | bytes 6291464 | tf_op jit(solution)/shard_map/ppermute | solution.py:368
  126.9 8.5 %copy-start.3 = (bf16[1024,1024]{1,0:T(8,128)(2,1)S(1)}, bf16[1024,1024]{1,0:T(8,128)(2,1)}, u32[]{:S(2)}) copy-start(bf16[1024,1024]{1,0:T(8,128)(2,1)} %get-tuple-element.100.refs_4_.refs_3_) | copy-start | bytes 6291460
  126.9 34.2 %all-to-all-start.2 = ((f32[64,4,8,256]{3,2,1,0:T(8,128)}), f32[64,4,8,256]{3,2,1,0:T(8,128)}, u32[]{:S(2)}, u32[]{:S(2)}) async-start(f32[64,4,8,256]{3,2,1,0:T(8,128)} %get-tuple-element.103), calls=%async_computation.2 | async-start | bytes 4194304 | tf_op jit(solution)/shard_map/all_to_all | solution.py:372
  133.9 62.9 %collective-permute-start.12 = (f32[64,4,8,256]{3,2,1,0:T(8,128)}, f32[64,4,8,256]{3,2,1,0:T(8,128)}, u32[]{:S(2)}, u32[]{:S(2)}) collective-permute-start(f32[64,4,8,256]{3,2,1,0:T(8,128)} %all_to_all.15.refs_1_), channel_id=1, source_target_pairs={{0,96},{1,97},{2,98},{3,99},{4,100},{5,101},{6,102},{7,103},{8,104... | collective-permute-start | bytes 6291464 | tf_op jit(solution)/shard_map/ppermute | solution.py:368
  161.0 26.0 %copy-start.2 = (f32[1,4,32,32,256]{4,3,2,1,0:T(8,128)S(1)}, f32[1,4,32,32,256]{4,3,2,1,0:T(8,128)}, u32[]{:S(2)}) copy-start(f32[1,4,32,32,256]{4,3,2,1,0:T(8,128)} %param.15) | copy-start | bytes 12582916
  164.3 44.5 %collective-permute-start.11 = (f32[32,4,8,256]{3,2,1,0:T(8,128)}, f32[32,4,8,256]{3,2,1,0:T(8,128)}, u32[]{:S(2)}, u32[]{:S(2)}) collective-permute-start(f32[32,4,8,256]{3,2,1,0:T(8,128)} %get-tuple-element.121), channel_id=1, source_target_pairs={{0,96},{1,97},{2,98},{3,99},{4,100},{5,101},{6,102},{7,103},{8,104... | collective-permute-start | bytes 3145736 | tf_op jit(solution)/shard_map/ppermute | solution.py:368
  165.6 65.5 %collective-permute-start.10 = (f32[32,4,8,256]{3,2,1,0:T(8,128)}, f32[32,4,8,256]{3,2,1,0:T(8,128)}, u32[]{:S(2)}, u32[]{:S(2)}) collective-permute-start(f32[32,4,8,256]{3,2,1,0:T(8,128)} %get-tuple-element.122), channel_id=1, source_target_pairs={{0,96},{1,97},{2,98},{3,99},{4,100},{5,101},{6,102},{7,103},{8,104... | collective-permute-start | bytes 3145736 | tf_op jit(solution)/shard_map/ppermute | solution.py:368
  166.9 8.0 %collective-permute-start.13 = (f32[4,32,256]{2,1,0:T(8,128)}, f32[4,32,256]{2,1,0:T(8,128)S(1)}, u32[]{:S(2)}, u32[]{:S(2)}) collective-permute-start(f32[4,32,256]{2,1,0:T(8,128)} %get-tuple-element.109), channel_id=1, source_target_pairs={{0,8},{8,16},{16,24},{24,32},{32,40},{40,48},{48,56},{1,9},{9,17},... | collective-permute-start | bytes 393224 | tf_op jit(solution)/shard_map/ppermute | solution.py:356
  168.8 10.7 %collective-permute-start.14 = (f32[4,32,256]{2,1,0:T(8,128)}, f32[4,32,256]{2,1,0:T(8,128)S(1)}, u32[]{:S(2)}, u32[]{:S(2)}) collective-permute-start(f32[4,32,256]{2,1,0:T(8,128)} %get-tuple-element.110), channel_id=1, source_target_pairs={{8,0},{16,8},{24,16},{32,24},{40,32},{48,40},{56,48},{9,1},{17,9},... | collective-permute-start | bytes 393224 | tf_op jit(solution)/shard_map/ppermute | solution.py:356
  174.9 11.5 %copy-start.12 = (f32[4,32,256]{2,1,0:T(8,128)}, f32[4,32,256]{2,1,0:T(8,128)S(1)}, u32[]{:S(2)}) copy-start(f32[4,32,256]{2,1,0:T(8,128)S(1)} %collective-permute-done.13.refs_4_) | copy-start | bytes 393220
  174.9 6.8 %collective-permute-start.15 = (f32[4,32,256]{2,1,0:T(8,128)}, f32[4,32,256]{2,1,0:T(8,128)S(1)}, u32[]{:S(2)}, u32[]{:S(2)}) collective-permute-start(f32[4,32,256]{2,1,0:T(8,128)} %get-tuple-element.111), channel_id=1, source_target_pairs={{0,1},{1,2},{2,3},{3,4},{4,5},{5,6},{6,7},{8,9},{9,10},{10,11},{11... | collective-permute-start | bytes 393224 | tf_op jit(solution)/shard_map/ppermute | solution.py:356
  179.5 6.9 %collective-permute-start.16 = (f32[4,32,256]{2,1,0:T(8,128)}, f32[4,32,256]{2,1,0:T(8,128)S(1)}, u32[]{:S(2)}, u32[]{:S(2)}) collective-permute-start(f32[4,32,256]{2,1,0:T(8,128)} %get-tuple-element.112), channel_id=1, source_target_pairs={{1,0},{2,1},{3,2},{4,3},{5,4},{6,5},{7,6},{9,8},{10,9},{11,10},{12... | collective-permute-start | bytes 393224 | tf_op jit(solution)/shard_map/ppermute | solution.py:356
  196.8 12.0 %copy-start.4 = (bf16[1024,1024]{1,0:T(8,128)(2,1)S(1)}, bf16[1024,1024]{1,0:T(8,128)(2,1)}, u32[]{:S(2)}) copy-start(bf16[1024,1024]{1,0:T(8,128)(2,1)} %get-tuple-element.101.refs_5_.refs_4_) | copy-start | bytes 6291460
  231.1 10.8 %copy-start.1 = (f32[1,1,128,4,8,8]{2,5,4,3,1,0:T(8,128)S(1)}, f32[1,1,128,4,8,8]{2,5,4,3,1,0:T(8,128)}, u32[]{:S(2)}) copy-start(f32[1,1,128,4,8,8]{2,5,4,3,1,0:T(8,128)} %param.25) | copy-start | bytes 393220
  (8 other events, 33.6 us)
